TPU v7x, 256 devices: a whole 4x4x8 slice. The times are simulated.
256 devices in a mesh: neur: 32 (over y, z_hi, core), tm: 8 (over x, z_lo).
Axes of the slice: x: 4, y: 4, z: 8 (z_hi: 4, z_lo: 2; z = z_hi * 2 + z_lo), core: 2. Of those that a mesh axis runs over, the one named last changes fastest.
Arguments:
- spikes: int32 [1024, 262144], P(None, ('neur', 'tm')), may hold values from 0 to 9
- held_in: int32 [262144], P(('neur', 'tm')), may hold values 0 or 1
- readin_weight: bfloat16 [262144, 1024], P(('neur', 'tm')), may hold values from -0.01171875 to 0.01171875
- qkv_weight: bfloat16 [1024, 3, 1024], P(None, None, 'tm'), may hold values from -0.1875 to 0.1875
- out_weight: bfloat16 [1024, 1024], P('tm'), may hold values from -0.1875 to 0.1875
- up_weight: bfloat16 [1024, 4096], P(None, 'tm'), may hold values from -0.1875 to 0.1875
- down_weight: bfloat16 [4096, 1024], P('tm'), may hold values from -0.09375 to 0.09375
- norm_gain: float32 [1024], replicated, may hold values from 0.25 to 1.75
- mlp_gain: float32 [1024], replicated, may hold values from 0.25 to 1.75
- final_gain: float32 [1024], replicated, may hold values from 0.25 to 1.75
- readout_weight: bfloat16 [262144, 1024], P(('neur', 'tm')), may hold values from -0.1875 to 0.1875
- readout_bias: float32 [262144], P(('neur', 'tm')), may hold values from -3 to 3
Outputs:
- latents: bfloat16 [1024, 1024], P('neur')
- neuron_bits: float32 [262144], P(('neur', 'tm'))
- bits_per_spike: float32 [], replicated
All inputs are finite; a program needn't handle non-finite values. No bound on the sum of `held_in` on one device may be relied on, other than what follows from the above.
Results may differ from a plain program's by a relative error of at most 0.006.
Values may be sent and summed in bfloat16 or wider, within the bound.
No kernel may reach another device: no remote copies, remote signals or barrier semaphores. Data moves between devices by JAX's collectives and lax.ppermute only.
A program may use at most 64 MiB of HBM per device.

v0:
```python
import math

import jax
import jax.numpy as jnp
from jax import lax
from jax.sharding import PartitionSpec as P

HEAD_DIM = 128


def normed(values, gain_vec):
    return values * lax.rsqrt(jnp.mean(values * values, -1, keepdims=True) + 1e-05) * gain_vec


def on_device(
    spikes,
    held_in,
    readin_weight,
    qkv_weight,
    out_weight,
    up_weight,
    down_weight,
    norm_gain,
    mlp_gain,
    final_gain,
    readout_weight,
    readout_bias,
):
    frames_all = spikes.shape[0]
    rows_here = frames_all // lax.axis_size("neur")
    masked = (spikes * held_in[None, :]).astype(jnp.bfloat16)
    heldout = (1 - held_in).astype(jnp.float32)
    counts = jnp.sum(spikes, 0).astype(jnp.float32)
    partial_sum = jnp.dot(masked, readin_weight, preferred_element_type=jnp.float32)
    summed = lax.psum(partial_sum, ("neur", "tm"))
    stream = lax.dynamic_slice_in_dim(summed, lax.axis_index("neur") * rows_here, rows_here, 0)
    model_dim = stream.shape[1]
    head_cols = qkv_weight.shape[2]
    local_heads = head_cols // HEAD_DIM
    attn_in = normed(stream, norm_gain).astype(jnp.bfloat16)
    projected = jnp.dot(
        attn_in, qkv_weight.reshape(model_dim, 3 * head_cols), preferred_element_type=jnp.float32
    ).astype(jnp.bfloat16)
    queries = projected[:, :head_cols].reshape(rows_here, local_heads, HEAD_DIM)
    keys_local = projected[:, head_cols : 2 * head_cols]
    values_local = projected[:, 2 * head_cols :]
    scaling = 1.0 / math.sqrt(HEAD_DIM)
    key_rows = lax.all_gather(keys_local, "neur", axis=0, tiled=True).reshape(
        -1, local_heads, HEAD_DIM
    )
    value_rows = lax.all_gather(values_local, "neur", axis=0, tiled=True).reshape(
        -1, local_heads, HEAD_DIM
    )
    scores = (
        jnp.einsum("qhd,khd->hqk", queries, key_rows, preferred_element_type=jnp.float32) * scaling
    )
    weights = jnp.exp(scores)
    numerator = jnp.einsum(
        "hqk,khd->qhd", weights.astype(jnp.bfloat16), value_rows, preferred_element_type=jnp.float32
    )
    denominator = jnp.sum(weights, -1).T
    numerator, denominator = (numerator, denominator)
    heads_out = (
        (numerator / denominator[:, :, None]).astype(jnp.bfloat16).reshape(rows_here, head_cols)
    )
    attn_part = jnp.dot(heads_out, out_weight, preferred_element_type=jnp.float32)
    mixed_state = stream + lax.psum(attn_part, "tm")
    mlp_in = normed(mixed_state, mlp_gain).astype(jnp.bfloat16)
    hidden_act = jax.nn.gelu(jnp.dot(mlp_in, up_weight, preferred_element_type=jnp.float32)).astype(
        jnp.bfloat16
    )
    mlp_part = jnp.dot(hidden_act, down_weight, preferred_element_type=jnp.float32)
    final_state = mixed_state + lax.psum(mlp_part, "tm")
    latents = normed(final_state, final_gain).astype(jnp.bfloat16)
    log_rate = (
        lax.dot_general(
            lax.all_gather(latents, "neur", axis=0, tiled=True),
            readout_weight,
            (((1,), (1,)), ((), ())),
            preferred_element_type=jnp.float32,
        )
        + readout_bias[None, :]
    )
    observed = spikes.astype(jnp.float32)
    model_ll = jnp.sum(observed * log_rate - jnp.exp(log_rate), 0)
    null_ll = counts * jnp.log((counts + 1.0) / frames_all) - (counts + 1.0)
    gained = heldout * (model_ll - null_ll)
    neuron_bits = gained / (math.log(2.0) * (counts + 1.0))
    score_sum, spike_sum = lax.psum((jnp.sum(gained), jnp.sum(heldout * counts)), ("neur", "tm"))
    bits_total = score_sum / (math.log(2.0) * (1.0 + spike_sum))
    return (latents, neuron_bits, bits_total)


def solution(mesh):
    in_specs = (
        P(None, ("neur", "tm")),
        P(("neur", "tm")),
        P(("neur", "tm"), None),
        P(None, None, "tm"),
        P("tm", None),
        P(None, "tm"),
        P("tm", None),
        P(),
        P(),
        P(),
        P(("neur", "tm"), None),
        P(("neur", "tm")),
    )
    out_specs = (P("neur", None), P(("neur", "tm")), P())
    return jax.shard_map(
        on_device, mesh=mesh, in_specs=in_specs, out_specs=out_specs, check_vma=False
    )
```

profile of v0, /device:TPU:1, one launch (start us, length us, event | category | flops | bytes accessed | tf_op | source)
XLA Modules:
  0.0 675.9 jit_solution(17022954513759164385)
XLA Ops:
  7.2 0.0 copy-start
  7.2 0.0 all-reduce.5.cloned.1.call-start
  7.2 1.5 copy-done
  8.8 6.5 fusion
  15.3 0.0 copy-start.2
  15.3 0.0 copy-start.1
  15.3 0.0 copy-start.5
  15.3 0.0 all-reduce.5.cloned.1.call-update
  15.3 0.0 copy-start.3
  15.3 0.0 all-reduce.7.cloned.1.call-start
  15.4 1.4 copy.15
  16.8 269.4 %all-reduce.5.cloned.1.call-done = f32[1024,1024]{1,0:T(8,128)} async-done(((f32[1024,1024]{1,0:T(8,128)}), f32[1024,1024]{1,0:T(8,128)}) %all-reduce.5.cloned.1.call-update) | async-done | bytes 4194320 | tf_op jit(solution)/shard_map/psum | solution.py:35
  286.2 1.0 multiply_reduce_fusion.2
  287.2 0.0 copy-done.2
  287.2 1.2 convolution_convert_fusion
  288.5 42.8 %all_gather.10 = bf16[1024,128]{1,0:T(8,128)(2,1)S(1)} all-gather(bf16[32,128]{1,0:T(8,128)(2,1)S(1)} %get-tuple-element.11), channel_id=1, replica_groups=mesh['neur'=32,'tm'=8] {'neur'}, dimensions={0}, use_global_device_ids=true | all-gather | bytes 270336 | tf_op jit(solution)/shard_map/all_gather | solution.py:48
  331.3 0.3 fusion.38
  331.6 42.1 %all_gather.9 = bf16[1024,128]{1,0:T(8,128)(2,1)S(1)} all-gather(bf16[32,128]{1,0:T(8,128)(2,1)S(1)} %get-tuple-element.12), channel_id=1, replica_groups=mesh['neur'=32,'tm'=8] {'neur'}, dimensions={0}, use_global_device_ids=true | all-gather | bytes 270336 | tf_op jit(solution)/shard_map/all_gather | solution.py:51
  373.7 0.0 copy-done.1
  373.7 0.0 copy-start.6
  373.7 0.9 fusion.6
  374.6 0.0 all-reduce.7.cloned.1.call-update
  374.6 0.0 all-reduce.9.cloned.1.call-start
  374.7 67.4 %all-reduce.7.cloned.1.call-done = f32[32,1024]{1,0:T(8,128)} async-done(((f32[32,1024]{1,0:T(8,128)}), f32[32,1024]{1,0:T(8,128)}) %all-reduce.7.cloned.1.call-update) | async-done | bytes 131088 | tf_op jit(solution)/shard_map/psum | solution.py:67
  442.1 1.1 multiply_reduce_fusion.1
  443.2 0.0 copy-done.5
  443.2 2.8 fusion.16
  446.0 0.0 all-reduce.9.cloned.1.call-update
  446.0 0.0 all-gather.2.cloned.1.call-start
  446.1 76.6 %all-reduce.9.cloned.1.call-done = f32[32,1024]{1,0:T(8,128)} async-done(((f32[32,1024]{1,0:T(8,128)}), f32[32,1024]{1,0:T(8,128)}) %all-reduce.9.cloned.1.call-update) | async-done | bytes 131088 | tf_op jit(solution)/shard_map/psum | solution.py:73
  522.6 1.0 multiply_reduce_fusion
  523.7 0.0 copy-done.3
  523.7 0.7 multiply_convert_fusion.2
  524.4 0.0 all-gather.2.cloned.1.call-update
  524.4 2.5 reduce_sum.77
  526.9 0.0 copy-start.4
  526.9 58.2 %all-gather.2.cloned.1.call-done = bf16[1024,1024]{1,0:T(8,128)(2,1)} async-done(((bf16[32,1024]{1,0:T(8,128)(2,1)}), bf16[1024,1024]{1,0:T(8,128)(2,1)}) %all-gather.2.cloned.1.call-update) | async-done | bytes 2097168 | tf_op jit(solution)/shard_map/all_gather | solution.py:77
  585.1 0.0 copy-done.6
  585.1 6.2 subtract_reduce_fusion
  591.3 0.0 copy-done.4
  591.3 1.3 multiply_reduce_fusion.3
  592.6 74.4 %all-reduce = (f32[]{:T(128)}, f32[]{:T(128)}) all-reduce(f32[]{:T(128)} %get-tuple-element.4, f32[]{:T(128)} %get-tuple-element.3), channel_id=1, replica_groups=mesh['neur'=32,'tm'=8] {'neur','tm'}, use_global_device_ids=true, to_apply=%region_10.0 | all-reduce | flops 2 | bytes 16 | tf_op jit(solution)/shard_map/psum | solution.py:89
  (4 shorter events, 0.0 us)
Async XLA Ops:
  7.2 1.6 copy-start
  7.2 279.0 %all-reduce.5.cloned.1.call-start = ((), (), s32[]{:S(2)}) async-start(), calls=%async_computation | async-start | bytes 8388608 | tf_op jit(solution)/shard_map/psum | solution.py:35
  15.3 271.9 %copy-start.2 = (f32[1024]{0:T(1024)S(1)}, f32[1024]{0:T(1024)}, u32[]{:S(2)}) copy-start(f32[1024]{0:T(1024)} %param.19) | copy-start | bytes 12292
  15.3 358.4 %copy-start.1 = (bf16[128,1024]{1,0:T(8,128)(2,1)S(1)}, bf16[128,1024]{1,0:T(8,128)(2,1)}, u32[]{:S(2)}) copy-start(bf16[128,1024]{1,0:T(8,128)(2,1)} %param.16) | copy-start | bytes 786436
  15.3 428.0 %copy-start.5 = (f32[1024]{0:T(1024)S(1)}, f32[1024]{0:T(1024)}, u32[]{:S(2)}) copy-start(f32[1024]{0:T(1024)} %param.20) | copy-start | bytes 12292
  15.3 508.4 %copy-start.3 = (f32[1024]{0:T(1024)S(1)}, f32[1024]{0:T(1024)}, u32[]{:S(2)}) copy-start(f32[1024]{0:T(1024)} %param.21) | copy-start | bytes 12292
  15.3 426.8 %all-reduce.7.cloned.1.call-start = ((), (), s32[]{:S(2)}) async-start(), calls=%async_computation.1 | async-start | bytes 262144 | tf_op jit(solution)/shard_map/psum | solution.py:67
  373.7 211.5 %copy-start.6 = (f32[1024]{0:T(1024)S(1)}, f32[1024]{0:T(1024)}, u32[]{:S(2)}) copy-start(f32[1024]{0:T(1024)} %param.23) | copy-start | bytes 12292
  374.6 148.0 %all-reduce.9.cloned.1.call-start = ((), (), s32[]{:S(2)}) async-start(), calls=%async_computation.2 | async-start | bytes 262144 | tf_op jit(solution)/shard_map/psum | solution.py:73
  446.0 139.1 %all-gather.2.cloned.1.call-start = ((), (), s32[]{:S(2)}) async-start(), calls=%async_computation.3 | async-start | bytes 2162688 | tf_op jit(solution)/shard_map/all_gather | solution.py:77
  526.9 64.4 %copy-start.4 = (s32[1024]{0:T(1024)S(1)}, s32[1024]{0:T(1024)}, u32[]{:S(2)}) copy-start(s32[1024]{0:T(1024)} %param.13) | copy-start | bytes 12292
Sparse Core Ops, SparseCore 0:
  15.4 270.7 all-reduce.4
  374.8 67.3 all-reduce.6
  446.2 76.4 all-reduce.8
  526.0 59.1 all-gather.1
where the time goes:
time: 676 us
  waiting for transfers between devices  472 us (70%)
  blocking collectives  159 us (24%)
  matrix products  18 us (3%)
  between operations  16.2 us (2%)
  other arithmetic  7.64 us (1%)
    psum x1, waiting for transfers between devices, on_device(): summed = lax.psum(partial_sum, ('neur', 'tm'))  269 us
    psum x1, waiting for transfers between devices, on_device(): final_state = mixed_state + lax.psum(mlp_part, 'tm')  76.6 us
    psum x1, blocking collectives, on_device(): lax.psum((jnp.sum(gained), jnp.sum(heldout * counts)), ('neur', 'tm'))  74.4 us
    psum x1, waiting for transfers between devices, on_device(): mixed_state = stream + lax.psum(attn_part, 'tm')  67.4 us
    all_gather x1, waiting for transfers between devices, on_device(): lax.all_gather(latents, 'neur', axis=0, tiled=True)  58.2 us
    all_gather x1, blocking collectives, on_device(): lax.all_gather(keys_local, 'neur', axis=0, tiled=True)  42.8 us
    all_gather x1, blocking collectives, on_device(): lax.all_gather(values_local, 'neur', axis=0, tiled=True)  42.1 us
  transfers between devices with their start and end apart: 4, of which 4 were waited for; matrix products, arithmetic and copies ran while one was open for 1% of the time, Pallas kernels for 0%

commit v1 on v0

v1 whole, which is shorter than its diff:
```python
import math

import jax
import jax.numpy as jnp
from jax import lax
from jax.sharding import Mesh
from jax.sharding import PartitionSpec as P

HEAD_DIM = 128
BF16 = jnp.bfloat16
F32 = jnp.float32
ROWS = ("y", "zh", "c")
TM = ("x", "zl")
YZ = ("y", "zh")
CHIPS = ("y", "zh", "x", "zl")
ALL = ("y", "zh", "c", "x", "zl")


def normed(values, gain_vec):
    return values * lax.rsqrt(jnp.mean(values * values, -1, keepdims=True) + 1e-05) * gain_vec


def exchange(blocks, axes):
    return lax.all_to_all(blocks, axes, 0, 0, tiled=True)


def to_all(block, axes):
    return exchange(jnp.broadcast_to(block[None], (lax.axis_size(axes),) + block.shape), axes)


def other_core(block):
    return lax.ppermute(block, "c", [(0, 1), (1, 0)])


def on_device(
    spikes,
    held_in,
    readin_weight,
    qkv_weight,
    out_weight,
    up_weight,
    down_weight,
    norm_gain,
    mlp_gain,
    final_gain,
    readout_weight,
    readout_bias,
):
    frames_all = spikes.shape[0]
    model_dim = readin_weight.shape[1]
    chips = lax.axis_size(CHIPS)
    half = frames_all // 2
    rows_own = half // chips
    rows_here = frames_all // lax.axis_size(ROWS)
    core = lax.axis_index("c")

    def readin(start):
        block = lax.dynamic_slice_in_dim(spikes, start, half, 0)
        masked = (block * held_in[None, :]).astype(BF16)
        return jnp.dot(masked, readin_weight, preferred_element_type=F32)

    theirs = other_core(readin((1 - core) * half).astype(BF16))
    chip_sum = (readin(core * half) + theirs.astype(F32)).astype(BF16)
    parts = exchange(chip_sum.reshape(chips, rows_own, model_dim), CHIPS)
    own_rows = jnp.sum(parts.astype(F32), 0)
    stream = to_all(own_rows, TM).reshape(rows_here, model_dim)

    attn_in = normed(stream, norm_gain).astype(BF16)
    queries, keys, values = (
        jnp.dot(attn_in, qkv_weight[:, i], preferred_element_type=F32).astype(BF16)
        for i in range(3)
    )
    kv_near = to_all(jnp.concatenate([keys, values], 1), YZ).reshape(half, 2 * HEAD_DIM)
    kv_far = other_core(kv_near)
    numerator = 0.0
    denominator = 0.0
    for kv in (kv_near, kv_far):
        scores = lax.dot_general(
            queries, kv[:, :HEAD_DIM], (((1,), (1,)), ((), ())), preferred_element_type=F32
        )
        weights = jnp.exp(scores * (1.0 / math.sqrt(HEAD_DIM)))
        numerator += jnp.dot(weights.astype(BF16), kv[:, HEAD_DIM:], preferred_element_type=F32)
        denominator += jnp.sum(weights, -1, keepdims=True)
    heads_out = (numerator / denominator).astype(BF16)
    attn_part = jnp.dot(heads_out, out_weight, preferred_element_type=F32)
    mixed_state = stream + jnp.sum(to_all(attn_part.astype(BF16), TM).astype(F32), 0)

    mlp_in = normed(mixed_state, mlp_gain).astype(BF16)
    hidden_act = jax.nn.gelu(jnp.dot(mlp_in, up_weight, preferred_element_type=F32)).astype(BF16)
    mlp_part = jnp.dot(hidden_act, down_weight, preferred_element_type=F32)
    mlp_sum = jnp.sum(
        exchange(mlp_part.astype(BF16).reshape(-1, rows_own, model_dim), TM).astype(F32), 0
    )
    own_mixed = lax.dynamic_slice_in_dim(mixed_state, lax.axis_index(TM) * rows_own, rows_own, 0)
    own_latents = normed(own_mixed + mlp_sum, final_gain).astype(BF16)

    lat_near = to_all(own_latents, CHIPS).reshape(half, model_dim)
    lat_far = other_core(lat_near)
    model_ll = 0.0
    for lat, start in ((lat_near, core * half), (lat_far, (1 - core) * half)):
        log_rate = (
            lax.dot_general(
                lat, readout_weight, (((1,), (1,)), ((), ())), preferred_element_type=F32
            )
            + readout_bias[None, :]
        )
        observed = lax.dynamic_slice_in_dim(spikes, start, half, 0).astype(F32)
        model_ll += jnp.sum(observed * log_rate - jnp.exp(log_rate), 0)
    out_start = lax.axis_index(ROWS) * rows_here
    near = out_start // half == core
    out_row = lax.rem(out_start, half)
    latents = jnp.where(
        near,
        lax.dynamic_slice_in_dim(lat_near, out_row, rows_here, 0),
        lax.dynamic_slice_in_dim(lat_far, out_row, rows_here, 0),
    )

    heldout = (1 - held_in).astype(F32)
    counts = jnp.sum(spikes, 0).astype(F32)
    null_ll = counts * jnp.log((counts + 1.0) / frames_all) - (counts + 1.0)
    gained = heldout * (model_ll - null_ll)
    neuron_bits = gained / (math.log(2.0) * (counts + 1.0))
    sums = jnp.stack([jnp.sum(gained), jnp.sum(heldout * counts)])
    totals = jnp.sum(to_all(jnp.pad(sums, (0, 126))[None], ALL), (0, 1))
    bits_total = totals[0] / (math.log(2.0) * (1.0 + totals[1]))
    return (latents, neuron_bits, bits_total)


def solution(mesh):
    fine = Mesh(mesh.devices.reshape(4, 4, 2, 4, 2), ALL)
    in_specs = (
        P(None, ALL),
        P(ALL),
        P(ALL, None),
        P(None, None, TM),
        P(TM, None),
        P(None, TM),
        P(TM, None),
        P(),
        P(),
        P(),
        P(ALL, None),
        P(ALL),
    )
    out_specs = (P(ROWS, None), P(ALL), P())
    return jax.shard_map(
        on_device, mesh=fine, in_specs=in_specs, out_specs=out_specs, check_vma=False
    )
```

time: 676 us -> 194 us (0.29)
  waiting for transfers between devices: 472 us -> 39.9 us
  blocking collectives: 159 us -> 84.9 us
  starting transfers between devices: 0.16 us -> 28.6 us
  between operations: 16.2 us -> 3.38 us
    psum x3 -> x0, waiting for transfers between devices: 413 us -> none  [the longest x1 269 us: on_device(): summed = lax.psum(partial_sum, ('neur', 'tm'))]
    all_to_all x0 -> x3, blocking collectives: none -> 84.9 us  [exchange(): return lax.all_to_all(blocks, axes, 0, 0, tiled=True)]
    all_gather x2 -> x0, blocking collectives: 84.9 us -> none  [the longest x1 42.8 us: on_device(): lax.all_gather(keys_local, 'neur', axis=0, tiled=True)]
    psum x1 -> x0, blocking collectives: 74.4 us -> none  [on_device(): lax.psum((jnp.sum(gained), jnp.sum(heldout * counts)), ('neur', 'tm'))]
    all_gather x1 -> x0, waiting for transfers between devices: 58.2 us -> none  [on_device(): lax.all_gather(latents, 'neur', axis=0, tiled=True)]
    all_to_all x0 -> x4, waiting for transfers between devices: none -> 36.7 us  [exchange(): return lax.all_to_all(blocks, axes, 0, 0, tiled=True)]
    all_to_all x0 -> x4, starting transfers between devices: none -> 16 us  [exchange(): return lax.all_to_all(blocks, axes, 0, 0, tiled=True)]
    ppermute x0 -> x3, starting transfers between devices: none -> 12.6 us  [other_core(): return lax.ppermute(block, 'c', [(0, 1), (1, 0)])]
  transfers between devices with their start and end apart: 4 -> 7, of which waited for: 4 -> 6; matrix products, arithmetic and copies ran while one was open for 1% -> 4% of each run, Pallas kernels for 0% -> 0%
where the time goes in v1:
time: 194 us; the launch traced here: 193 us
  blocking collectives  84.9 us (44%)
  waiting for transfers between devices  39.9 us (21%)
  starting transfers between devices  28.6 us (15%)
  matrix products  19.8 us (10%)
  local copies, waits for them, and re-layouts  8.47 us (4%)
  other arithmetic  7.78 us (4%)
  between operations  3.38 us (2%)
    all_to_all x3, blocking collectives, exchange(): return lax.all_to_all(blocks, axes, 0, 0, tiled=True)  84.9 us
    all_to_all x4, waiting for transfers between devices, exchange(): return lax.all_to_all(blocks, axes, 0, 0, tiled=True)  36.7 us
    all_to_all x4, starting transfers between devices, exchange(): return lax.all_to_all(blocks, axes, 0, 0, tiled=True)  16 us
    ppermute x3, starting transfers between devices, other_core(): return lax.ppermute(block, 'c', [(0, 1), (1, 0)])  12.6 us
    dot_general x2, matrix products, readin(): return jnp.dot(masked, readin_weight, preferred_element_type=F32)  7.68 us
    dot_general x2, matrix products, on_device(): lax.dot_general(lat, readout_weight, (((1,), (1,)), ((), ())), preferred_...  6.67 us
  transfers between devices with their start and end apart: 7, of which 6 were waited for; matrix products, arithmetic and copies ran while one was open for 4% of the time, Pallas kernels for 0%

profile of v1, /device:TPU:1, one launch (start us, length us, event | category | flops | bytes accessed | tf_op | source)
XLA Modules:
  0.0 192.9 jit_solution(15791323354438174600)
XLA Ops:
  0.7 1.6 copy-done
  2.2 3.8 %convolution_convert_fusion = bf16[512,1024]{1,0:T(8,128)(2,1)} fusion(bf16[1024,1024]{1,0:T(8,128)(2,1)S(1)} %copy-done, s32[1024,1024]{1,0:T(8,128)} %param.12, s32[]{:T(128)S(6)} %select_n.31, s32[1024]{0:T(1024)} %param.13), kind=kOutput, calls=%fused_computation.6 | convolution fusion | flops 1075314688 | bytes 5246980 | tf_op jit(solution)/shard_map/dot_general | solution.py:60
  6.1 3.2 %collective-permute-start = (bf16[512,1024]{1,0:T(8,128)(2,1)}, bf16[512,1024]{1,0:T(8,128)(2,1)S(1)}, u32[]{:S(2)}, u32[]{:S(2)}) collective-permute-start(bf16[512,1024]{1,0:T(8,128)(2,1)} %convolution_convert_fusion), channel_id=1, source_target_pairs={{0,8},{8,0},{1,9},{9,1},{2,10},{10,2},{3,11},{11,3},{4,12},{12,4},... | collective-permute-start | bytes 3145736 | tf_op jit(solution)/shard_map/ppermute | solution.py:32
  9.3 2.5 %collective-permute-done = bf16[512,1024]{1,0:T(8,128)(2,1)S(1)} collective-permute-done((bf16[512,1024]{1,0:T(8,128)(2,1)}, bf16[512,1024]{1,0:T(8,128)(2,1)S(1)}, u32[]{:S(2)}, u32[]{:S(2)}) %collective-permute-start) | collective-permute-done | bytes 1048608 | tf_op jit(solution)/shard_map/ppermute | solution.py:32
  11.8 3.8 %add_convert_fusion = bf16[512,1024]{1,0:T(8,128)(2,1)} fusion(bf16[512,1024]{1,0:T(8,128)(2,1)S(1)} %collective-permute-done, bf16[1024,1024]{1,0:T(8,128)(2,1)S(1)} %copy-done, s32[1024,1024]{1,0:T(8,128)} %param.12, s32[]{:T(128)S(6)} %select_n.30, s32[1024]{0:T(1024)S(1)} %copy-done.7), kind=kOutput, calls=%fused_computation.3 | convolution fusion | flops 1076363264 | bytes 6295556 | tf_op jit(solution)/shard_map/dot_general | solution.py:60
  15.7 1.5 reshape.112
  17.1 43.6 %all_to_all.35 = bf16[128,4,1024]{2,1,0:T(4,128)(2,1)S(1)} all-to-all(bf16[128,4,1024]{2,1,0:T(4,128)(2,1)S(1)} %reshape.112), channel_id=1, replica_groups=mesh['y'=4,'zh'=4,'c'=2,'x'=4,'zl'=2] {'y','zh','x','zl'}, dimensions={0} | all-to-all | bytes 2097152 | tf_op jit(solution)/shard_map/all_to_all | solution.py:24
  60.8 0.5 convert_reduce_fusion
  61.3 7.9 %all_to_all.36 = f32[8,4,1024]{2,1,0:T(4,128)S(1)} all-to-all(f32[8,4,1024]{2,1,0:T(4,128)S(1)} %broadcast_in_dim.10), channel_id=1, replica_groups=mesh['y'=4,'zh'=4,'c'=2,'x'=4,'zl'=2] {'x','zl'}, dimensions={0} | all-to-all | bytes 262144 | tf_op jit(solution)/shard_map/all_to_all | solution.py:24
  69.2 0.1 multiply_reduce_fusion.1
  69.3 0.1 multiply_convert_fusion.7
  69.5 1.1 convolution_convert_fusion.3
  70.6 0.2 convolution_convert_fusion.4
  70.8 0.7 broadcast_in_dim.11
  71.5 4.0 %all-to-all-start.2 = ((bf16[16,32,256]{2,1,0:T(8,128)(2,1)}), bf16[16,32,256]{2,1,0:T(8,128)(2,1)S(1)}, u32[]{:S(2)}, u32[]{:S(2)}) async-start(bf16[16,32,256]{2,1,0:T(8,128)(2,1)} %broadcast_in_dim.11), calls=%async_computation.2 | async-start | bytes 524288 | tf_op jit(solution)/shard_map/all_to_all | solution.py:24
  75.5 0.2 convolution_convert_fusion.5
  75.6 10.5 %all-to-all-done.2 = bf16[16,32,256]{2,1,0:T(8,128)(2,1)S(1)} async-done(((bf16[16,32,256]{2,1,0:T(8,128)(2,1)}), bf16[16,32,256]{2,1,0:T(8,128)(2,1)S(1)}, u32[]{:S(2)}, u32[]{:S(2)}) %all-to-all-start.2) | async-done | bytes 262176 | tf_op jit(solution)/shard_map/all_to_all | solution.py:24
  86.1 4.3 %collective-permute-start.1 = (bf16[512,256]{1,0:T(8,128)(2,1)S(1)}, bf16[512,256]{1,0:T(8,128)(2,1)S(1)}, u32[]{:S(2)}, u32[]{:S(2)}) collective-permute-start(bf16[512,256]{1,0:T(8,128)(2,1)S(1)} %bitcast.30), channel_id=1, source_target_pairs={{0,8},{8,0},{1,9},{9,1},{2,10},{10,2},{3,11},{11,3},{4,12},{12,4},... | collective-permute-start | bytes 786440 | tf_op jit(solution)/shard_map/ppermute | solution.py:32
  90.4 0.3 fusion.49
  90.7 0.1 fusion.16
  90.9 0.7 collective-permute-done.1
  91.6 0.3 fusion.50
  91.9 1.2 convolution_convert_fusion.2
  93.1 0.9 broadcast_in_dim.12
  94.0 3.5 %all-to-all-start.3 = ((bf16[8,32,1024]{2,1,0:T(8,128)(2,1)}), bf16[8,32,1024]{2,1,0:T(8,128)(2,1)S(1)}, u32[]{:S(2)}, u32[]{:S(2)}) async-start(bf16[8,32,1024]{2,1,0:T(8,128)(2,1)} %broadcast_in_dim.12), calls=%async_computation.3 | async-start | bytes 1048576 | tf_op jit(solution)/shard_map/all_to_all | solution.py:24
  97.5 9.4 %all-to-all-done.3 = bf16[8,32,1024]{2,1,0:T(8,128)(2,1)S(1)} async-done(((bf16[8,32,1024]{2,1,0:T(8,128)(2,1)}), bf16[8,32,1024]{2,1,0:T(8,128)(2,1)S(1)}, u32[]{:S(2)}, u32[]{:S(2)}) %all-to-all-start.3) | async-done | bytes 524320 | tf_op jit(solution)/shard_map/all_to_all | solution.py:24
  107.1 0.1 multiply_reduce_fusion
  107.2 0.1 rsqrt.29
  107.3 2.1 %convolution_convert_fusion.1 = bf16[32,1024]{1,0:T(8,128)(2,1)S(1)} fusion(bf16[512,1024]{1,0:T(8,128)(2,1)} %param.18, bf16[1024,512]{1,0:T(8,128)(2,1)} %param.17, f32[32,1024]{1,0:T(8,128)S(1)} %add.118, f32[1024]{0:T(1024)S(1)} %copy-done.4, f32[32]{0:T(128)S(1)} %rsqrt.29), kind=kOutput, calls=%fused_computation.7 | convolution fusion | flops 67387392 | bytes 2297984 | tf_op jit(solution)/shard_map/dot_general | solution.py:90
  109.4 0.7 reshape.115
  110.1 3.4 %all-to-all-start.4 = ((bf16[8,4,1024]{2,1,0:T(4,128)(2,1)}), bf16[8,4,1024]{2,1,0:T(4,128)(2,1)S(1)}, u32[]{:S(2)}, u32[]{:S(2)}) async-start(bf16[8,4,1024]{2,1,0:T(4,128)(2,1)} %reshape.115), calls=%async_computation.4 | async-start | bytes 131072 | tf_op jit(solution)/shard_map/all_to_all | solution.py:24
  113.5 5.2 %all-to-all-done.4 = bf16[8,4,1024]{2,1,0:T(4,128)(2,1)S(1)} async-done(((bf16[8,4,1024]{2,1,0:T(4,128)(2,1)}), bf16[8,4,1024]{2,1,0:T(4,128)(2,1)S(1)}, u32[]{:S(2)}, u32[]{:S(2)}) %all-to-all-start.4) | async-done | bytes 65568 | tf_op jit(solution)/shard_map/all_to_all | solution.py:24
  118.7 0.1 multiply_reduce_fusion.2
  119.0 0.3 broadcast_in_dim.13
  119.3 33.4 %all_to_all.37 = bf16[128,4,1024]{2,1,0:T(4,128)(2,1)S(1)} all-to-all(bf16[128,4,1024]{2,1,0:T(4,128)(2,1)S(1)} %broadcast_in_dim.13), channel_id=1, replica_groups=mesh['y'=4,'zh'=4,'c'=2,'x'=4,'zl'=2] {'y','zh','x','zl'}, dimensions={0} | all-to-all | bytes 2097152 | tf_op jit(solution)/shard_map/all_to_all | solution.py:24
  152.6 1.2 reshape.116
  153.8 5.0 %collective-permute-start.2 = (bf16[512,1024]{1,0:T(8,128)(2,1)}, bf16[512,1024]{1,0:T(8,128)(2,1)}, u32[]{:S(2)}, u32[]{:S(2)}) collective-permute-start(bf16[512,1024]{1,0:T(8,128)(2,1)} %reshape.116), channel_id=1, source_target_pairs={{0,8},{8,0},{1,9},{9,1},{2,10},{10,2},{3,11},{11,3},{4,12},{12,4},... | collective-permute-start | bytes 3145736 | tf_op jit(solution)/shard_map/ppermute | solution.py:32
  158.8 2.5 %reduce_sum.139 = s32[1024]{0:T(1024)S(1)} reduce(s32[1024,1024]{1,0:T(8,128)} %param.12, s32[]{:T(128)} %constant.64.clone.1), dimensions={0}, to_apply=%region_10.11 | reduce | flops 1047552 | bytes 4198404 | tf_op jit(solution)/shard_map/reduce_sum | solution.py:119
  161.3 3.9 %subtract_reduce_fusion.1 = f32[1024]{0:T(1024)S(1)} fusion(s32[1024,1024]{1,0:T(8,128)} %param.12, s32[]{:T(128)S(6)} %select_n.30, bf16[512,1024]{1,0:T(8,128)(2,1)S(1)} %copy-done.2, bf16[1024,1024]{1,0:T(8,128)(2,1)} %param.22, f32[1024]{0:T(1024)S(1)} %copy-done.9), kind=kOutput, calls=%fused_computation.1 | convolution fusion | flops 1076362240 | bytes 5251076 | tf_op jit(solution)/shard_map/dot_general | solution.py:102
  165.2 0.2 copy-done.8
  165.4 2.8 %subtract_reduce_fusion = f32[1024]{0:T(1024)S(1)} fusion(s32[1024,1024]{1,0:T(8,128)S(1)} %copy-done.1, s32[]{:T(128)S(6)} %select_n.31, bf16[512,1024]{1,0:T(8,128)(2,1)} %collective-permute-done.2, bf16[1024,1024]{1,0:T(8,128)(2,1)S(1)} %copy-done.8, f32[1024]{0:T(1024)S(1)} %copy-done.9), kind=kOutput, calls=%fused_computation | convolution fusion | flops 1076362240 | bytes 5251076 | tf_op jit(solution)/shard_map/dot_general | solution.py:102
  168.2 1.2 fusion.47
  169.4 1.4 fusion.42
  170.8 0.7 broadcast_in_dim.14
  171.5 5.1 %all-to-all-start.6 = ((f32[256,1,128]{2,1,0:T(1,128)}), f32[256,1,128]{2,1,0:T(1,128)S(1)}, u32[]{:S(2)}, u32[]{:S(2)}) async-start(f32[256,1,128]{2,1,0:T(1,128)} %broadcast_in_dim.14), calls=%async_computation.6 | async-start | bytes 262144 | tf_op jit(solution)/shard_map/all_to_all | solution.py:24
  176.6 1.5 dynamic-slice_select_fusion
  178.1 11.6 %all-to-all-done.6 = f32[256,1,128]{2,1,0:T(1,128)S(1)} async-done(((f32[256,1,128]{2,1,0:T(1,128)}), f32[256,1,128]{2,1,0:T(1,128)S(1)}, u32[]{:S(2)}, u32[]{:S(2)}) %all-to-all-start.6) | async-done | bytes 131104 | tf_op jit(solution)/shard_map/all_to_all | solution.py:24
  189.8 0.6 fusion.48
  (33 shorter events, 0.5 us)
Async XLA Ops:
  0.6 1.6 copy-start
  2.2 9.6 %copy-start.7 = (s32[1024]{0:T(1024)S(1)}, s32[1024]{0:T(1024)}, u32[]{:S(2)}) copy-start(s32[1024]{0:T(1024)} %param.13) | copy-start | bytes 12292
  6.1 5.7 %collective-permute-start = (bf16[512,1024]{1,0:T(8,128)(2,1)}, bf16[512,1024]{1,0:T(8,128)(2,1)S(1)}, u32[]{:S(2)}, u32[]{:S(2)}) collective-permute-start(bf16[512,1024]{1,0:T(8,128)(2,1)} %convolution_convert_fusion), channel_id=1, source_target_pairs={{0,8},{8,0},{1,9},{9,1},{2,10},{10,2},{3,11},{11,3},{4,12},{12,4},... | collective-permute-start | bytes 3145736 | tf_op jit(solution)/shard_map/ppermute | solution.py:32
  17.1 52.2 %copy-start.5 = (f32[1024]{0:T(1024)S(1)}, f32[1024]{0:T(1024)}, u32[]{:S(2)}) copy-start(f32[1024]{0:T(1024)} %param.19) | copy-start | bytes 12292
  60.8 9.8 %copy-start.3 = (bf16[1024,3,128]{2,0,1:T(8,128)(2,1)S(1)}, bf16[1024,3,128]{2,0,1:T(8,128)(2,1)}, u32[]{:S(2)}) copy-start(bf16[1024,3,128]{2,0,1:T(8,128)(2,1)} %param.15) | copy-start | bytes 2359300
  71.5 14.6 %all-to-all-start.2 = ((bf16[16,32,256]{2,1,0:T(8,128)(2,1)}), bf16[16,32,256]{2,1,0:T(8,128)(2,1)S(1)}, u32[]{:S(2)}, u32[]{:S(2)}) async-start(bf16[16,32,256]{2,1,0:T(8,128)(2,1)} %broadcast_in_dim.11), calls=%async_computation.2 | async-start | bytes 524288 | tf_op jit(solution)/shard_map/all_to_all | solution.py:24
  86.1 5.5 %collective-permute-start.1 = (bf16[512,256]{1,0:T(8,128)(2,1)S(1)}, bf16[512,256]{1,0:T(8,128)(2,1)S(1)}, u32[]{:S(2)}, u32[]{:S(2)}) collective-permute-start(bf16[512,256]{1,0:T(8,128)(2,1)S(1)} %bitcast.30), channel_id=1, source_target_pairs={{0,8},{8,0},{1,9},{9,1},{2,10},{10,2},{3,11},{11,3},{4,12},{12,4},... | collective-permute-start | bytes 786440 | tf_op jit(solution)/shard_map/ppermute | solution.py:32
  90.8 16.5 %copy-start.4 = (f32[1024]{0:T(1024)S(1)}, f32[1024]{0:T(1024)}, u32[]{:S(2)}) copy-start(f32[1024]{0:T(1024)} %param.20) | copy-start | bytes 12292
  94.0 13.0 %all-to-all-start.3 = ((bf16[8,32,1024]{2,1,0:T(8,128)(2,1)}), bf16[8,32,1024]{2,1,0:T(8,128)(2,1)S(1)}, u32[]{:S(2)}, u32[]{:S(2)}) async-start(bf16[8,32,1024]{2,1,0:T(8,128)(2,1)} %broadcast_in_dim.12), calls=%async_computation.3 | async-start | bytes 1048576 | tf_op jit(solution)/shard_map/all_to_all | solution.py:24
  97.5 21.4 %copy-start.6 = (f32[1024]{0:T(1024)S(1)}, f32[1024]{0:T(1024)}, u32[]{:S(2)}) copy-start(f32[1024]{0:T(1024)} %param.21) | copy-start | bytes 12292
  110.1 8.6 %all-to-all-start.4 = ((bf16[8,4,1024]{2,1,0:T(4,128)(2,1)}), bf16[8,4,1024]{2,1,0:T(4,128)(2,1)S(1)}, u32[]{:S(2)}, u32[]{:S(2)}) async-start(bf16[8,4,1024]{2,1,0:T(4,128)(2,1)} %reshape.115), calls=%async_computation.4 | async-start | bytes 131072 | tf_op jit(solution)/shard_map/all_to_all | solution.py:24
  153.8 7.5 %copy-start.2 = (bf16[512,1024]{1,0:T(8,128)(2,1)S(1)}, bf16[512,1024]{1,0:T(8,128)(2,1)}, u32[]{:S(2)}) copy-start(bf16[512,1024]{1,0:T(8,128)(2,1)} %reshape.116) | copy-start | bytes 3145732
  153.8 7.5 %copy-start.9 = (f32[1024]{0:T(1024)S(1)}, f32[1024]{0:T(1024)}, u32[]{:S(2)}) copy-start(f32[1024]{0:T(1024)} %param.23) | copy-start | bytes 12292
  153.8 11.4 %collective-permute-start.2 = (bf16[512,1024]{1,0:T(8,128)(2,1)}, bf16[512,1024]{1,0:T(8,128)(2,1)}, u32[]{:S(2)}, u32[]{:S(2)}) collective-permute-start(bf16[512,1024]{1,0:T(8,128)(2,1)} %reshape.116), channel_id=1, source_target_pairs={{0,8},{8,0},{1,9},{9,1},{2,10},{10,2},{3,11},{11,3},{4,12},{12,4},... | collective-permute-start | bytes 3145736 | tf_op jit(solution)/shard_map/ppermute | solution.py:32
  161.3 3.9 %copy-start.1 = (s32[1024,1024]{1,0:T(8,128)S(1)}, s32[1024,1024]{1,0:T(8,128)}, u32[]{:S(2)}) copy-start(s32[1024,1024]{1,0:T(8,128)} %param.12) | copy-start | bytes 12582916
  161.3 4.1 %copy-start.8 = (bf16[1024,1024]{1,0:T(8,128)(2,1)S(1)}, bf16[1024,1024]{1,0:T(8,128)(2,1)}, u32[]{:S(2)}) copy-start(bf16[1024,1024]{1,0:T(8,128)(2,1)} %param.22) | copy-start | bytes 6291460
  171.5 18.3 %all-to-all-start.6 = ((f32[256,1,128]{2,1,0:T(1,128)}), f32[256,1,128]{2,1,0:T(1,128)S(1)}, u32[]{:S(2)}, u32[]{:S(2)}) async-start(f32[256,1,128]{2,1,0:T(1,128)} %broadcast_in_dim.14), calls=%async_computation.6 | async-start | bytes 262144 | tf_op jit(solution)/shard_map/all_to_all | solution.py:24

commit v2 on v1

--- a/solution.py
+++ b/solution.py
@@ -12,7 +12,8 @@
 ROWS = ("y", "zh", "c")
 TM = ("x", "zl")
 YZ = ("y", "zh")
-CHIPS = ("y", "zh", "x", "zl")
+PLANE = ("y", "x")
+COLUMN = ("x", "zh", "zl")
 ALL = ("y", "zh", "c", "x", "zl")
 
 
@@ -48,11 +49,12 @@
 ):
     frames_all = spikes.shape[0]
     model_dim = readin_weight.shape[1]
-    chips = lax.axis_size(CHIPS)
     half = frames_all // 2
-    rows_own = half // chips
     rows_here = frames_all // lax.axis_size(ROWS)
+    chunk = half // lax.axis_size("y")
+    piece = chunk // (lax.axis_size("x") * lax.axis_size("zh"))
     core = lax.axis_index("c")
+    y_at = lax.axis_index("y")
 
     def readin(start):
         block = lax.dynamic_slice_in_dim(spikes, start, half, 0)
@@ -60,10 +62,16 @@
         return jnp.dot(masked, readin_weight, preferred_element_type=F32)
 
     theirs = other_core(readin((1 - core) * half).astype(BF16))
+    counts = jnp.sum(spikes, 0).astype(F32)
+    theirs, counts = lax.optimization_barrier((theirs, counts))
     chip_sum = (readin(core * half) + theirs.astype(F32)).astype(BF16)
-    parts = exchange(chip_sum.reshape(chips, rows_own, model_dim), CHIPS)
-    own_rows = jnp.sum(parts.astype(F32), 0)
-    stream = to_all(own_rows, TM).reshape(rows_here, model_dim)
+    plane_sum = jnp.sum(exchange(chip_sum.reshape(16, -1, model_dim), PLANE).astype(F32), 0)
+    blocks = jnp.broadcast_to(
+        plane_sum.astype(BF16).reshape(1, 4, 1, piece, model_dim), (4, 4, 2, piece, model_dim)
+    )
+    parts = exchange(blocks.reshape(32, piece, model_dim), COLUMN)
+    stream = jnp.sum(parts.reshape(4, 8, piece, model_dim).astype(F32), 1)
+    stream = stream.reshape(rows_here, model_dim)
 
     attn_in = normed(stream, norm_gain).astype(BF16)
     queries, keys, values = (
@@ -88,35 +96,38 @@
     mlp_in = normed(mixed_state, mlp_gain).astype(BF16)
     hidden_act = jax.nn.gelu(jnp.dot(mlp_in, up_weight, preferred_element_type=F32)).astype(BF16)
     mlp_part = jnp.dot(hidden_act, down_weight, preferred_element_type=F32)
-    mlp_sum = jnp.sum(
-        exchange(mlp_part.astype(BF16).reshape(-1, rows_own, model_dim), TM).astype(F32), 0
-    )
-    own_mixed = lax.dynamic_slice_in_dim(mixed_state, lax.axis_index(TM) * rows_own, rows_own, 0)
-    own_latents = normed(own_mixed + mlp_sum, final_gain).astype(BF16)
+    final_state = mixed_state + jnp.sum(to_all(mlp_part.astype(BF16), TM).astype(F32), 0)
+    own_latents = normed(final_state, final_gain).astype(BF16)
 
-    lat_near = to_all(own_latents, CHIPS).reshape(half, model_dim)
-    lat_far = other_core(lat_near)
+    spread = to_all(own_latents.reshape(4, piece, model_dim), "zh")
+    first = jnp.swapaxes(spread.reshape(4, 4, piece, model_dim), 0, 1).reshape(chunk, model_dim)
+    near = [first] + [
+        lax.ppermute(first, "y", [(i, (i + k) % 4) for i in range(4)]) for k in (1, 3, 2)
+    ]
+    chunks = []
+    for lat, k in zip(near, (0, 1, 3, 2)):
+        y_from = lax.rem(y_at + 4 - k, 4)
+        chunks.append((lat, core, y_from))
+        chunks.append((other_core(lat), 1 - core, y_from))
+    out_start = lax.axis_index(ROWS) * rows_here
+    out_chunk = out_start // chunk
+    out_row = lax.rem(out_start, chunk)
     model_ll = 0.0
-    for lat, start in ((lat_near, core * half), (lat_far, (1 - core) * half)):
+    latents = 0.0
+    for lat, c_from, y_from in chunks:
+        at = c_from * 4 + y_from
         log_rate = (
             lax.dot_general(
                 lat, readout_weight, (((1,), (1,)), ((), ())), preferred_element_type=F32
             )
             + readout_bias[None, :]
         )
-        observed = lax.dynamic_slice_in_dim(spikes, start, half, 0).astype(F32)
+        observed = lax.dynamic_slice_in_dim(spikes, at * chunk, chunk, 0).astype(F32)
         model_ll += jnp.sum(observed * log_rate - jnp.exp(log_rate), 0)
-    out_start = lax.axis_index(ROWS) * rows_here
-    near = out_start // half == core
-    out_row = lax.rem(out_start, half)
-    latents = jnp.where(
-        near,
-        lax.dynamic_slice_in_dim(lat_near, out_row, rows_here, 0),
-        lax.dynamic_slice_in_dim(lat_far, out_row, rows_here, 0),
-    )
+        rows = lax.dynamic_slice_in_dim(lat, out_row, rows_here, 0)
+        latents += jnp.where(at == out_chunk, rows, jnp.zeros_like(rows))
 
     heldout = (1 - held_in).astype(F32)
-    counts = jnp.sum(spikes, 0).astype(F32)
     null_ll = counts * jnp.log((counts + 1.0) / frames_all) - (counts + 1.0)
     gained = heldout * (model_ll - null_ll)
     neuron_bits = gained / (math.log(2.0) * (counts + 1.0))

time: 194 us -> 175 us (0.902)
  waiting for transfers between devices: 39.9 us -> 21 us
  matrix products: 19.8 us -> 24.9 us
  blocking collectives: 84.9 us -> 80.8 us
  local copies, waits for them, and re-layouts: 8.47 us -> 4.39 us
  starting transfers between devices: 28.6 us -> 31.9 us
    all_to_all x4 -> x2, waiting for transfers between devices: 36.7 us -> 21 us  [exchange(): return lax.all_to_all(blocks, axes, 0, 0, tiled=True)]
    ppermute x3 -> x6, starting transfers between devices: 12.6 us -> 17.3 us  [other_core(): return lax.ppermute(block, 'c', [(0, 1), (1, 0)])]
    dot_general x2 -> x8, matrix products: 6.67 us -> 11.1 us  [on_device(): lax.dot_general(lat, readout_weight, (((1,), (1,)), ((), ())), preferred_...]
    all_to_all x3 -> x5, blocking collectives: 84.9 us -> 80.8 us  [exchange(): return lax.all_to_all(blocks, axes, 0, 0, tiled=True)]
    all_to_all x4 -> x2, starting transfers between devices: 16 us -> 12.2 us  [exchange(): return lax.all_to_all(blocks, axes, 0, 0, tiled=True)]
    reshape x4 -> x0, local copies, waits for them, and re-layouts: 3.33 us -> none  [the longest x1 1.46 us: on_device(): parts = exchange(chip_sum.reshape(chips, rows_own, model_dim), CHIPS)]
    ppermute x3 -> x6, waiting for transfers between devices: 3.25 us -> 0.02 us  [other_core(): return lax.ppermute(block, 'c', [(0, 1), (1, 0)])]
    ppermute x0 -> x3, starting transfers between devices: none -> 2.47 us  [on_device(): lax.ppermute(first, 'y', [(i, (i + k) % 4) for i in range(4)])]
  transfers between devices with their start and end apart: 7 -> 11, of which waited for: 6 -> 2; matrix products, arithmetic and copies ran while one was open for 4% -> 12% of each run, Pallas kernels for 0% -> 0%
where the time goes in v2:
time: 175 us
  blocking collectives  80.8 us (46%)
  starting transfers between devices  31.9 us (18%)
  matrix products  24.9 us (14%)
  waiting for transfers between devices  21 us (12%)
  other arithmetic  8.15 us (5%)
  local copies, waits for them, and re-layouts  4.39 us (3%)
  between operations  3.51 us (2%)
    all_to_all x5, blocking collectives, exchange(): return lax.all_to_all(blocks, axes, 0, 0, tiled=True)  80.8 us
    all_to_all x2, waiting for transfers between devices, exchange(): return lax.all_to_all(blocks, axes, 0, 0, tiled=True)  21 us
    ppermute x6, starting transfers between devices, other_core(): return lax.ppermute(block, 'c', [(0, 1), (1, 0)])  17.3 us
    all_to_all x2, starting transfers between devices, exchange(): return lax.all_to_all(blocks, axes, 0, 0, tiled=True)  12.2 us
    dot_general x8, matrix products, on_device(): lax.dot_general(lat, readout_weight, (((1,), (1,)), ((), ())), preferred_...  11.1 us
    dot_general x2, matrix products, readin(): return jnp.dot(masked, readin_weight, preferred_element_type=F32)  6.68 us
  transfers between devices with their start and end apart: 11, of which 2 were waited for; matrix products, arithmetic and copies ran while one was open for 12% of the time, Pallas kernels for 0%

profile of v2, /device:TPU:1, one launch (start us, length us, event | category | flops | bytes accessed | tf_op | source)
XLA Modules:
  0.0 174.7 jit_solution(15903108501634987206)
XLA Ops:
  0.7 1.6 copy-done
  2.2 3.8 %convolution_convert_fusion = bf16[512,1024]{1,0:T(8,128)(2,1)} fusion(bf16[1024,1024]{1,0:T(8,128)(2,1)S(1)} %copy-done, s32[1024,1024]{1,0:T(8,128)} %param.12, s32[]{:T(128)S(6)} %select_n.98, s32[1024]{0:T(1024)} %param.13), kind=kOutput, calls=%fused_computation.3 | convolution fusion | flops 1075314688 | bytes 5246980 | tf_op jit(solution)/shard_map/dot_general | solution.py:62
  6.1 3.2 %collective-permute-start = (bf16[512,1024]{1,0:T(8,128)(2,1)}, bf16[512,1024]{1,0:T(8,128)(2,1)S(1)}, u32[]{:S(2)}, u32[]{:S(2)}) collective-permute-start(bf16[512,1024]{1,0:T(8,128)(2,1)} %convolution_convert_fusion), channel_id=1, source_target_pairs={{0,8},{8,0},{1,9},{9,1},{2,10},{10,2},{3,11},{11,3},{4,12},{12,4},... | collective-permute-start | bytes 3145736 | tf_op jit(solution)/shard_map/ppermute | solution.py:33
  9.3 2.5 %reduce_sum.196 = s32[1024]{0:T(1024)S(1)} reduce(s32[1024,1024]{1,0:T(8,128)} %param.12, s32[]{:T(128)} %constant.72.clone.1), dimensions={0}, to_apply=%region_0.0 | reduce | flops 1047552 | bytes 4198404 | tf_op jit(solution)/shard_map/reduce_sum | solution.py:65
  11.8 2.8 %fusion.4 = f32[512,1024]{1,0:T(8,128)S(1)} fusion(bf16[1024,1024]{1,0:T(8,128)(2,1)S(1)} %copy-done, s32[1024,1024]{1,0:T(8,128)} %param.12, s32[]{:T(128)S(6)} %select_n.97, s32[1024]{0:T(1024)S(1)} %copy-done.13), kind=kOutput, calls=%fused_computation.24 | convolution fusion | flops 1074790400 | bytes 6295556 | tf_op jit(solution)/shard_map/dot_general | solution.py:62
  14.7 0.4 add_convert_fusion
  15.1 21.6 %all_to_all.35 = bf16[16,32,1024]{2,1,0:T(8,128)(2,1)S(1)} all-to-all(bf16[16,32,1024]{2,1,0:T(8,128)(2,1)S(1)} %bitcast.75), channel_id=1, replica_groups=mesh['y'=4,'zh'=4,'c'=2,'x'=4,'zl'=2] {'y','x'}, dimensions={0} | all-to-all | bytes 2097152 | tf_op jit(solution)/shard_map/all_to_all | solution.py:25
  36.6 0.2 reduce_sum.197
  36.9 23.8 %all_to_all.36 = bf16[32,8,1024]{2,1,0:T(8,128)(2,1)S(1)} all-to-all(bf16[32,8,1024]{2,1,0:T(8,128)(2,1)S(1)} %bitcast.76), channel_id=1, replica_groups=mesh['y'=4,'zh'=4,'c'=2,'x'=4,'zl'=2] {'x','zh','zl'}, dimensions={0} | all-to-all | bytes 1048576 | tf_op jit(solution)/shard_map/all_to_all | solution.py:25
  61.0 0.2 convolution_convert_fusion.3
  61.1 0.2 convolution_convert_fusion.4
  61.3 0.7 broadcast_in_dim.16
  62.0 6.4 %all-to-all-start.2 = ((bf16[16,32,256]{2,1,0:T(8,128)(2,1)}), bf16[16,32,256]{2,1,0:T(8,128)(2,1)}, u32[]{:S(2)}, u32[]{:S(2)}) async-start(bf16[16,32,256]{2,1,0:T(8,128)(2,1)} %broadcast_in_dim.16), calls=%async_computation.2 | async-start | bytes 524288 | tf_op jit(solution)/shard_map/all_to_all | solution.py:25
  68.4 1.2 convolution_convert_fusion.5
  69.6 10.2 %all-to-all-done.2 = bf16[16,32,256]{2,1,0:T(8,128)(2,1)} async-done(((bf16[16,32,256]{2,1,0:T(8,128)(2,1)}), bf16[16,32,256]{2,1,0:T(8,128)(2,1)}, u32[]{:S(2)}, u32[]{:S(2)}) %all-to-all-start.2) | async-done | bytes 262176 | tf_op jit(solution)/shard_map/all_to_all | solution.py:25
  79.9 3.2 %collective-permute-start.1 = (bf16[512,256]{1,0:T(8,128)(2,1)}, bf16[512,256]{1,0:T(8,128)(2,1)S(1)}, u32[]{:S(2)}, u32[]{:S(2)}) collective-permute-start(bf16[512,256]{1,0:T(8,128)(2,1)} %bitcast.8), channel_id=1, source_target_pairs={{0,8},{8,0},{1,9},{9,1},{2,10},{10,2},{3,11},{11,3},{4,12},{12,4},... | collective-permute-start | bytes 786440 | tf_op jit(solution)/shard_map/ppermute | solution.py:33
  83.0 1.2 fusion.53
  84.2 1.0 fusion.16
  85.3 0.3 fusion.54
  85.5 0.4 copy-done.9
  85.9 1.3 convolution_convert_fusion.2
  87.3 13.3 %all_to_all.37 = bf16[8,32,1024]{2,1,0:T(8,128)(2,1)S(1)} all-to-all(bf16[8,32,1024]{2,1,0:T(8,128)(2,1)S(1)} %broadcast_in_dim.17), channel_id=1, replica_groups=mesh['y'=4,'zh'=4,'c'=2,'x'=4,'zl'=2] {'x','zl'}, dimensions={0} | all-to-all | bytes 1048576 | tf_op jit(solution)/shard_map/all_to_all | solution.py:25
  100.9 1.8 %convolution_convert_fusion.1 = bf16[32,1024]{1,0:T(8,128)(2,1)S(1)} fusion(bf16[512,1024]{1,0:T(8,128)(2,1)S(1)} %copy-done.3, bf16[1024,512]{1,0:T(8,128)(2,1)} %param.17, f32[1024]{0:T(1024)S(1)} %copy-done.10, f32[32]{0:T(128)S(1)} %add_rsqrt_fusion.2, f32[32,1024]{1,0:T(8,128)S(1)} %convert_reduce_fusion.2, f32[4,8,1024]{2,1,0:T(8,128)S(1)} %convert_reduce_fusion), kind=kOutput, calls=%fused_computation.12 | convolution fusion | flops 67420160 | bytes 2429056 | tf_op jit(solution)/shard_map/dot_general | solution.py:98
  102.8 11.3 %all_to_all.38 = bf16[8,32,1024]{2,1,0:T(8,128)(2,1)S(1)} all-to-all(bf16[8,32,1024]{2,1,0:T(8,128)(2,1)S(1)} %broadcast_in_dim.18), channel_id=1, replica_groups=mesh['y'=4,'zh'=4,'c'=2,'x'=4,'zl'=2] {'x','zl'}, dimensions={0} | all-to-all | bytes 1048576 | tf_op jit(solution)/shard_map/all_to_all | solution.py:25
  114.5 10.9 %all_to_all.39 = bf16[4,4,8,1024]{3,2,1,0:T(8,128)(2,1)S(1)} all-to-all(bf16[4,4,8,1024]{3,2,1,0:T(8,128)(2,1)S(1)} %broadcast_in_dim.19), channel_id=1, replica_groups=mesh['y'=4,'zh'=4,'c'=2,'x'=4,'zl'=2] {'zh'}, dimensions={0} | all-to-all | bytes 524288 | tf_op jit(solution)/shard_map/all_to_all | solution.py:25
  125.4 1.0 collective-permute-start.7
  126.4 1.0 collective-permute-start.5
  127.4 0.4 collective-permute-start.3
  127.9 4.6 %collective-permute-start.2 = (bf16[128,1024]{1,0:T(8,128)(2,1)S(1)}, bf16[128,1024]{1,0:T(8,128)(2,1)S(1)}, u32[]{:S(2)}, u32[]{:S(2)}) collective-permute-start(bf16[128,1024]{1,0:T(8,128)(2,1)S(1)} %bitcast.80), channel_id=1, source_target_pairs={{0,8},{8,0},{1,9},{9,1},{2,10},{10,2},{3,11},{11,3},{4,12},{12,4},... | collective-permute-start | bytes 786440 | tf_op jit(solution)/shard_map/ppermute | solution.py:33
  132.5 2.6 %subtract_reduce_fusion.7 = f32[1024]{0:T(1024)S(1)} fusion(bf16[128,1024]{1,0:T(8,128)(2,1)S(1)} %bitcast.81, bf16[1024,1024]{1,0:T(8,128)(2,1)} %param.22, s32[1024,1024]{1,0:T(8,128)} %param.12, s32[]{:T(128)S(6)} %select_n.115, f32[1024]{0:T(1024)S(1)} %copy-done.8), kind=kOutput, calls=%fused_computation.37 | convolution fusion | flops 269089792 | bytes 2891780 | tf_op jit(solution)/shard_map/dot_general | solution.py:120
  135.1 3.5 %collective-permute-start.8 = (bf16[128,1024]{1,0:T(8,128)(2,1)S(1)}, bf16[128,1024]{1,0:T(8,128)(2,1)S(1)}, u32[]{:S(2)}, u32[]{:S(2)}) collective-permute-start(bf16[128,1024]{1,0:T(8,128)(2,1)S(1)} %collective-permute-done.7), channel_id=1, source_target_pairs={{0,8},{8,0},{1,9},{9,1},{2,10},{10,2},{3,11},{11,3},{4,12},{12,4},... | collective-permute-start | bytes 786440 | tf_op jit(solution)/shard_map/ppermute | solution.py:33
  138.6 1.0 collective-permute-start.6
  139.7 1.7 collective-permute-start.4
  141.3 2.1 %subtract_reduce_fusion.1 = f32[1024]{0:T(1024)S(1)} fusion(bf16[128,1024]{1,0:T(8,128)(2,1)S(1)} %collective-permute-done.7, bf16[1024,1024]{1,0:T(8,128)(2,1)S(1)} %copy-done.1, s32[1024,1024]{1,0:T(8,128)} %param.12, s32[]{:T(128)S(6)} %select_n.121, f32[1024]{0:T(1024)S(1)} %copy-done.8), kind=kOutput, calls=%fused_computation.31 | convolution fusion | flops 269089792 | bytes 2891780 | tf_op jit(solution)/shard_map/dot_general | solution.py:120
  143.4 2.0 %subtract_reduce_fusion.3 = f32[1024]{0:T(1024)S(1)} fusion(bf16[128,1024]{1,0:T(8,128)(2,1)S(1)} %collective-permute-done.5, bf16[1024,1024]{1,0:T(8,128)(2,1)S(1)} %copy-done.1, s32[1024,1024]{1,0:T(8,128)} %param.12, s32[]{:T(128)S(6)} %select_n.119, f32[1024]{0:T(1024)S(1)} %copy-done.8), kind=kOutput, calls=%fused_computation.33 | convolution fusion | flops 269089792 | bytes 2891780 | tf_op jit(solution)/shard_map/dot_general | solution.py:120
  145.4 0.9 subtract_reduce_fusion.5
  146.3 0.9 subtract_reduce_fusion.6
  147.3 0.9 subtract_reduce_fusion
  148.2 0.9 subtract_reduce_fusion.2
  149.1 0.9 subtract_reduce_fusion.4
  150.0 0.6 fusion.51
  150.7 1.4 fusion.46
  152.0 0.7 broadcast_in_dim.20
  152.7 5.8 %all-to-all-start.6 = ((f32[256,1,128]{2,1,0:T(1,128)}), f32[256,1,128]{2,1,0:T(1,128)S(1)}, u32[]{:S(2)}, u32[]{:S(2)}) async-start(f32[256,1,128]{2,1,0:T(1,128)} %broadcast_in_dim.20), calls=%async_computation.6 | async-start | bytes 262144 | tf_op jit(solution)/shard_map/all_to_all | solution.py:25
  158.6 1.6 select_add_fusion
  160.2 0.6 multiply_divide_fusion
  160.8 10.8 %all-to-all-done.6 = f32[256,1,128]{2,1,0:T(1,128)S(1)} async-done(((f32[256,1,128]{2,1,0:T(1,128)}), f32[256,1,128]{2,1,0:T(1,128)S(1)}, u32[]{:S(2)}, u32[]{:S(2)}) %all-to-all-start.6) | async-done | bytes 131104 | tf_op jit(solution)/shard_map/all_to_all | solution.py:25
  171.6 0.6 fusion.52
  (56 shorter events, 1.2 us)
Async XLA Ops:
  0.6 1.6 copy-start
  6.1 5.7 %copy-start.13 = (s32[1024]{0:T(1024)S(1)}, s32[1024]{0:T(1024)}, u32[]{:S(2)}) copy-start(s32[1024]{0:T(1024)} %param.13) | copy-start | bytes 12292
  6.1 8.6 %collective-permute-start = (bf16[512,1024]{1,0:T(8,128)(2,1)}, bf16[512,1024]{1,0:T(8,128)(2,1)S(1)}, u32[]{:S(2)}, u32[]{:S(2)}) collective-permute-start(bf16[512,1024]{1,0:T(8,128)(2,1)} %convolution_convert_fusion), channel_id=1, source_target_pairs={{0,8},{8,0},{1,9},{9,1},{2,10},{10,2},{3,11},{11,3},{4,12},{12,4},... | collective-permute-start | bytes 3145736 | tf_op jit(solution)/shard_map/ppermute | solution.py:33
  36.6 24.2 %copy-start.12 = (f32[1024]{0:T(1024)S(1)}, f32[1024]{0:T(1024)}, u32[]{:S(2)}) copy-start(f32[1024]{0:T(1024)} %param.19) | copy-start | bytes 12292
  36.8 24.1 %copy-start.4 = (bf16[1024,3,128]{2,0,1:T(8,128)(2,1)S(1)}, bf16[1024,3,128]{2,0,1:T(8,128)(2,1)}, u32[]{:S(2)}) copy-start(bf16[1024,3,128]{2,0,1:T(8,128)(2,1)} %param.15) | copy-start | bytes 2359300
  62.0 17.8 %all-to-all-start.2 = ((bf16[16,32,256]{2,1,0:T(8,128)(2,1)}), bf16[16,32,256]{2,1,0:T(8,128)(2,1)}, u32[]{:S(2)}, u32[]{:S(2)}) async-start(bf16[16,32,256]{2,1,0:T(8,128)(2,1)} %broadcast_in_dim.16), calls=%async_computation.2 | async-start | bytes 524288 | tf_op jit(solution)/shard_map/all_to_all | solution.py:25
  68.4 32.4 %copy-start.3 = (bf16[512,1024]{1,0:T(8,128)(2,1)S(1)}, bf16[512,1024]{1,0:T(8,128)(2,1)}, u32[]{:S(2)}) copy-start(bf16[512,1024]{1,0:T(8,128)(2,1)} %param.18) | copy-start | bytes 3145732
  68.4 32.4 %copy-start.10 = (f32[1024]{0:T(1024)S(1)}, f32[1024]{0:T(1024)}, u32[]{:S(2)}) copy-start(f32[1024]{0:T(1024)} %param.20) | copy-start | bytes 12292
  79.9 5.4 %collective-permute-start.1 = (bf16[512,256]{1,0:T(8,128)(2,1)}, bf16[512,256]{1,0:T(8,128)(2,1)S(1)}, u32[]{:S(2)}, u32[]{:S(2)}) collective-permute-start(bf16[512,256]{1,0:T(8,128)(2,1)} %bitcast.8), channel_id=1, source_target_pairs={{0,8},{8,0},{1,9},{9,1},{2,10},{10,2},{3,11},{11,3},{4,12},{12,4},... | collective-permute-start | bytes 786440 | tf_op jit(solution)/shard_map/ppermute | solution.py:33
  85.2 0.7 copy-start.9
  100.9 13.5 %copy-start.11 = (f32[1024]{0:T(1024)S(1)}, f32[1024]{0:T(1024)}, u32[]{:S(2)}) copy-start(f32[1024]{0:T(1024)} %param.21) | copy-start | bytes 12292
  102.8 29.7 %copy-start.8 = (f32[1024]{0:T(1024)S(1)}, f32[1024]{0:T(1024)}, u32[]{:S(2)}) copy-start(f32[1024]{0:T(1024)} %param.23) | copy-start | bytes 12292
  125.4 9.7 %collective-permute-start.7 = (bf16[128,1024]{1,0:T(8,128)(2,1)S(1)}, bf16[128,1024]{1,0:T(8,128)(2,1)S(1)}, u32[]{:S(2)}, u32[]{:S(2)}) collective-permute-start(bf16[128,1024]{1,0:T(8,128)(2,1)S(1)} %bitcast.77), channel_id=1, source_target_pairs={{0,128},{64,192},{128,0},{192,64},{1,129},{65,193},{129,1},{193,65... | collective-permute-start | bytes 786440 | tf_op jit(solution)/shard_map/ppermute | solution.py:105
  126.4 12.2 %collective-permute-start.5 = (bf16[128,1024]{1,0:T(8,128)(2,1)S(1)}, bf16[128,1024]{1,0:T(8,128)(2,1)S(1)}, u32[]{:S(2)}, u32[]{:S(2)}) collective-permute-start(bf16[128,1024]{1,0:T(8,128)(2,1)S(1)} %bitcast.78), channel_id=1, source_target_pairs={{0,192},{64,0},{128,64},{192,128},{1,193},{65,1},{129,65},{193,129... | collective-permute-start | bytes 786440 | tf_op jit(solution)/shard_map/ppermute | solution.py:105
  127.4 12.2 %collective-permute-start.3 = (bf16[128,1024]{1,0:T(8,128)(2,1)S(1)}, bf16[128,1024]{1,0:T(8,128)(2,1)S(1)}, u32[]{:S(2)}, u32[]{:S(2)}) collective-permute-start(bf16[128,1024]{1,0:T(8,128)(2,1)S(1)} %bitcast.79), channel_id=1, source_target_pairs={{0,64},{64,128},{128,192},{192,0},{1,65},{65,129},{129,193},{193,1... | collective-permute-start | bytes 786440 | tf_op jit(solution)/shard_map/ppermute | solution.py:105
  127.9 13.5 %copy-start.1 = (bf16[1024,1024]{1,0:T(8,128)(2,1)S(1)}, bf16[1024,1024]{1,0:T(8,128)(2,1)}, u32[]{:S(2)}) copy-start(bf16[1024,1024]{1,0:T(8,128)(2,1)} %param.22) | copy-start | bytes 6291460
  127.9 18.5 %collective-permute-start.2 = (bf16[128,1024]{1,0:T(8,128)(2,1)S(1)}, bf16[128,1024]{1,0:T(8,128)(2,1)S(1)}, u32[]{:S(2)}, u32[]{:S(2)}) collective-permute-start(bf16[128,1024]{1,0:T(8,128)(2,1)S(1)} %bitcast.80), channel_id=1, source_target_pairs={{0,8},{8,0},{1,9},{9,1},{2,10},{10,2},{3,11},{11,3},{4,12},{12,4},... | collective-permute-start | bytes 786440 | tf_op jit(solution)/shard_map/ppermute | solution.py:33
  135.1 12.2 %collective-permute-start.8 = (bf16[128,1024]{1,0:T(8,128)(2,1)S(1)}, bf16[128,1024]{1,0:T(8,128)(2,1)S(1)}, u32[]{:S(2)}, u32[]{:S(2)}) collective-permute-start(bf16[128,1024]{1,0:T(8,128)(2,1)S(1)} %collective-permute-done.7), channel_id=1, source_target_pairs={{0,8},{8,0},{1,9},{9,1},{2,10},{10,2},{3,11},{11,3},{4,12},{12,4},... | collective-permute-start | bytes 786440 | tf_op jit(solution)/shard_map/ppermute | solution.py:33
  138.6 9.6 %collective-permute-start.6 = (bf16[128,1024]{1,0:T(8,128)(2,1)S(1)}, bf16[128,1024]{1,0:T(8,128)(2,1)S(1)}, u32[]{:S(2)}, u32[]{:S(2)}) collective-permute-start(bf16[128,1024]{1,0:T(8,128)(2,1)S(1)} %collective-permute-done.5), channel_id=1, source_target_pairs={{0,8},{8,0},{1,9},{9,1},{2,10},{10,2},{3,11},{11,3},{4,12},{12,4},... | collective-permute-start | bytes 786440 | tf_op jit(solution)/shard_map/ppermute | solution.py:33
  139.7 9.4 %collective-permute-start.4 = (bf16[128,1024]{1,0:T(8,128)(2,1)S(1)}, bf16[128,1024]{1,0:T(8,128)(2,1)S(1)}, u32[]{:S(2)}, u32[]{:S(2)}) collective-permute-start(bf16[128,1024]{1,0:T(8,128)(2,1)S(1)} %collective-permute-done.3), channel_id=1, source_target_pairs={{0,8},{8,0},{1,9},{9,1},{2,10},{10,2},{3,11},{11,3},{4,12},{12,4},... | collective-permute-start | bytes 786440 | tf_op jit(solution)/shard_map/ppermute | solution.py:33
  141.3 4.1 %copy-start.2 = (s32[1024,1024]{1,0:T(8,128)S(1)}, s32[1024,1024]{1,0:T(8,128)}, u32[]{:S(2)}) copy-start(s32[1024,1024]{1,0:T(8,128)} %param.12) | copy-start | bytes 12582916
  147.3 1.8 %copy-start.5 = (bf16[128,1024]{1,0:T(8,128)(2,1)}, bf16[128,1024]{1,0:T(8,128)(2,1)S(1)}, u32[]{:S(2)}) copy-start(bf16[128,1024]{1,0:T(8,128)(2,1)S(1)} %collective-permute-done.8) | copy-start | bytes 786436
  148.2 1.8 %copy-start.6 = (bf16[128,1024]{1,0:T(8,128)(2,1)}, bf16[128,1024]{1,0:T(8,128)(2,1)S(1)}, u32[]{:S(2)}) copy-start(bf16[128,1024]{1,0:T(8,128)(2,1)S(1)} %collective-permute-done.6) | copy-start | bytes 786436
  149.1 1.5 copy-start.7
  152.7 18.8 %all-to-all-start.6 = ((f32[256,1,128]{2,1,0:T(1,128)}), f32[256,1,128]{2,1,0:T(1,128)S(1)}, u32[]{:S(2)}, u32[]{:S(2)}) async-start(f32[256,1,128]{2,1,0:T(1,128)} %broadcast_in_dim.20), calls=%async_computation.6 | async-start | bytes 262144 | tf_op jit(solution)/shard_map/all_to_all | solution.py:25

commit v3 on v2

--- a/solution.py
+++ b/solution.py
@@ -11,9 +11,7 @@
 F32 = jnp.float32
 ROWS = ("y", "zh", "c")
 TM = ("x", "zl")
-YZ = ("y", "zh")
 PLANE = ("y", "x")
-COLUMN = ("x", "zh", "zl")
 ALL = ("y", "zh", "c", "x", "zl")
 
 
@@ -52,7 +50,6 @@
     half = frames_all // 2
     rows_here = frames_all // lax.axis_size(ROWS)
     chunk = half // lax.axis_size("y")
-    piece = chunk // (lax.axis_size("x") * lax.axis_size("zh"))
     core = lax.axis_index("c")
     y_at = lax.axis_index("y")
 
@@ -66,32 +63,33 @@
     theirs, counts = lax.optimization_barrier((theirs, counts))
     chip_sum = (readin(core * half) + theirs.astype(F32)).astype(BF16)
     plane_sum = jnp.sum(exchange(chip_sum.reshape(16, -1, model_dim), PLANE).astype(F32), 0)
-    blocks = jnp.broadcast_to(
-        plane_sum.astype(BF16).reshape(1, 4, 1, piece, model_dim), (4, 4, 2, piece, model_dim)
-    )
-    parts = exchange(blocks.reshape(32, piece, model_dim), COLUMN)
-    stream = jnp.sum(parts.reshape(4, 8, piece, model_dim).astype(F32), 1)
-    stream = stream.reshape(rows_here, model_dim)
+    stream = jnp.sum(to_all(plane_sum.astype(BF16), ("zh", "zl")).astype(F32), 0)
 
-    attn_in = normed(stream, norm_gain).astype(BF16)
-    queries, keys, values = (
-        jnp.dot(attn_in, qkv_weight[:, i], preferred_element_type=F32).astype(BF16)
-        for i in range(3)
-    )
-    kv_near = to_all(jnp.concatenate([keys, values], 1), YZ).reshape(half, 2 * HEAD_DIM)
-    kv_far = other_core(kv_near)
+    attn_own = normed(stream, norm_gain).astype(BF16)
+    attn_near = to_all(attn_own, PLANE).reshape(half, model_dim)
+    attn_far = other_core(attn_near)
+
+    def project(frames, part):
+        return jnp.dot(frames, qkv_weight[:, part], preferred_element_type=F32).astype(BF16)
+
+    own_start = y_at * chunk + lax.axis_index("zh") * rows_here
+    queries = project(lax.dynamic_slice_in_dim(attn_near, own_start, rows_here, 0), 0)
     numerator = 0.0
     denominator = 0.0
-    for kv in (kv_near, kv_far):
+    for frames in (attn_near, attn_far):
         scores = lax.dot_general(
-            queries, kv[:, :HEAD_DIM], (((1,), (1,)), ((), ())), preferred_element_type=F32
+            queries, project(frames, 1), (((1,), (1,)), ((), ())), preferred_element_type=F32
         )
         weights = jnp.exp(scores * (1.0 / math.sqrt(HEAD_DIM)))
-        numerator += jnp.dot(weights.astype(BF16), kv[:, HEAD_DIM:], preferred_element_type=F32)
+        numerator += jnp.dot(
+            weights.astype(BF16), project(frames, 2), preferred_element_type=F32
+        )
         denominator += jnp.sum(weights, -1, keepdims=True)
     heads_out = (numerator / denominator).astype(BF16)
     attn_part = jnp.dot(heads_out, out_weight, preferred_element_type=F32)
-    mixed_state = stream + jnp.sum(to_all(attn_part.astype(BF16), TM).astype(F32), 0)
+    holder = (lax.axis_index("x") == lax.axis_index("zh")) & (lax.axis_index("zl") == 0)
+    attn_part += jnp.where(holder, stream, jnp.zeros_like(stream))
+    mixed_state = jnp.sum(to_all(attn_part.astype(BF16), TM).astype(F32), 0)
 
     mlp_in = normed(mixed_state, mlp_gain).astype(BF16)
     hidden_act = jax.nn.gelu(jnp.dot(mlp_in, up_weight, preferred_element_type=F32)).astype(BF16)
@@ -99,8 +97,7 @@
     final_state = mixed_state + jnp.sum(to_all(mlp_part.astype(BF16), TM).astype(F32), 0)
     own_latents = normed(final_state, final_gain).astype(BF16)
 
-    spread = to_all(own_latents.reshape(4, piece, model_dim), "zh")
-    first = jnp.swapaxes(spread.reshape(4, 4, piece, model_dim), 0, 1).reshape(chunk, model_dim)
+    first = to_all(own_latents, "zh").reshape(chunk, model_dim)
     near = [first] + [
         lax.ppermute(first, "y", [(i, (i + k) % 4) for i in range(4)]) for k in (1, 3, 2)
     ]

time: 175 us -> 180 us (1.029)
  blocking collectives: 80.8 us -> 98 us
  waiting for transfers between devices: 21 us -> 10.8 us
  starting transfers between devices: 31.9 us -> 26.7 us
  matrix products: 24.9 us -> 29 us
    all_to_all x5 -> x6, blocking collectives: 80.8 us -> 98 us  [exchange(): return lax.all_to_all(blocks, axes, 0, 0, tiled=True)]
    all_to_all x2 -> x1, waiting for transfers between devices: 21 us -> 10.8 us  [exchange(): return lax.all_to_all(blocks, axes, 0, 0, tiled=True)]
    all_to_all x2 -> x1, starting transfers between devices: 12.2 us -> 6.18 us  [exchange(): return lax.all_to_all(blocks, axes, 0, 0, tiled=True)]
    dot_general x6 -> x5, matrix products: 4 us -> 8.32 us  [the longest x2 3.72 us: on_device(): lax.dot_general(queries, project(frames, 1), (((1,), (1,)), ((), ())), pr...]
  transfers between devices with their start and end apart: 11 -> 10, of which waited for: 2 -> 1; matrix products, arithmetic and copies ran while one was open for 12% -> 12% of each run, Pallas kernels for 0% -> 0%
where the time goes in v3:
time: 180 us; the launch traced here: 179 us
  blocking collectives  98 us (54%)
  matrix products  29 us (16%)
  starting transfers between devices  26.7 us (15%)
  waiting for transfers between devices  10.8 us (6%)
  other arithmetic  8.14 us (5%)
  between operations  3.5 us (2%)
  local copies, waits for them, and re-layouts  3.24 us (2%)
    all_to_all x6, blocking collectives, exchange(): return lax.all_to_all(blocks, axes, 0, 0, tiled=True)  98 us
    ppermute x6, starting transfers between devices, other_core(): return lax.ppermute(block, 'c', [(0, 1), (1, 0)])  18.6 us
    dot_general x8, matrix products, on_device(): lax.dot_general(lat, readout_weight, (((1,), (1,)), ((), ())), preferred_...  11.1 us
    all_to_all x1, waiting for transfers between devices, exchange(): return lax.all_to_all(blocks, axes, 0, 0, tiled=True)  10.8 us
    dot_general x2, matrix products, readin(): return jnp.dot(masked, readin_weight, preferred_element_type=F32)  6.68 us
    all_to_all x1, starting transfers between devices, exchange(): return lax.all_to_all(blocks, axes, 0, 0, tiled=True)  6.18 us
    dot_general x2, matrix products, on_device(): lax.dot_general(queries, project(frames, 1), (((1,), (1,)), ((), ())), pr...  3.72 us
  transfers between devices with their start and end apart: 10, of which 1 were waited for; matrix products, arithmetic and copies ran while one was open for 12% of the time, Pallas kernels for 0%

profile of v3, /device:TPU:1, one launch (start us, length us, event | category | flops | bytes accessed | tf_op | source)
XLA Modules:
  0.0 179.4 jit_solution(13359966689932846569)
XLA Ops:
  0.7 1.6 copy-done
  2.2 3.8 %convolution_convert_fusion = bf16[512,1024]{1,0:T(8,128)(2,1)} fusion(bf16[1024,1024]{1,0:T(8,128)(2,1)S(1)} %copy-done, s32[1024,1024]{1,0:T(8,128)} %param.12, s32[]{:T(128)S(6)} %select_n.109, s32[1024]{0:T(1024)} %param.13), kind=kOutput, calls=%fused_computation.3 | convolution fusion | flops 1075314688 | bytes 5246980 | tf_op jit(solution)/shard_map/dot_general | solution.py:59
  6.1 3.2 %collective-permute-start = (bf16[512,1024]{1,0:T(8,128)(2,1)}, bf16[512,1024]{1,0:T(8,128)(2,1)S(1)}, u32[]{:S(2)}, u32[]{:S(2)}) collective-permute-start(bf16[512,1024]{1,0:T(8,128)(2,1)} %convolution_convert_fusion), channel_id=1, source_target_pairs={{0,8},{8,0},{1,9},{9,1},{2,10},{10,2},{3,11},{11,3},{4,12},{12,4},... | collective-permute-start | bytes 3145736 | tf_op jit(solution)/shard_map/ppermute | solution.py:31
  9.3 2.5 %reduce_sum.192 = s32[1024]{0:T(1024)S(1)} reduce(s32[1024,1024]{1,0:T(8,128)} %param.12, s32[]{:T(128)} %constant.77.clone.1), dimensions={0}, to_apply=%region_0.0 | reduce | flops 1047552 | bytes 4198404 | tf_op jit(solution)/shard_map/reduce_sum | solution.py:62
  11.8 2.8 %fusion.12 = f32[512,1024]{1,0:T(8,128)S(1)} fusion(bf16[1024,1024]{1,0:T(8,128)(2,1)S(1)} %copy-done, s32[1024,1024]{1,0:T(8,128)} %param.12, s32[]{:T(128)S(6)} %select_n.108, s32[1024]{0:T(1024)S(1)} %copy-done.11), kind=kOutput, calls=%fused_computation.31 | convolution fusion | flops 1074790400 | bytes 6295556 | tf_op jit(solution)/shard_map/dot_general | solution.py:59
  14.7 0.4 add_convert_fusion
  15.1 21.6 %all_to_all.35 = bf16[16,32,1024]{2,1,0:T(8,128)(2,1)S(1)} all-to-all(bf16[16,32,1024]{2,1,0:T(8,128)(2,1)S(1)} %bitcast.58), channel_id=1, replica_groups=mesh['y'=4,'zh'=4,'c'=2,'x'=4,'zl'=2] {'y','x'}, dimensions={0} | all-to-all | bytes 2097152 | tf_op jit(solution)/shard_map/all_to_all | solution.py:23
  36.6 0.2 reduce_sum.193
  36.9 23.0 %all_to_all.36 = bf16[8,32,1024]{2,1,0:T(8,128)(2,1)S(1)} all-to-all(bf16[8,32,1024]{2,1,0:T(8,128)(2,1)S(1)} %broadcast_in_dim.14), channel_id=1, replica_groups=mesh['y'=4,'zh'=4,'c'=2,'x'=4,'zl'=2] {'zh','zl'}, dimensions={0} | all-to-all | bytes 1048576 | tf_op jit(solution)/shard_map/all_to_all | solution.py:23
  60.0 0.1 multiply_reduce_fusion.2
  60.2 0.1 broadcast_in_dim.15
  60.3 18.1 %all_to_all.37 = bf16[16,32,1024]{2,1,0:T(8,128)(2,1)S(1)} all-to-all(bf16[16,32,1024]{2,1,0:T(8,128)(2,1)S(1)} %broadcast_in_dim.15), channel_id=1, replica_groups=mesh['y'=4,'zh'=4,'c'=2,'x'=4,'zl'=2] {'y','x'}, dimensions={0} | all-to-all | bytes 2097152 | tf_op jit(solution)/shard_map/all_to_all | solution.py:23
  78.5 4.0 %collective-permute-start.1 = (bf16[512,1024]{1,0:T(8,128)(2,1)S(1)}, bf16[512,1024]{1,0:T(8,128)(2,1)}, u32[]{:S(2)}, u32[]{:S(2)}) collective-permute-start(bf16[512,1024]{1,0:T(8,128)(2,1)S(1)} %bitcast.65), channel_id=1, source_target_pairs={{0,8},{8,0},{1,9},{9,1},{2,10},{10,2},{3,11},{11,3},{4,12},{12,4},... | collective-permute-start | bytes 3145736 | tf_op jit(solution)/shard_map/ppermute | solution.py:31
  82.5 1.1 convolution_convert_fusion.6
  83.6 1.7 fusion.63
  85.3 1.5 fusion.2
  86.8 2.0 %fusion.66 = (f32[32]{0:T(128)S(1)}, bf16[32,512]{1,0:T(8,128)(2,1)S(1)}) fusion(bf16[32,128]{1,0:T(8,128)(2,1)S(1)} %convolution_convert_fusion.6, bf16[512,1024]{1,0:T(8,128)(2,1)} %collective-permute-done.1, bf16[1024,3,128]{2,0,1:T(8,128)(2,1)} %param.15), kind=kOutput, calls=%fused_computation.100 | convolution fusion | flops 138526688 | bytes 1351808 | tf_op jit(solution)/shard_map/dot_general | solution.py:80
  88.9 2.0 %fusion.11 = bf16[32,128]{1,0:T(8,128)(2,1)S(1)} fusion(f32[32,128]{1,0:T(8,128)S(1)} %fusion.2, bf16[512,1024]{1,0:T(8,128)(2,1)} %collective-permute-done.1, bf16[1024,3,128]{2,0,1:T(8,128)(2,1)} %param.15, bf16[32,512]{1,0:T(8,128)(2,1)S(1)} %get-tuple-element.17, f32[32]{0:T(128)S(1)} %add.263), kind=kOutput, calls=%fused_computation.29 | convolution fusion | flops 138489856 | bytes 1368192 | tf_op jit(solution)/shard_map/dot_general | solution.py:84
  90.9 1.1 fusion.4
  92.1 12.4 %all_to_all.38 = bf16[8,32,1024]{2,1,0:T(8,128)(2,1)S(1)} all-to-all(bf16[8,32,1024]{2,1,0:T(8,128)(2,1)S(1)} %broadcast_in_dim.17), channel_id=1, replica_groups=mesh['y'=4,'zh'=4,'c'=2,'x'=4,'zl'=2] {'x','zl'}, dimensions={0} | all-to-all | bytes 1048576 | tf_op jit(solution)/shard_map/all_to_all | solution.py:23
  104.5 0.1 multiply_reduce_fusion.1
  104.7 1.8 %convolution_convert_fusion.5 = bf16[32,1024]{1,0:T(8,128)(2,1)S(1)} fusion(bf16[512,1024]{1,0:T(8,128)(2,1)S(1)} %copy-done.3, bf16[1024,512]{1,0:T(8,128)(2,1)} %param.17, f32[32,1024]{1,0:T(8,128)S(1)} %convert_reduce_fusion.1, f32[1024]{0:T(1024)S(1)} %copy-done.8, f32[32]{0:T(128)S(1)} %add_rsqrt_fusion.1), kind=kOutput, calls=%fused_computation.22 | convolution fusion | flops 67387392 | bytes 2297984 | tf_op jit(solution)/shard_map/dot_general | solution.py:96
  106.6 12.0 %all_to_all.39 = bf16[8,32,1024]{2,1,0:T(8,128)(2,1)S(1)} all-to-all(bf16[8,32,1024]{2,1,0:T(8,128)(2,1)S(1)} %broadcast_in_dim.18), channel_id=1, replica_groups=mesh['y'=4,'zh'=4,'c'=2,'x'=4,'zl'=2] {'x','zl'}, dimensions={0} | all-to-all | bytes 1048576 | tf_op jit(solution)/shard_map/all_to_all | solution.py:23
  118.6 0.1 multiply_reduce_fusion
  118.9 10.9 %all_to_all.40 = bf16[4,32,1024]{2,1,0:T(8,128)(2,1)S(1)} all-to-all(bf16[4,32,1024]{2,1,0:T(8,128)(2,1)S(1)} %broadcast_in_dim.19), channel_id=1, replica_groups=mesh['y'=4,'zh'=4,'c'=2,'x'=4,'zl'=2] {'zh'}, dimensions={0} | all-to-all | bytes 524288 | tf_op jit(solution)/shard_map/all_to_all | solution.py:23
  129.8 0.4 collective-permute-start.7
  130.2 0.8 collective-permute-start.5
  131.0 0.7 collective-permute-start.3
  131.7 5.2 %collective-permute-start.2 = (bf16[128,1024]{1,0:T(8,128)(2,1)S(1)}, bf16[128,1024]{1,0:T(8,128)(2,1)S(1)}, u32[]{:S(2)}, u32[]{:S(2)}) collective-permute-start(bf16[128,1024]{1,0:T(8,128)(2,1)S(1)} %bitcast.62), channel_id=1, source_target_pairs={{0,8},{8,0},{1,9},{9,1},{2,10},{10,2},{3,11},{11,3},{4,12},{12,4},... | collective-permute-start | bytes 786440 | tf_op jit(solution)/shard_map/ppermute | solution.py:31
  136.9 2.6 %subtract_reduce_fusion.7 = f32[1024]{0:T(1024)S(1)} fusion(bf16[128,1024]{1,0:T(8,128)(2,1)S(1)} %bitcast.63, bf16[1024,1024]{1,0:T(8,128)(2,1)} %param.22, s32[1024,1024]{1,0:T(8,128)} %param.12, s32[]{:T(128)S(6)} %select_n.129, f32[1024]{0:T(1024)S(1)} %copy-done.7), kind=kOutput, calls=%fused_computation.44 | convolution fusion | flops 269089792 | bytes 2891780 | tf_op jit(solution)/shard_map/dot_general | solution.py:117
  139.5 3.5 %collective-permute-start.8 = (bf16[128,1024]{1,0:T(8,128)(2,1)S(1)}, bf16[128,1024]{1,0:T(8,128)(2,1)S(1)}, u32[]{:S(2)}, u32[]{:S(2)}) collective-permute-start(bf16[128,1024]{1,0:T(8,128)(2,1)S(1)} %collective-permute-done.7), channel_id=1, source_target_pairs={{0,8},{8,0},{1,9},{9,1},{2,10},{10,2},{3,11},{11,3},{4,12},{12,4},... | collective-permute-start | bytes 786440 | tf_op jit(solution)/shard_map/ppermute | solution.py:31
  143.0 0.9 collective-permute-start.6
  143.9 1.7 collective-permute-start.4
  145.6 2.1 %subtract_reduce_fusion.1 = f32[1024]{0:T(1024)S(1)} fusion(bf16[128,1024]{1,0:T(8,128)(2,1)S(1)} %collective-permute-done.7, bf16[1024,1024]{1,0:T(8,128)(2,1)S(1)} %copy-done.1, s32[1024,1024]{1,0:T(8,128)} %param.12, s32[]{:T(128)S(6)} %select_n.135, f32[1024]{0:T(1024)S(1)} %copy-done.7), kind=kOutput, calls=%fused_computation.38 | convolution fusion | flops 269089792 | bytes 2891780 | tf_op jit(solution)/shard_map/dot_general | solution.py:117
  147.7 2.0 %subtract_reduce_fusion.3 = f32[1024]{0:T(1024)S(1)} fusion(bf16[128,1024]{1,0:T(8,128)(2,1)S(1)} %collective-permute-done.5, bf16[1024,1024]{1,0:T(8,128)(2,1)S(1)} %copy-done.1, s32[1024,1024]{1,0:T(8,128)} %param.12, s32[]{:T(128)S(6)} %select_n.133, f32[1024]{0:T(1024)S(1)} %copy-done.7), kind=kOutput, calls=%fused_computation.40 | convolution fusion | flops 269089792 | bytes 2891780 | tf_op jit(solution)/shard_map/dot_general | solution.py:117
  149.7 0.9 subtract_reduce_fusion.5
  150.6 0.9 subtract_reduce_fusion.6
  151.6 0.9 subtract_reduce_fusion
  152.5 0.9 subtract_reduce_fusion.2
  153.4 0.9 subtract_reduce_fusion.4
  154.3 0.6 fusion.61
  155.0 1.4 fusion.56
  156.3 0.7 broadcast_in_dim.20
  157.0 6.2 %all-to-all-start.6 = ((f32[256,1,128]{2,1,0:T(1,128)}), f32[256,1,128]{2,1,0:T(1,128)S(1)}, u32[]{:S(2)}, u32[]{:S(2)}) async-start(f32[256,1,128]{2,1,0:T(1,128)} %broadcast_in_dim.20), calls=%async_computation.6 | async-start | bytes 262144 | tf_op jit(solution)/shard_map/all_to_all | solution.py:23
  163.2 1.6 select_add_fusion
  164.9 0.6 multiply_divide_fusion
  165.5 10.8 %all-to-all-done.6 = f32[256,1,128]{2,1,0:T(1,128)S(1)} async-done(((f32[256,1,128]{2,1,0:T(1,128)}), f32[256,1,128]{2,1,0:T(1,128)S(1)}, u32[]{:S(2)}, u32[]{:S(2)}) %all-to-all-start.6) | async-done | bytes 131104 | tf_op jit(solution)/shard_map/all_to_all | solution.py:23
  176.3 0.6 fusion.62
  (47 shorter events, 0.7 us)
Async XLA Ops:
  0.6 1.6 copy-start
  6.1 5.7 %copy-start.11 = (s32[1024]{0:T(1024)S(1)}, s32[1024]{0:T(1024)}, u32[]{:S(2)}) copy-start(s32[1024]{0:T(1024)} %param.13) | copy-start | bytes 12292
  6.1 8.6 %collective-permute-start = (bf16[512,1024]{1,0:T(8,128)(2,1)}, bf16[512,1024]{1,0:T(8,128)(2,1)S(1)}, u32[]{:S(2)}, u32[]{:S(2)}) collective-permute-start(bf16[512,1024]{1,0:T(8,128)(2,1)} %convolution_convert_fusion), channel_id=1, source_target_pairs={{0,8},{8,0},{1,9},{9,1},{2,10},{10,2},{3,11},{11,3},{4,12},{12,4},... | collective-permute-start | bytes 3145736 | tf_op jit(solution)/shard_map/ppermute | solution.py:31
  36.6 23.5 %copy-start.9 = (f32[1024]{0:T(1024)S(1)}, f32[1024]{0:T(1024)}, u32[]{:S(2)}) copy-start(f32[1024]{0:T(1024)} %param.19) | copy-start | bytes 12292
  78.5 8.4 %collective-permute-start.1 = (bf16[512,1024]{1,0:T(8,128)(2,1)S(1)}, bf16[512,1024]{1,0:T(8,128)(2,1)}, u32[]{:S(2)}, u32[]{:S(2)}) collective-permute-start(bf16[512,1024]{1,0:T(8,128)(2,1)S(1)} %bitcast.65), channel_id=1, source_target_pairs={{0,8},{8,0},{1,9},{9,1},{2,10},{10,2},{3,11},{11,3},{4,12},{12,4},... | collective-permute-start | bytes 3145736 | tf_op jit(solution)/shard_map/ppermute | solution.py:31
  88.9 15.8 %copy-start.3 = (bf16[512,1024]{1,0:T(8,128)(2,1)S(1)}, bf16[512,1024]{1,0:T(8,128)(2,1)}, u32[]{:S(2)}) copy-start(bf16[512,1024]{1,0:T(8,128)(2,1)} %param.18) | copy-start | bytes 3145732
  88.9 15.8 %copy-start.8 = (f32[1024]{0:T(1024)S(1)}, f32[1024]{0:T(1024)}, u32[]{:S(2)}) copy-start(f32[1024]{0:T(1024)} %param.20) | copy-start | bytes 12292
  104.6 14.1 %copy-start.10 = (f32[1024]{0:T(1024)S(1)}, f32[1024]{0:T(1024)}, u32[]{:S(2)}) copy-start(f32[1024]{0:T(1024)} %param.21) | copy-start | bytes 12292
  106.5 30.4 %copy-start.7 = (f32[1024]{0:T(1024)S(1)}, f32[1024]{0:T(1024)}, u32[]{:S(2)}) copy-start(f32[1024]{0:T(1024)} %param.23) | copy-start | bytes 12292
  129.8 9.7 %collective-permute-start.7 = (bf16[128,1024]{1,0:T(8,128)(2,1)S(1)}, bf16[128,1024]{1,0:T(8,128)(2,1)S(1)}, u32[]{:S(2)}, u32[]{:S(2)}) collective-permute-start(bf16[128,1024]{1,0:T(8,128)(2,1)S(1)} %bitcast.59), channel_id=1, source_target_pairs={{0,128},{64,192},{128,0},{192,64},{1,129},{65,193},{129,1},{193,65... | collective-permute-start | bytes 786440 | tf_op jit(solution)/shard_map/ppermute | solution.py:102
  130.2 12.8 %collective-permute-start.5 = (bf16[128,1024]{1,0:T(8,128)(2,1)S(1)}, bf16[128,1024]{1,0:T(8,128)(2,1)S(1)}, u32[]{:S(2)}, u32[]{:S(2)}) collective-permute-start(bf16[128,1024]{1,0:T(8,128)(2,1)S(1)} %bitcast.60), channel_id=1, source_target_pairs={{0,192},{64,0},{128,64},{192,128},{1,193},{65,1},{129,65},{193,129... | collective-permute-start | bytes 786440 | tf_op jit(solution)/shard_map/ppermute | solution.py:102
  131.0 12.9 %collective-permute-start.3 = (bf16[128,1024]{1,0:T(8,128)(2,1)S(1)}, bf16[128,1024]{1,0:T(8,128)(2,1)S(1)}, u32[]{:S(2)}, u32[]{:S(2)}) collective-permute-start(bf16[128,1024]{1,0:T(8,128)(2,1)S(1)} %bitcast.61), channel_id=1, source_target_pairs={{0,64},{64,128},{128,192},{192,0},{1,65},{65,129},{129,193},{193,1... | collective-permute-start | bytes 786440 | tf_op jit(solution)/shard_map/ppermute | solution.py:102
  131.7 14.0 %copy-start.1 = (bf16[1024,1024]{1,0:T(8,128)(2,1)S(1)}, bf16[1024,1024]{1,0:T(8,128)(2,1)}, u32[]{:S(2)}) copy-start(bf16[1024,1024]{1,0:T(8,128)(2,1)} %param.22) | copy-start | bytes 6291460
  131.7 19.0 %collective-permute-start.2 = (bf16[128,1024]{1,0:T(8,128)(2,1)S(1)}, bf16[128,1024]{1,0:T(8,128)(2,1)S(1)}, u32[]{:S(2)}, u32[]{:S(2)}) collective-permute-start(bf16[128,1024]{1,0:T(8,128)(2,1)S(1)} %bitcast.62), channel_id=1, source_target_pairs={{0,8},{8,0},{1,9},{9,1},{2,10},{10,2},{3,11},{11,3},{4,12},{12,4},... | collective-permute-start | bytes 786440 | tf_op jit(solution)/shard_map/ppermute | solution.py:31
  139.5 12.1 %collective-permute-start.8 = (bf16[128,1024]{1,0:T(8,128)(2,1)S(1)}, bf16[128,1024]{1,0:T(8,128)(2,1)S(1)}, u32[]{:S(2)}, u32[]{:S(2)}) collective-permute-start(bf16[128,1024]{1,0:T(8,128)(2,1)S(1)} %collective-permute-done.7), channel_id=1, source_target_pairs={{0,8},{8,0},{1,9},{9,1},{2,10},{10,2},{3,11},{11,3},{4,12},{12,4},... | collective-permute-start | bytes 786440 | tf_op jit(solution)/shard_map/ppermute | solution.py:31
  143.0 9.5 %collective-permute-start.6 = (bf16[128,1024]{1,0:T(8,128)(2,1)S(1)}, bf16[128,1024]{1,0:T(8,128)(2,1)S(1)}, u32[]{:S(2)}, u32[]{:S(2)}) collective-permute-start(bf16[128,1024]{1,0:T(8,128)(2,1)S(1)} %collective-permute-done.5), channel_id=1, source_target_pairs={{0,8},{8,0},{1,9},{9,1},{2,10},{10,2},{3,11},{11,3},{4,12},{12,4},... | collective-permute-start | bytes 786440 | tf_op jit(solution)/shard_map/ppermute | solution.py:31
  143.9 9.5 %collective-permute-start.4 = (bf16[128,1024]{1,0:T(8,128)(2,1)S(1)}, bf16[128,1024]{1,0:T(8,128)(2,1)S(1)}, u32[]{:S(2)}, u32[]{:S(2)}) collective-permute-start(bf16[128,1024]{1,0:T(8,128)(2,1)S(1)} %collective-permute-done.3), channel_id=1, source_target_pairs={{0,8},{8,0},{1,9},{9,1},{2,10},{10,2},{3,11},{11,3},{4,12},{12,4},... | collective-permute-start | bytes 786440 | tf_op jit(solution)/shard_map/ppermute | solution.py:31
  145.6 4.1 %copy-start.2 = (s32[1024,1024]{1,0:T(8,128)S(1)}, s32[1024,1024]{1,0:T(8,128)}, u32[]{:S(2)}) copy-start(s32[1024,1024]{1,0:T(8,128)} %param.12) | copy-start | bytes 12582916
  151.6 2.7 %copy-start.4 = (bf16[128,1024]{1,0:T(8,128)(2,1)}, bf16[128,1024]{1,0:T(8,128)(2,1)S(1)}, u32[]{:S(2)}) copy-start(bf16[128,1024]{1,0:T(8,128)(2,1)S(1)} %collective-permute-done.8) | copy-start | bytes 786436
  152.5 1.8 %copy-start.5 = (bf16[128,1024]{1,0:T(8,128)(2,1)}, bf16[128,1024]{1,0:T(8,128)(2,1)S(1)}, u32[]{:S(2)}) copy-start(bf16[128,1024]{1,0:T(8,128)(2,1)S(1)} %collective-permute-done.6) | copy-start | bytes 786436
  153.4 1.6 copy-start.6
  157.0 19.2 %all-to-all-start.6 = ((f32[256,1,128]{2,1,0:T(1,128)}), f32[256,1,128]{2,1,0:T(1,128)S(1)}, u32[]{:S(2)}, u32[]{:S(2)}) async-start(f32[256,1,128]{2,1,0:T(1,128)} %broadcast_in_dim.20), calls=%async_computation.6 | async-start | bytes 262144 | tf_op jit(solution)/shard_map/all_to_all | solution.py:23

commit v4 on v3

v4 whole, which is shorter than its diff:
```python
import functools
import math

import jax
import jax.numpy as jnp
from jax import lax
from jax.experimental import pallas as pl
from jax.experimental.pallas import tpu as pltpu
from jax.sharding import Mesh
from jax.sharding import PartitionSpec as P

HEAD_DIM = 128
BF16 = jnp.bfloat16
F32 = jnp.float32
ROWS = ("y", "zh", "c")
TM = ("x", "zl")
PLANE = ("y", "x")
ALL = ("y", "zh", "c", "x", "zl")


def normed(values, gain_vec):
    return values * lax.rsqrt(jnp.mean(values * values, -1, keepdims=True) + 1e-05) * gain_vec


def exchange(blocks, axes):
    return lax.all_to_all(blocks, axes, 0, 0, tiled=True)


def to_all(block, axes):
    return exchange(jnp.broadcast_to(block[None], (lax.axis_size(axes),) + block.shape), axes)


def other_core(block):
    return lax.ppermute(block, "c", [(0, 1), (1, 0)])


def whole(array):
    return pl.BlockSpec(array.shape, lambda *_: (0,) * array.ndim)


def in_hbm(array):
    return pltpu.with_memory_space_constraint(array, pltpu.HBM)


def params(semantics):
    return pltpu.CompilerParams(
        dimension_semantics=semantics, vmem_limit_bytes=40 * 1024 * 1024
    )


def matmul(left, right):
    return jnp.dot(left, right, preferred_element_type=F32)


def matmul_nt(left, right):
    return lax.dot_general(left, right, (((1,), (1,)), ((), ())), preferred_element_type=F32)


def readin_kernel(at_ref, spikes_ref, held_ref, weight_ref, out_ref, counts_ref):
    block = spikes_ref[...]
    masked = (block * held_ref[...]).astype(F32).astype(BF16)
    out_ref[...] = matmul(masked, weight_ref[...]).astype(out_ref.dtype)
    counted = jnp.sum(block.astype(F32), 0, keepdims=True)

    @pl.when(pl.program_id(0) == 0)
    def _():
        counts_ref[...] = counted

    @pl.when(pl.program_id(0) > 0)
    def _():
        counts_ref[...] += counted


def readin(spikes, held, weight, which_half, dtype):
    frames, neurons = spikes.shape
    dim = weight.shape[1]
    rows = frames // 4
    return pl.pallas_call(
        readin_kernel,
        out_shape=(
            jax.ShapeDtypeStruct((frames // 2, dim), dtype),
            jax.ShapeDtypeStruct((1, neurons), F32),
        ),
        grid_spec=pltpu.PrefetchScalarGridSpec(
            num_scalar_prefetch=1,
            grid=(2,),
            in_specs=[
                pl.BlockSpec((rows, neurons), lambda i, at: (2 * at[0] + i, 0)),
                pl.BlockSpec((1, neurons), lambda i, at: (0, 0)),
                pl.BlockSpec((neurons, dim), lambda i, at: (0, 0)),
            ],
            out_specs=[
                pl.BlockSpec((rows, dim), lambda i, at: (i, 0)),
                pl.BlockSpec((1, neurons), lambda i, at: (0, 0)),
            ],
        ),
        compiler_params=params(("arbitrary",)),
        cost_estimate=pl.CostEstimate(
            flops=frames * neurons * dim,
            bytes_accessed=2 * frames * neurons + 2 * neurons * dim + frames * dim,
            transcendentals=0,
        ),
        name="readin",
    )(which_half.reshape(1), in_hbm(spikes), held, in_hbm(weight))


def attend(queries, frames_ref, weight_ref):
    frames = frames_ref[...]
    keys = matmul(frames, weight_ref[1]).astype(BF16)
    values = matmul(frames, weight_ref[2]).astype(BF16)
    weights = jnp.exp(matmul_nt(queries, keys) * (1.0 / math.sqrt(HEAD_DIM)))
    return matmul(weights.astype(BF16), values), jnp.sum(weights, -1, keepdims=True)


def attend_near_kernel(at_ref, frames_ref, weight_ref, queries_ref, num_ref, den_ref):
    rows = queries_ref.shape[0]
    own = frames_ref[pl.ds(pl.multiple_of(at_ref[0] * rows, rows), rows), :]
    queries = matmul(own, weight_ref[0]).astype(BF16)
    queries_ref[...] = queries
    numerator, denominator = attend(queries, frames_ref, weight_ref)
    num_ref[...] = numerator
    den_ref[...] = jnp.broadcast_to(denominator, den_ref.shape)


def attend_near(frames, weight, block_at, rows):
    smem = pl.BlockSpec(memory_space=pltpu.SMEM)
    shape = (rows, HEAD_DIM)
    return pl.pallas_call(
        attend_near_kernel,
        out_shape=(
            jax.ShapeDtypeStruct(shape, BF16),
            jax.ShapeDtypeStruct(shape, F32),
            jax.ShapeDtypeStruct(shape, F32),
        ),
        in_specs=[smem, whole(frames), whole(weight)],
        out_specs=[pl.BlockSpec(shape, lambda: (0, 0))] * 3,
        compiler_params=params(None),
        cost_estimate=pl.CostEstimate(
            flops=4 * frames.shape[0] * frames.shape[1] * HEAD_DIM,
            bytes_accessed=2 * frames.size,
            transcendentals=rows * frames.shape[0],
        ),
        name="attend_near",
    )(block_at.reshape(1), frames, weight)


def attend_far_kernel(
    holder_ref, frames_ref, weight_ref, queries_ref, num_ref, den_ref, mix_ref, stream_ref, out_ref
):
    numerator, denominator = attend(queries_ref[...], frames_ref, weight_ref)
    heads_out = ((num_ref[...] + numerator) / (den_ref[...] + denominator)).astype(BF16)
    held = jnp.where(holder_ref[0] == 1, stream_ref[...], jnp.zeros_like(stream_ref))
    part = (matmul(heads_out, mix_ref[...]) + held).astype(BF16)
    for i in range(out_ref.shape[0]):
        out_ref[i] = part


def attend_far(holder, frames, weight, queries, numerator, denominator, mix, stream, copies):
    smem = pl.BlockSpec(memory_space=pltpu.SMEM)
    shape = (copies,) + stream.shape
    operands = (frames, weight, queries, numerator, denominator, mix, stream)
    return pl.pallas_call(
        attend_far_kernel,
        out_shape=jax.ShapeDtypeStruct(shape, BF16),
        in_specs=[smem] + [whole(array) for array in operands],
        out_specs=pl.BlockSpec(shape, lambda: (0, 0, 0)),
        compiler_params=params(None),
        cost_estimate=pl.CostEstimate(
            flops=4 * frames.shape[0] * frames.shape[1] * HEAD_DIM,
            bytes_accessed=2 * frames.size,
            transcendentals=stream.shape[0] * frames.shape[0],
        ),
        name="attend_far",
    )(holder.reshape(1), *operands)


def score_kernel(frames, near_ref, far_ref, held_ref, seen_ref, seen_too_ref, bits_ref, sums_ref):
    heldout = (1 - held_ref[...]).astype(F32)
    count = seen_ref[...] + seen_too_ref[...]
    null_ll = count * jnp.log((count + 1.0) / frames) - (count + 1.0)
    gained = heldout * (near_ref[...] + far_ref[...] - null_ll)
    bits_ref[...] = gained / (math.log(2.0) * (count + 1.0))
    lane = lax.broadcasted_iota(jnp.int32, (1, 128), 1)
    gain_sum = jnp.sum(gained, 1, keepdims=True)
    spike_sum = jnp.sum(heldout * count, 1, keepdims=True)
    here = jnp.where(lane == 0, gain_sum, jnp.where(lane == 1, spike_sum, 0.0))
    sums_ref[...] = jnp.broadcast_to(here[None], sums_ref.shape)


def score(frames, copies, *rows):
    shape = (copies, 1, 128)
    return pl.pallas_call(
        functools.partial(score_kernel, float(frames)),
        out_shape=(
            jax.ShapeDtypeStruct(rows[0].shape, F32),
            jax.ShapeDtypeStruct(shape, F32),
        ),
        in_specs=[whole(row) for row in rows],
        out_specs=[whole(rows[0]), pl.BlockSpec(shape, lambda: (0, 0, 0))],
        name="score",
    )(*rows)


def on_device(
    spikes,
    held_in,
    readin_weight,
    qkv_weight,
    out_weight,
    up_weight,
    down_weight,
    norm_gain,
    mlp_gain,
    final_gain,
    readout_weight,
    readout_bias,
):
    frames_all = spikes.shape[0]
    model_dim = readin_weight.shape[1]
    half = frames_all // 2
    rows_here = frames_all // lax.axis_size(ROWS)
    chunk = half // lax.axis_size("y")
    core = lax.axis_index("c")
    y_at = lax.axis_index("y")
    held_row = held_in[None, :]

    given, counts_far = readin(spikes, held_row, readin_weight, 1 - core, BF16)
    theirs = other_core(given)
    own, counts_near = readin(spikes, held_row, readin_weight, core, F32)
    chip_sum = (own + theirs.astype(F32)).astype(BF16)
    plane_sum = jnp.sum(exchange(chip_sum.reshape(16, -1, model_dim), PLANE).astype(F32), 0)
    stream = jnp.sum(to_all(plane_sum.astype(BF16), ("zh", "zl")).astype(F32), 0)

    attn_own = normed(stream, norm_gain).astype(BF16)
    attn_near = to_all(attn_own, PLANE).reshape(half, model_dim)
    attn_far = other_core(attn_near)
    qkv = jnp.swapaxes(qkv_weight, 0, 1)
    own_block = y_at * lax.axis_size("zh") + lax.axis_index("zh")
    queries, numerator, denominator = attend_near(attn_near, qkv, own_block, rows_here)
    holder = (lax.axis_index("x") == lax.axis_index("zh")) & (lax.axis_index("zl") == 0)
    parts = attend_far(
        holder.astype(jnp.int32), attn_far, qkv, queries, numerator, denominator,
        out_weight, stream, lax.axis_size(TM),
    )
    mixed_state = jnp.sum(exchange(parts, TM).astype(F32), 0)

    mlp_in = normed(mixed_state, mlp_gain).astype(BF16)
    hidden_act = jax.nn.gelu(jnp.dot(mlp_in, up_weight, preferred_element_type=F32)).astype(BF16)
    mlp_part = jnp.dot(hidden_act, down_weight, preferred_element_type=F32)
    final_state = mixed_state + jnp.sum(to_all(mlp_part.astype(BF16), TM).astype(F32), 0)
    own_latents = normed(final_state, final_gain).astype(BF16)

    mine = to_all(own_latents, "zh").reshape(chunk, model_dim)
    lat_near = to_all(mine, "y").reshape(half, model_dim)
    lat_far = other_core(lat_near)

    def likelihood(lat, start):
        log_rate = matmul_nt(lat, readout_weight) + readout_bias[None, :]
        observed = lax.dynamic_slice_in_dim(spikes, start, half, 0).astype(F32)
        return jnp.sum(observed * log_rate - jnp.exp(log_rate), 0, keepdims=True)

    bits, sums = score(
        frames_all, lax.axis_size(ALL),
        likelihood(lat_near, core * half), likelihood(lat_far, (1 - core) * half),
        held_row, counts_near, counts_far,
    )
    totals = jnp.sum(exchange(sums, ALL), (0, 1))
    bits_total = totals[0] / (math.log(2.0) * (1.0 + totals[1]))

    out_start = lax.axis_index(ROWS) * rows_here
    out_row = lax.rem(out_start, half)
    latents = jnp.where(
        out_start // half == core,
        lax.dynamic_slice_in_dim(lat_near, out_row, rows_here, 0),
        lax.dynamic_slice_in_dim(lat_far, out_row, rows_here, 0),
    )
    return (latents, bits[0], bits_total)


def solution(mesh):
    fine = Mesh(mesh.devices.reshape(4, 4, 2, 4, 2), ALL)
    in_specs = (
        P(None, ALL),
        P(ALL),
        P(ALL, None),
        P(None, None, TM),
        P(TM, None),
        P(None, TM),
        P(TM, None),
        P(),
        P(),
        P(),
        P(ALL, None),
        P(ALL),
    )
    out_specs = (P(ROWS, None), P(ALL), P())
    return jax.shard_map(
        on_device, mesh=fine, in_specs=in_specs, out_specs=out_specs, check_vma=False
    )
```

time: 180 us -> 171 us (0.950)
  matrix products: 29 us -> 9.03 us
  blocking collectives: 98 us -> 111 us
  Pallas kernels: 0 us -> 11.8 us
  starting transfers between devices: 26.7 us -> 17.5 us
  other arithmetic: 8.14 us -> 3.16 us
    dot_general x16 -> x2, matrix products: 27.2 us -> 7.22 us  [matmul_nt(): lax.dot_general(left, right, (((1,), (1,)), ((), ())), preferred_element_...]
    all_to_all x6 -> x7, blocking collectives: 98 us -> 111 us  [exchange(): return lax.all_to_all(blocks, axes, 0, 0, tiled=True)]
    pallas_call x0 -> x5, Pallas kernels: none -> 11.8 us  [the longest x2 6.83 us: readin(): pl.pallas_call(readin_kernel, out_shape=(jax.ShapeDtypeStruct((frames //...]
    ppermute x6 -> x3, starting transfers between devices: 18.6 us -> 12.1 us  [other_core(): return lax.ppermute(block, 'c', [(0, 1), (1, 0)])]
    reduce_sum x4 -> x2, other arithmetic: 3.21 us -> 0.36 us  [the longest x1 0.29 us: on_device(): totals = jnp.sum(exchange(sums, ALL), (0, 1))]
    ppermute x3 -> x0, starting transfers between devices: 1.87 us -> none  [on_device(): lax.ppermute(first, 'y', [(i, (i + k) % 4) for i in range(4)])]
  transfers between devices with their start and end apart: 10 -> 4, of which waited for: 1 -> 2; matrix products, arithmetic and copies ran while one was open for 12% -> 3% of each run, Pallas kernels for 0% -> 3%
where the time goes in v4:
time: 171 us
  blocking collectives  111 us (65%)
  starting transfers between devices  17.5 us (10%)
  Pallas kernels  11.8 us (7%)
  waiting for transfers between devices  11.8 us (7%)
  matrix products  9.03 us (5%)
  between operations  3.36 us (2%)
  other arithmetic  3.16 us (2%)
  local copies, waits for them, and re-layouts  3.14 us (2%)
    all_to_all x7, blocking collectives, exchange(): return lax.all_to_all(blocks, axes, 0, 0, tiled=True)  111 us
    ppermute x3, starting transfers between devices, other_core(): return lax.ppermute(block, 'c', [(0, 1), (1, 0)])  12.1 us
    all_to_all x1, waiting for transfers between devices, exchange(): return lax.all_to_all(blocks, axes, 0, 0, tiled=True)  11.5 us
    dot_general x2, matrix products, matmul_nt(): lax.dot_general(left, right, (((1,), (1,)), ((), ())), preferred_element_...  7.22 us
    pallas_call x2, Pallas kernels, readin(): pl.pallas_call(readin_kernel, out_shape=(jax.ShapeDtypeStruct((frames //...  6.83 us
    all_to_all x1, starting transfers between devices, exchange(): return lax.all_to_all(blocks, axes, 0, 0, tiled=True)  5.4 us
  transfers between devices with their start and end apart: 4, of which 2 were waited for; matrix products, arithmetic and copies ran while one was open for 3% of the time, Pallas kernels for 3%

profile of v4, /device:TPU:1, one launch (start us, length us, event | category | flops | bytes accessed | tf_op | source)
XLA Modules:
  0.0 170.5 jit_solution(3469894907236028222)
XLA Ops:
  0.6 0.0 copy-start
  0.7 0.0 copy-start.4
  0.7 0.8 copy-done.4
  1.5 3.4 %readin.3 = (bf16[512,1024]{1,0:T(8,128)(2,1)S(1)}, f32[1,1024]{1,0:T(1,128)S(1)}) custom-call(s32[1]{0:T(128)} %bitcast.3.at_ref, s32[1024,1024]{1,0:T(8,128)} %spikes_ref.3, s32[1,1024]{1,0:T(1,128)S(1)} %bitcast.25, bf16[1024,1024]{1,0:T(8,128)(2,1)} %weight_ref.3), custom_call_target="tpu_custom_call" | custom-call | flops 1073741824 | bytes 5242880 | tf_op jit(solution)/shard_map/readin/pallas_call | solution.py:78
  4.9 3.3 %collective-permute-start = (bf16[512,1024]{1,0:T(8,128)(2,1)S(1)}, bf16[512,1024]{1,0:T(8,128)(2,1)S(1)}, u32[]{:S(2)}, u32[]{:S(2)}) collective-permute-start(bf16[512,1024]{1,0:T(8,128)(2,1)S(1)} %get-tuple-element.13), channel_id=1, source_target_pairs={{0,8},{8,0},{1,9},{9,1},{2,10},{10,2},{3,11},{11,3},{4,12},{12,4},... | collective-permute-start | bytes 3145736 | tf_op jit(solution)/shard_map/ppermute | solution.py:34
  8.3 3.4 %readin.2 = (f32[512,1024]{1,0:T(8,128)S(1)}, f32[1,1024]{1,0:T(1,128)S(1)}) custom-call(s32[1]{0:T(128)} %bitcast.1.at_ref, s32[1024,1024]{1,0:T(8,128)} %spikes_ref.3, s32[1,1024]{1,0:T(1,128)S(1)} %bitcast.26, bf16[1024,1024]{1,0:T(8,128)(2,1)} %weight_ref.3), custom_call_target="tpu_custom_call" | custom-call | flops 1073741824 | bytes 5242880 | tf_op jit(solution)/shard_map/readin/pallas_call | solution.py:78
  11.7 0.0 collective-permute-done
  11.7 0.4 add_convert_fusion
  12.1 0.2 copy-done.7
  12.3 21.5 %all_to_all.40 = bf16[16,32,1024]{2,1,0:T(8,128)(2,1)S(1)} all-to-all(bf16[16,32,1024]{2,1,0:T(8,128)(2,1)S(1)} %bitcast.27), channel_id=1, replica_groups=mesh['y'=4,'zh'=4,'c'=2,'x'=4,'zl'=2] {'y','x'}, dimensions={0} | all-to-all | bytes 2097152 | tf_op jit(solution)/shard_map/all_to_all | solution.py:26
  33.8 0.2 reduce_sum.93
  34.0 0.1 broadcast_in_dim.19
  34.0 23.0 %all_to_all.41 = bf16[8,32,1024]{2,1,0:T(8,128)(2,1)S(1)} all-to-all(bf16[8,32,1024]{2,1,0:T(8,128)(2,1)S(1)} %broadcast_in_dim.19), channel_id=1, replica_groups=mesh['y'=4,'zh'=4,'c'=2,'x'=4,'zl'=2] {'zh','zl'}, dimensions={0} | all-to-all | bytes 1048576 | tf_op jit(solution)/shard_map/all_to_all | solution.py:26
  57.0 0.1 convert_reduce_fusion.2.stream_ref
  57.1 0.1 multiply_reduce_fusion.2
  57.2 0.1 multiply_convert_fusion.2
  57.3 0.1 broadcast_in_dim.20
  57.4 0.0 copy-start.3
  57.4 18.4 %all_to_all.42 = bf16[16,32,1024]{2,1,0:T(8,128)(2,1)S(1)} all-to-all(bf16[16,32,1024]{2,1,0:T(8,128)(2,1)S(1)} %broadcast_in_dim.20), channel_id=1, replica_groups=mesh['y'=4,'zh'=4,'c'=2,'x'=4,'zl'=2] {'y','x'}, dimensions={0} | all-to-all | bytes 2097152 | tf_op jit(solution)/shard_map/all_to_all | solution.py:26
  75.9 4.0 %collective-permute-start.1 = (bf16[512,1024]{1,0:T(8,128)(2,1)S(1)}, bf16[512,1024]{1,0:T(8,128)(2,1)}, u32[]{:S(2)}, u32[]{:S(2)}) collective-permute-start(bf16[512,1024]{1,0:T(8,128)(2,1)S(1)} %bitcast.20), channel_id=1, source_target_pairs={{0,8},{8,0},{1,9},{9,1},{2,10},{10,2},{3,11},{11,3},{4,12},{12,4},... | collective-permute-start | bytes 3145736 | tf_op jit(solution)/shard_map/ppermute | solution.py:34
  79.8 1.1 copy-done.1
  80.9 1.0 attend_near.1
  82.0 0.3 collective-permute-done.1.frames_ref
  82.2 2.4 %attend_far.1 = bf16[8,32,1024]{2,1,0:T(8,128)(2,1)S(1)} custom-call(s32[1]{0:T(128)} %bitcast.holder_ref, bf16[512,1024]{1,0:T(8,128)(2,1)} %collective-permute-done.1.frames_ref, bf16[3,1024,128]{2,1,0:T(8,128)(2,1)S(1)} %bitcast.23, bf16[32,128]{1,0:T(8,128)(2,1)S(1)} %get-tuple-element.14.queries_ref, f32[32,128]{1,0:T(8,128)S(1)} %get-tuple-element.15.num_ref, ...), custom_call_target="tpu_custom_call" | custom-call | flops 268435456 | bytes 1048576 | tf_op jit(solution)/shard_map/attend_far/pallas_call | solution.py:162
  84.7 12.2 %all_to_all.43 = bf16[8,32,1024]{2,1,0:T(8,128)(2,1)S(1)} all-to-all(bf16[8,32,1024]{2,1,0:T(8,128)(2,1)S(1)} %attend_far.1), channel_id=1, replica_groups=mesh['y'=4,'zh'=4,'c'=2,'x'=4,'zl'=2] {'x','zl'}, dimensions={0} | all-to-all | bytes 1048576 | tf_op jit(solution)/shard_map/all_to_all | solution.py:26
  96.9 0.1 convert_reduce_fusion.1
  97.0 0.1 multiply_reduce_fusion.1
  97.1 0.0 copy-start.12
  97.2 1.8 %convolution_convert_fusion = bf16[32,1024]{1,0:T(8,128)(2,1)S(1)} fusion(bf16[512,1024]{1,0:T(8,128)(2,1)S(1)} %copy-done.9, bf16[1024,512]{1,0:T(8,128)(2,1)} %param.17, f32[32,1024]{1,0:T(8,128)S(1)} %convert_reduce_fusion.1, f32[1024]{0:T(1024)S(1)} %copy-done.10, f32[32]{0:T(128)S(1)} %add_rsqrt_fusion.1), kind=kOutput, calls=%fused_computation.3 | convolution fusion | flops 67387392 | bytes 2297984 | tf_op jit(solution)/shard_map/dot_general | solution.py:249
  99.0 0.1 broadcast_in_dim.21
  99.0 11.2 %all_to_all.44 = bf16[8,32,1024]{2,1,0:T(8,128)(2,1)S(1)} all-to-all(bf16[8,32,1024]{2,1,0:T(8,128)(2,1)S(1)} %broadcast_in_dim.21), channel_id=1, replica_groups=mesh['y'=4,'zh'=4,'c'=2,'x'=4,'zl'=2] {'x','zl'}, dimensions={0} | all-to-all | bytes 1048576 | tf_op jit(solution)/shard_map/all_to_all | solution.py:26
  110.3 0.1 convert_reduce_fusion
  110.3 0.1 multiply_reduce_fusion
  110.5 0.1 multiply_convert_fusion
  110.6 0.0 copy-start.13
  110.6 10.8 %all_to_all.45 = bf16[4,32,1024]{2,1,0:T(8,128)(2,1)S(1)} all-to-all(bf16[4,32,1024]{2,1,0:T(8,128)(2,1)S(1)} %broadcast_in_dim.22), channel_id=1, replica_groups=mesh['y'=4,'zh'=4,'c'=2,'x'=4,'zl'=2] {'zh'}, dimensions={0} | all-to-all | bytes 524288 | tf_op jit(solution)/shard_map/all_to_all | solution.py:26
  121.4 0.1 broadcast_in_dim.24
  121.5 13.6 %all_to_all.46 = bf16[4,128,1024]{2,1,0:T(8,128)(2,1)S(1)} all-to-all(bf16[4,128,1024]{2,1,0:T(8,128)(2,1)S(1)} %broadcast_in_dim.24), channel_id=1, replica_groups=mesh['y'=4,'zh'=4,'c'=2,'x'=4,'zl'=2] {'y'}, dimensions={0} | all-to-all | bytes 2097152 | tf_op jit(solution)/shard_map/all_to_all | solution.py:26
  135.1 4.8 %collective-permute-start.2 = (bf16[512,1024]{1,0:T(8,128)(2,1)S(1)}, bf16[512,1024]{1,0:T(8,128)(2,1)}, u32[]{:S(2)}, u32[]{:S(2)}) collective-permute-start(bf16[512,1024]{1,0:T(8,128)(2,1)S(1)} %bitcast.28), channel_id=1, source_target_pairs={{0,8},{8,0},{1,9},{9,1},{2,10},{10,2},{3,11},{11,3},{4,12},{12,4},... | collective-permute-start | bytes 3145736 | tf_op jit(solution)/shard_map/ppermute | solution.py:34
  140.0 3.9 %subtract_reduce_fusion.1 = f32[1024]{0:T(1024)} fusion(s32[1024,1024]{1,0:T(8,128)} %spikes_ref.3, s32[]{:T(128)S(6)} %select_n.27, bf16[512,1024]{1,0:T(8,128)(2,1)S(1)} %bitcast.29, bf16[1024,1024]{1,0:T(8,128)(2,1)S(1)} %copy-done, f32[1024]{0:T(1024)S(1)} %copy-done.13), kind=kOutput, calls=%fused_computation.1 | convolution fusion | flops 1076362240 | bytes 5251076 | tf_op jit(solution)/shard_map/dot_general | solution.py:56
  143.9 0.0 collective-permute-done.2
  143.9 3.4 %subtract_reduce_fusion = f32[1024]{0:T(1024)} fusion(s32[1024,1024]{1,0:T(8,128)S(1)} %copy-done.8, s32[]{:T(128)S(6)} %select_n.28, bf16[512,1024]{1,0:T(8,128)(2,1)} %collective-permute-done.2, bf16[1024,1024]{1,0:T(8,128)(2,1)S(1)} %copy-done, f32[1024]{0:T(1024)S(1)} %copy-done.13), kind=kOutput, calls=%fused_computation | convolution fusion | flops 1076362240 | bytes 5251076 | tf_op jit(solution)/shard_map/dot_general | solution.py:56
  147.2 1.5 score.1
  148.7 5.4 %all-to-all-start.7 = ((f32[256,1,128]{2,1,0:T(1,128)}), f32[256,1,128]{2,1,0:T(1,128)S(1)}, u32[]{:S(2)}, u32[]{:S(2)}) async-start(f32[256,1,128]{2,1,0:T(1,128)} %get-tuple-element.20), calls=%async_computation.7 | async-start | bytes 262144 | tf_op jit(solution)/shard_map/all_to_all | solution.py:26
  154.2 1.5 dynamic-slice_select_fusion
  155.7 11.5 %all-to-all-done.7 = f32[256,1,128]{2,1,0:T(1,128)S(1)} async-done(((f32[256,1,128]{2,1,0:T(1,128)}), f32[256,1,128]{2,1,0:T(1,128)S(1)}, u32[]{:S(2)}, u32[]{:S(2)}) %all-to-all-start.7) | async-done | bytes 131104 | tf_op jit(solution)/shard_map/all_to_all | solution.py:26
  167.2 0.3 reduce_sum.102
  167.4 0.6 fusion.21
  (24 shorter events, 0.1 us)
Async XLA Ops:
  0.6 139.4 %copy-start = (bf16[1024,1024]{1,0:T(8,128)(2,1)S(1)}, bf16[1024,1024]{1,0:T(8,128)(2,1)}, u32[]{:S(2)}) copy-start(bf16[1024,1024]{1,0:T(8,128)(2,1)} %param.22) | copy-start | bytes 6291460
  0.7 0.8 copy-start.4
  1.5 6.8 %copy-start.5 = (s32[1024]{0:T(1024)S(1)}, s32[1024]{0:T(1024)}, u32[]{:S(2)}) copy-start(s32[1024]{0:T(1024)} %param.13) | copy-start | bytes 12292
  4.9 6.8 %copy-start.6 = (f32[1,1024]{1,0:T(1,128)}, f32[1,1024]{1,0:T(1,128)S(1)}, u32[]{:S(2)}) copy-start(f32[1,1024]{1,0:T(1,128)S(1)} %get-tuple-element.18.seen_too_ref) | copy-start | bytes 12292
  4.9 6.8 %collective-permute-start = (bf16[512,1024]{1,0:T(8,128)(2,1)S(1)}, bf16[512,1024]{1,0:T(8,128)(2,1)S(1)}, u32[]{:S(2)}, u32[]{:S(2)}) collective-permute-start(bf16[512,1024]{1,0:T(8,128)(2,1)S(1)} %get-tuple-element.13), channel_id=1, source_target_pairs={{0,8},{8,0},{1,9},{9,1},{2,10},{10,2},{3,11},{11,3},{4,12},{12,4},... | collective-permute-start | bytes 3145736 | tf_op jit(solution)/shard_map/ppermute | solution.py:34
  11.7 0.6 copy-start.7
  33.8 23.4 %copy-start.11 = (f32[1024]{0:T(1024)S(1)}, f32[1024]{0:T(1024)}, u32[]{:S(2)}) copy-start(f32[1024]{0:T(1024)} %param.19) | copy-start | bytes 12292
  57.4 24.8 %copy-start.3 = (bf16[128,1024]{1,0:T(8,128)(2,1)S(1)}, bf16[128,1024]{1,0:T(8,128)(2,1)}, u32[]{:S(2)}) copy-start(bf16[128,1024]{1,0:T(8,128)(2,1)} %mix_ref.1) | copy-start | bytes 786436
  75.9 6.4 %collective-permute-start.1 = (bf16[512,1024]{1,0:T(8,128)(2,1)S(1)}, bf16[512,1024]{1,0:T(8,128)(2,1)}, u32[]{:S(2)}, u32[]{:S(2)}) collective-permute-start(bf16[512,1024]{1,0:T(8,128)(2,1)S(1)} %bitcast.20), channel_id=1, source_target_pairs={{0,8},{8,0},{1,9},{9,1},{2,10},{10,2},{3,11},{11,3},{4,12},{12,4},... | collective-permute-start | bytes 3145736 | tf_op jit(solution)/shard_map/ppermute | solution.py:34
  79.8 1.1 copy-start.1
  80.9 1.3 copy-start.2
  82.2 14.9 %copy-start.9 = (bf16[512,1024]{1,0:T(8,128)(2,1)S(1)}, bf16[512,1024]{1,0:T(8,128)(2,1)}, u32[]{:S(2)}) copy-start(bf16[512,1024]{1,0:T(8,128)(2,1)} %param.18) | copy-start | bytes 3145732
  82.2 14.9 %copy-start.10 = (f32[1024]{0:T(1024)S(1)}, f32[1024]{0:T(1024)}, u32[]{:S(2)}) copy-start(f32[1024]{0:T(1024)} %param.20) | copy-start | bytes 12292
  97.1 13.3 %copy-start.12 = (f32[1024]{0:T(1024)S(1)}, f32[1024]{0:T(1024)}, u32[]{:S(2)}) copy-start(f32[1024]{0:T(1024)} %param.21) | copy-start | bytes 12292
  110.6 29.4 %copy-start.13 = (f32[1024]{0:T(1024)S(1)}, f32[1024]{0:T(1024)}, u32[]{:S(2)}) copy-start(f32[1024]{0:T(1024)} %param.23) | copy-start | bytes 12292
  135.1 8.7 %collective-permute-start.2 = (bf16[512,1024]{1,0:T(8,128)(2,1)S(1)}, bf16[512,1024]{1,0:T(8,128)(2,1)}, u32[]{:S(2)}, u32[]{:S(2)}) collective-permute-start(bf16[512,1024]{1,0:T(8,128)(2,1)S(1)} %bitcast.28), channel_id=1, source_target_pairs={{0,8},{8,0},{1,9},{9,1},{2,10},{10,2},{3,11},{11,3},{4,12},{12,4},... | collective-permute-start | bytes 3145736 | tf_op jit(solution)/shard_map/ppermute | solution.py:34
  140.0 3.9 %copy-start.8 = (s32[1024,1024]{1,0:T(8,128)S(1)}, s32[1024,1024]{1,0:T(8,128)}, u32[]{:S(2)}) copy-start(s32[1024,1024]{1,0:T(8,128)} %spikes_ref.3) | copy-start | bytes 12582916
  148.7 18.4 %all-to-all-start.7 = ((f32[256,1,128]{2,1,0:T(1,128)}), f32[256,1,128]{2,1,0:T(1,128)S(1)}, u32[]{:S(2)}, u32[]{:S(2)}) async-start(f32[256,1,128]{2,1,0:T(1,128)} %get-tuple-element.20), calls=%async_computation.7 | async-start | bytes 262144 | tf_op jit(solution)/shard_map/all_to_all | solution.py:26

commit v5 on v4

v5 whole, which is shorter than its diff:
```python
import functools
import math

import jax
import jax.numpy as jnp
from jax import lax
from jax.experimental import pallas as pl
from jax.experimental.pallas import tpu as pltpu
from jax.sharding import Mesh
from jax.sharding import PartitionSpec as P

HEAD_DIM = 128
BF16 = jnp.bfloat16
F32 = jnp.float32
ROWS = ("y", "zh", "c")
TM = ("x", "zl")
PLANE = ("y", "x")
YZ = ("y", "zh")
ALL = ("y", "zh", "c", "x", "zl")


def normed(values, gain_vec):
    return values * lax.rsqrt(jnp.mean(values * values, -1, keepdims=True) + 1e-05) * gain_vec


def exchange(blocks, axes):
    return lax.all_to_all(blocks, axes, 0, 0, tiled=True)


def to_all(block, axes):
    return exchange(jnp.broadcast_to(block[None], (lax.axis_size(axes),) + block.shape), axes)


def other_core(block):
    return lax.ppermute(block, "c", [(0, 1), (1, 0)])


def other_layer(block):
    return lax.ppermute(block, "zl", [(0, 1), (1, 0)])


def whole(array):
    return pl.BlockSpec(array.shape, lambda *_: (0,) * array.ndim)


def in_hbm(array):
    return pltpu.with_memory_space_constraint(array, pltpu.HBM)


def params(semantics):
    return pltpu.CompilerParams(
        dimension_semantics=semantics, vmem_limit_bytes=40 * 1024 * 1024
    )


def matmul(left, right):
    return jnp.dot(left, right, preferred_element_type=F32)


def matmul_nt(left, right):
    return lax.dot_general(left, right, (((1,), (1,)), ((), ())), preferred_element_type=F32)


def readin_kernel(at_ref, spikes_ref, held_ref, weight_ref, out_ref, counts_ref, total):
    step = pl.program_id(0)
    block = spikes_ref[...]
    masked = (block * held_ref[...]).astype(F32).astype(BF16)
    product = matmul(masked, weight_ref[...])
    counts_ref[...] = jnp.sum(block.astype(F32), 0, keepdims=True)

    @pl.when(step == 0)
    def _():
        total[...] = product

    @pl.when(step > 0)
    def _():
        total[...] += product

    @pl.when(step == pl.num_programs(0) - 1)
    def _():
        out_ref[...] = total[...].astype(out_ref.dtype)


def readin(spikes, held, weight, which_half, dtype):
    frames, neurons = spikes.shape
    dim = weight.shape[1]
    rows, width = frames // 2, neurons // 4
    return pl.pallas_call(
        readin_kernel,
        out_shape=(
            jax.ShapeDtypeStruct((rows, dim), dtype),
            jax.ShapeDtypeStruct((1, neurons), F32),
        ),
        grid_spec=pltpu.PrefetchScalarGridSpec(
            num_scalar_prefetch=1,
            grid=(4,),
            in_specs=[
                pl.BlockSpec((rows, width), lambda k, at: (at[0], k)),
                pl.BlockSpec((1, width), lambda k, at: (0, k)),
                pl.BlockSpec((width, dim), lambda k, at: (k, 0)),
            ],
            out_specs=[
                pl.BlockSpec((rows, dim), lambda k, at: (0, 0)),
                pl.BlockSpec((1, width), lambda k, at: (0, k)),
            ],
            scratch_shapes=[pltpu.VMEM((rows, dim), F32)],
        ),
        compiler_params=params(("arbitrary",)),
        cost_estimate=pl.CostEstimate(
            flops=frames * neurons * dim,
            bytes_accessed=2 * frames * neurons + 2 * neurons * dim + frames * dim,
            transcendentals=0,
        ),
        name="readin",
    )(which_half.reshape(1), in_hbm(spikes), held, in_hbm(weight))


def project_kernel(parts_ref, gain_ref, weight_ref, stream_ref, queries_ref, kv_ref):
    groups = parts_ref.shape[0] // 4
    piece = parts_ref.shape[1]
    for x in range(4):
        rows = parts_ref[groups * x].astype(F32)
        for i in range(1, groups):
            rows += parts_ref[groups * x + i].astype(F32)
        stream_ref[piece * x : piece * (x + 1), :] = rows
    attn_in = normed(stream_ref[...], gain_ref[...]).astype(BF16)
    queries_ref[...] = matmul(attn_in, weight_ref[0]).astype(BF16)
    keys = matmul(attn_in, weight_ref[1]).astype(BF16)
    values = matmul(attn_in, weight_ref[2]).astype(BF16)
    for i in range(kv_ref.shape[0]):
        kv_ref[i, :, :HEAD_DIM] = keys
        kv_ref[i, :, HEAD_DIM:] = values


def project(parts, gain, weight, copies):
    rows, dim = 4 * parts.shape[1], parts.shape[2]
    shapes = ((rows, dim), F32), ((rows, HEAD_DIM), BF16), ((copies, rows, 2 * HEAD_DIM), BF16)
    return pl.pallas_call(
        project_kernel,
        out_shape=[jax.ShapeDtypeStruct(*shape) for shape in shapes],
        in_specs=[whole(array) for array in (parts, gain, weight)],
        out_specs=[
            pl.BlockSpec(shape, lambda n=len(shape): (0,) * n) for shape, _ in shapes
        ],
        compiler_params=params(None),
        name="project",
    )(parts, gain, weight)


def attend_kernel(queries_ref, near_ref, far_ref, mix_ref, out_ref):
    queries = queries_ref[...]
    numerator, denominator = 0.0, 0.0
    for kv in (near_ref, far_ref):
        scores = matmul_nt(queries, kv[:, :HEAD_DIM])
        weights = jnp.exp(scores * (1.0 / math.sqrt(HEAD_DIM)))
        numerator += matmul(weights.astype(BF16), kv[:, HEAD_DIM:])
        denominator += jnp.sum(weights, -1, keepdims=True)
    part = matmul((numerator / denominator).astype(BF16), mix_ref[...]).astype(BF16)
    for i in range(out_ref.shape[0]):
        out_ref[i] = part


def attend(queries, near, far, mix, copies):
    shape = (copies, queries.shape[0], mix.shape[1])
    operands = (queries, near, far, mix)
    return pl.pallas_call(
        attend_kernel,
        out_shape=jax.ShapeDtypeStruct(shape, BF16),
        in_specs=[whole(array) for array in operands],
        out_specs=pl.BlockSpec(shape, lambda: (0, 0, 0)),
        compiler_params=params(None),
        name="attend",
    )(*operands)


def score_kernel(frames, near_ref, far_ref, held_ref, seen_ref, seen_too_ref, bits_ref, sums_ref):
    heldout = (1 - held_ref[...]).astype(F32)
    count = seen_ref[...] + seen_too_ref[...]
    null_ll = count * jnp.log((count + 1.0) / frames) - (count + 1.0)
    gained = heldout * (near_ref[...] + far_ref[...] - null_ll)
    bits_ref[...] = gained / (math.log(2.0) * (count + 1.0))
    lane = lax.broadcasted_iota(jnp.int32, (1, 128), 1)
    gain_sum = jnp.sum(gained, 1, keepdims=True)
    spike_sum = jnp.sum(heldout * count, 1, keepdims=True)
    here = jnp.where(lane == 0, gain_sum, jnp.where(lane == 1, spike_sum, 0.0))
    sums_ref[...] = jnp.broadcast_to(here[None], sums_ref.shape)


def score(frames, copies, *rows):
    shape = (copies, 1, 128)
    return pl.pallas_call(
        functools.partial(score_kernel, float(frames)),
        out_shape=(
            jax.ShapeDtypeStruct(rows[0].shape, F32),
            jax.ShapeDtypeStruct(shape, F32),
        ),
        in_specs=[whole(row) for row in rows],
        out_specs=[whole(rows[0]), pl.BlockSpec(shape, lambda: (0, 0, 0))],
        name="score",
    )(*rows)


def on_device(
    spikes,
    held_in,
    readin_weight,
    qkv_weight,
    out_weight,
    up_weight,
    down_weight,
    norm_gain,
    mlp_gain,
    final_gain,
    readout_weight,
    readout_bias,
):
    frames_all = spikes.shape[0]
    model_dim = readin_weight.shape[1]
    half = frames_all // 2
    rows_here = frames_all // lax.axis_size(ROWS)
    core = lax.axis_index("c")
    held_row = held_in[None, :]

    given, counts_far = readin(spikes, held_row, readin_weight, 1 - core, BF16)
    theirs = other_core(given)
    own, counts_near = readin(spikes, held_row, readin_weight, core, F32)
    chip_sum = (own + theirs.astype(F32)).astype(BF16)
    plane_sum = jnp.sum(exchange(chip_sum.reshape(16, -1, model_dim), PLANE).astype(F32), 0)
    plane_sum = plane_sum.astype(BF16)
    pair_sum = (plane_sum.astype(F32) + other_layer(plane_sum).astype(F32)).astype(BF16)
    blocks = jnp.broadcast_to(pair_sum.reshape(1, 4, -1, model_dim), (4, 4, 8, model_dim))
    parts = exchange(blocks.reshape(16, 8, model_dim), ("x", "zh"))

    stream, queries, kv_own = project(
        parts, norm_gain[None, :], jnp.swapaxes(qkv_weight, 0, 1), lax.axis_size(YZ)
    )
    kv_near = exchange(kv_own, YZ).reshape(half, 2 * HEAD_DIM)
    attn_parts = attend(queries, kv_near, other_core(kv_near), out_weight, lax.axis_size(TM))
    mixed_state = stream + jnp.sum(exchange(attn_parts, TM).astype(F32), 0)

    mlp_in = normed(mixed_state, mlp_gain).astype(BF16)
    hidden_act = jax.nn.gelu(jnp.dot(mlp_in, up_weight, preferred_element_type=F32)).astype(BF16)
    mlp_part = jnp.dot(hidden_act, down_weight, preferred_element_type=F32)
    mlp_sum = jnp.sum(
        exchange(mlp_part.astype(BF16).reshape(8, -1, model_dim), TM).astype(F32), 0
    )
    rows_own = mlp_sum.shape[0]
    own_mixed = lax.dynamic_slice_in_dim(mixed_state, lax.axis_index(TM) * rows_own, rows_own, 0)
    own_latents = normed(own_mixed + mlp_sum, final_gain).astype(BF16)

    column = to_all(own_latents, ("zh", "zl")).reshape(rows_here, model_dim)
    lat_near = to_all(column, PLANE).reshape(half, model_dim)
    lat_far = other_core(lat_near)

    def likelihood(lat, start):
        log_rate = matmul_nt(lat, readout_weight) + readout_bias[None, :]
        observed = lax.dynamic_slice_in_dim(spikes, start, half, 0).astype(F32)
        return jnp.sum(observed * log_rate - jnp.exp(log_rate), 0, keepdims=True)

    bits, sums = score(
        frames_all, lax.axis_size(ALL),
        likelihood(lat_near, core * half), likelihood(lat_far, (1 - core) * half),
        held_row, counts_near, counts_far,
    )
    totals = jnp.sum(exchange(sums, ALL), (0, 1))
    bits_total = totals[0] / (math.log(2.0) * (1.0 + totals[1]))

    out_start = lax.axis_index(ROWS) * rows_here
    out_row = lax.rem(out_start, half)
    latents = jnp.where(
        out_start // half == core,
        lax.dynamic_slice_in_dim(lat_near, out_row, rows_here, 0),
        lax.dynamic_slice_in_dim(lat_far, out_row, rows_here, 0),
    )
    return (latents, bits[0], bits_total)


def solution(mesh):
    fine = Mesh(mesh.devices.reshape(4, 4, 2, 4, 2), ALL)
    in_specs = (
        P(None, ALL),
        P(ALL),
        P(ALL, None),
        P(None, None, TM),
        P(TM, None),
        P(None, TM),
        P(TM, None),
        P(),
        P(),
        P(),
        P(ALL, None),
        P(ALL),
    )
    out_specs = (P(ROWS, None), P(ALL), P())
    return jax.shard_map(
        on_device, mesh=fine, in_specs=in_specs, out_specs=out_specs, check_vma=False
    )
```

time: 171 us -> 167 us (0.977)
  blocking collectives: 111 us -> 94 us
  waiting for transfers between devices: 11.8 us -> 19.3 us
  starting transfers between devices: 17.5 us -> 22.2 us
    all_to_all x7 -> x6, blocking collectives: 111 us -> 94 us  [exchange(): return lax.all_to_all(blocks, axes, 0, 0, tiled=True)]
    all_to_all x1 -> x2, waiting for transfers between devices: 11.5 us -> 16.5 us  [exchange(): return lax.all_to_all(blocks, axes, 0, 0, tiled=True)]
    all_to_all x1 -> x2, starting transfers between devices: 5.4 us -> 8.51 us  [exchange(): return lax.all_to_all(blocks, axes, 0, 0, tiled=True)]
  transfers between devices with their start and end apart: 4 -> 6, of which waited for: 2 -> 4; matrix products, arithmetic and copies ran while one was open for 3% -> 3% of each run, Pallas kernels for 3% -> 3%
where the time goes in v5:
time: 167 us; the launch traced here: 166 us
  blocking collectives  94 us (56%)
  starting transfers between devices  22.2 us (13%)
  waiting for transfers between devices  19.3 us (12%)
  Pallas kernels  11.4 us (7%)
  matrix products  9.02 us (5%)
  other arithmetic  4.12 us (2%)
  between operations  3.26 us (2%)
  local copies, waits for them, and re-layouts  2.48 us (1%)
    all_to_all x6, blocking collectives, exchange(): return lax.all_to_all(blocks, axes, 0, 0, tiled=True)  94 us
    all_to_all x2, waiting for transfers between devices, exchange(): return lax.all_to_all(blocks, axes, 0, 0, tiled=True)  16.5 us
    ppermute x3, starting transfers between devices, other_core(): return lax.ppermute(block, 'c', [(0, 1), (1, 0)])  12 us
    pallas_call x2, Pallas kernels, readin(): pl.pallas_call(readin_kernel, out_shape=(jax.ShapeDtypeStruct((rows, dim)...  9 us
    all_to_all x2, starting transfers between devices, exchange(): return lax.all_to_all(blocks, axes, 0, 0, tiled=True)  8.51 us
    dot_general x2, matrix products, matmul_nt(): lax.dot_general(left, right, (((1,), (1,)), ((), ())), preferred_element_...  7.21 us
  transfers between devices with their start and end apart: 6, of which 4 were waited for; matrix products, arithmetic and copies ran while one was open for 3% of the time, Pallas kernels for 3%

profile of v5, /device:TPU:1, one launch (start us, length us, event | category | flops | bytes accessed | tf_op | source)
XLA Modules:
  0.0 165.8 jit_solution(12613837632818756189)
XLA Ops:
  0.6 0.0 copy-start
  0.7 0.0 copy-start.3
  0.7 0.8 copy-done.3
  1.5 4.5 %readin.3 = (bf16[512,1024]{1,0:T(8,128)(2,1)S(1)}, f32[1,1024]{1,0:T(1,128)S(1)}) custom-call(s32[1]{0:T(128)} %bitcast.2.at_ref, s32[1024,1024]{1,0:T(8,128)} %spikes_ref.3, s32[1,1024]{1,0:T(1,128)S(1)} %bitcast.25, bf16[1024,1024]{1,0:T(8,128)(2,1)} %weight_ref.3), custom_call_target="tpu_custom_call" | custom-call | flops 1073741824 | bytes 5242880 | tf_op jit(solution)/shard_map/readin/pallas_call | solution.py:88
  6.0 0.0 copy-start.6
  6.0 3.3 %collective-permute-start = (bf16[512,1024]{1,0:T(8,128)(2,1)S(1)}, bf16[512,1024]{1,0:T(8,128)(2,1)S(1)}, u32[]{:S(2)}, u32[]{:S(2)}) collective-permute-start(bf16[512,1024]{1,0:T(8,128)(2,1)S(1)} %get-tuple-element.13), channel_id=1, source_target_pairs={{0,8},{8,0},{1,9},{9,1},{2,10},{10,2},{3,11},{11,3},{4,12},{12,4},... | collective-permute-start | bytes 3145736 | tf_op jit(solution)/shard_map/ppermute | solution.py:35
  9.3 0.0 copy-done.4
  9.3 4.5 %readin.2 = (f32[512,1024]{1,0:T(8,128)S(1)}, f32[1,1024]{1,0:T(1,128)S(1)}) custom-call(s32[1]{0:T(128)} %bitcast.at_ref, s32[1024,1024]{1,0:T(8,128)} %spikes_ref.3, s32[1,1024]{1,0:T(1,128)S(1)} %bitcast.26, bf16[1024,1024]{1,0:T(8,128)(2,1)} %weight_ref.3), custom_call_target="tpu_custom_call" | custom-call | flops 1073741824 | bytes 5242880 | tf_op jit(solution)/shard_map/readin/pallas_call | solution.py:88
  13.9 0.0 collective-permute-done
  13.9 0.4 add_convert_fusion
  14.3 0.2 copy-done.7
  14.5 21.8 %all_to_all.40 = bf16[16,32,1024]{2,1,0:T(8,128)(2,1)} all-to-all(bf16[16,32,1024]{2,1,0:T(8,128)(2,1)S(1)} %bitcast.28), channel_id=1, replica_groups=mesh['y'=4,'zh'=4,'c'=2,'x'=4,'zl'=2] {'y','x'}, dimensions={0} | all-to-all | bytes 2097152 | tf_op jit(solution)/shard_map/all_to_all | solution.py:27
  36.2 1.5 reduce_sum.75
  37.7 1.7 %collective-permute-start.1 = (bf16[32,1024]{1,0:T(8,128)(2,1)S(1)}, bf16[32,1024]{1,0:T(8,128)(2,1)S(1)}, u32[]{:S(2)}, u32[]{:S(2)}) collective-permute-start(bf16[32,1024]{1,0:T(8,128)(2,1)S(1)} %reduce_sum.75), channel_id=1, source_target_pairs={{0,1},{1,0},{2,3},{3,2},{4,5},{5,4},{6,7},{7,6},{8,9},{9,8},{10,11... | collective-permute-start | bytes 196616 | tf_op jit(solution)/shard_map/ppermute | solution.py:39
  39.4 1.7 collective-permute-done.1
  41.1 21.1 %all_to_all.41.parts_ref = bf16[16,8,1024]{2,1,0:T(8,128)(2,1)S(1)} all-to-all(bf16[16,8,1024]{2,1,0:T(8,128)(2,1)S(1)} %bitcast.32), channel_id=1, replica_groups=mesh['y'=4,'zh'=4,'c'=2,'x'=4,'zl'=2] {'x','zh'}, dimensions={0} | all-to-all | bytes 524288 | tf_op jit(solution)/shard_map/all_to_all | solution.py:27
  62.2 0.0 copy-done.5
  62.2 0.4 project.1
  62.6 0.0 copy-start.9
  62.6 0.0 copy-start.10
  62.6 13.3 %all_to_all.42 = bf16[16,32,256]{2,1,0:T(8,128)(2,1)S(1)} all-to-all(bf16[16,32,256]{2,1,0:T(8,128)(2,1)S(1)} %get-tuple-element.16), channel_id=1, replica_groups=mesh['y'=4,'zh'=4,'c'=2,'x'=4,'zl'=2] {'y','zh'}, dimensions={0} | all-to-all | bytes 524288 | tf_op jit(solution)/shard_map/all_to_all | solution.py:27
  75.9 3.9 %collective-permute-start.2 = (bf16[512,256]{1,0:T(8,128)(2,1)S(1)}, bf16[512,256]{1,0:T(8,128)(2,1)S(1)}, u32[]{:S(2)}, u32[]{:S(2)}) collective-permute-start(bf16[512,256]{1,0:T(8,128)(2,1)S(1)} %bitcast.21), channel_id=1, source_target_pairs={{0,8},{8,0},{1,9},{9,1},{2,10},{10,2},{3,11},{11,3},{4,12},{12,4},... | collective-permute-start | bytes 786440 | tf_op jit(solution)/shard_map/ppermute | solution.py:35
  79.8 1.2 collective-permute-done.2.far_ref
  80.9 0.5 attend.1
  81.4 12.2 %all_to_all.43 = bf16[8,32,1024]{2,1,0:T(8,128)(2,1)S(1)} all-to-all(bf16[8,32,1024]{2,1,0:T(8,128)(2,1)S(1)} %attend.1), channel_id=1, replica_groups=mesh['y'=4,'zh'=4,'c'=2,'x'=4,'zl'=2] {'x','zl'}, dimensions={0} | all-to-all | bytes 1048576 | tf_op jit(solution)/shard_map/all_to_all | solution.py:27
  93.7 0.1 convert_reduce_fusion
  93.8 0.1 multiply_reduce_fusion
  93.9 1.8 %convolution_convert_fusion = bf16[32,1024]{1,0:T(8,128)(2,1)S(1)} fusion(bf16[512,1024]{1,0:T(8,128)(2,1)S(1)} %copy-done.9, bf16[1024,512]{1,0:T(8,128)(2,1)} %param.17, f32[32,1024]{1,0:T(8,128)S(1)} %get-tuple-element.22, f32[1024]{0:T(1024)S(1)} %copy-done.10, f32[32]{0:T(128)S(1)} %add_rsqrt_fusion.1), kind=kOutput, calls=%fused_computation.3 | convolution fusion | flops 67387392 | bytes 2297984 | tf_op jit(solution)/shard_map/dot_general | solution.py:243
  95.7 0.0 copy-start.12
  95.8 0.7 reshape.60
  96.4 3.4 %all-to-all-start.4 = ((bf16[8,4,1024]{2,1,0:T(4,128)(2,1)}), bf16[8,4,1024]{2,1,0:T(4,128)(2,1)S(1)}, u32[]{:S(2)}, u32[]{:S(2)}) async-start(bf16[8,4,1024]{2,1,0:T(4,128)(2,1)} %reshape.60), calls=%async_computation.4 | async-start | bytes 131072 | tf_op jit(solution)/shard_map/all_to_all | solution.py:27
  99.8 5.1 %all-to-all-done.4 = bf16[8,4,1024]{2,1,0:T(4,128)(2,1)S(1)} async-done(((bf16[8,4,1024]{2,1,0:T(4,128)(2,1)}), bf16[8,4,1024]{2,1,0:T(4,128)(2,1)S(1)}, u32[]{:S(2)}, u32[]{:S(2)}) %all-to-all-start.4) | async-done | bytes 65568 | tf_op jit(solution)/shard_map/all_to_all | solution.py:27
  104.9 0.1 multiply_reduce_fusion.1
  105.1 0.0 copy-done.11
  105.1 0.1 multiply_convert_fusion.6
  105.2 9.6 %all_to_all.44 = bf16[8,4,1024]{2,1,0:T(4,128)(2,1)S(1)} all-to-all(bf16[8,4,1024]{2,1,0:T(4,128)(2,1)S(1)} %broadcast_in_dim.42), channel_id=1, replica_groups=mesh['y'=4,'zh'=4,'c'=2,'x'=4,'zl'=2] {'zh','zl'}, dimensions={0} | all-to-all | bytes 131072 | tf_op jit(solution)/shard_map/all_to_all | solution.py:27
  114.8 0.1 broadcast_in_dim.44
  114.9 16.0 %all_to_all.45 = bf16[16,32,1024]{2,1,0:T(8,128)(2,1)S(1)} all-to-all(bf16[16,32,1024]{2,1,0:T(8,128)(2,1)S(1)} %broadcast_in_dim.44), channel_id=1, replica_groups=mesh['y'=4,'zh'=4,'c'=2,'x'=4,'zl'=2] {'y','x'}, dimensions={0} | all-to-all | bytes 2097152 | tf_op jit(solution)/shard_map/all_to_all | solution.py:27
  130.9 4.8 %collective-permute-start.3 = (bf16[512,1024]{1,0:T(8,128)(2,1)S(1)}, bf16[512,1024]{1,0:T(8,128)(2,1)}, u32[]{:S(2)}, u32[]{:S(2)}) collective-permute-start(bf16[512,1024]{1,0:T(8,128)(2,1)S(1)} %bitcast.29), channel_id=1, source_target_pairs={{0,8},{8,0},{1,9},{9,1},{2,10},{10,2},{3,11},{11,3},{4,12},{12,4},... | collective-permute-start | bytes 3145736 | tf_op jit(solution)/shard_map/ppermute | solution.py:35
  135.7 3.8 %subtract_reduce_fusion.1 = f32[1024]{0:T(1024)} fusion(s32[1024,1024]{1,0:T(8,128)} %spikes_ref.3, s32[]{:T(128)S(6)} %select_n.31, bf16[512,1024]{1,0:T(8,128)(2,1)S(1)} %bitcast.30, bf16[1024,1024]{1,0:T(8,128)(2,1)S(1)} %copy-done, f32[1024]{0:T(1024)S(1)} %copy-done.12), kind=kOutput, calls=%fused_computation.1 | convolution fusion | flops 1076362240 | bytes 5251076 | tf_op jit(solution)/shard_map/dot_general | solution.py:61
  139.6 0.0 collective-permute-done.3
  139.6 3.4 %subtract_reduce_fusion = f32[1024]{0:T(1024)} fusion(s32[1024,1024]{1,0:T(8,128)S(1)} %copy-done.8, s32[]{:T(128)S(6)} %select_n.32, bf16[512,1024]{1,0:T(8,128)(2,1)} %collective-permute-done.3, bf16[1024,1024]{1,0:T(8,128)(2,1)S(1)} %copy-done, f32[1024]{0:T(1024)S(1)} %copy-done.12), kind=kOutput, calls=%fused_computation | convolution fusion | flops 1076362240 | bytes 5251076 | tf_op jit(solution)/shard_map/dot_general | solution.py:61
  142.9 1.5 score.1
  144.5 5.2 %all-to-all-start.7 = ((f32[256,1,128]{2,1,0:T(1,128)}), f32[256,1,128]{2,1,0:T(1,128)S(1)}, u32[]{:S(2)}, u32[]{:S(2)}) async-start(f32[256,1,128]{2,1,0:T(1,128)} %get-tuple-element.20), calls=%async_computation.7 | async-start | bytes 262144 | tf_op jit(solution)/shard_map/all_to_all | solution.py:27
  149.7 1.5 dynamic-slice_select_fusion
  151.2 11.4 %all-to-all-done.7 = f32[256,1,128]{2,1,0:T(1,128)S(1)} async-done(((f32[256,1,128]{2,1,0:T(1,128)}), f32[256,1,128]{2,1,0:T(1,128)S(1)}, u32[]{:S(2)}, u32[]{:S(2)}) %all-to-all-start.7) | async-done | bytes 131104 | tf_op jit(solution)/shard_map/all_to_all | solution.py:27
  162.6 0.3 reduce_sum.82
  162.9 0.6 fusion.22
  (22 shorter events, 0.2 us)
Async XLA Ops:
  0.6 135.1 %copy-start = (bf16[1024,1024]{1,0:T(8,128)(2,1)S(1)}, bf16[1024,1024]{1,0:T(8,128)(2,1)}, u32[]{:S(2)}) copy-start(bf16[1024,1024]{1,0:T(8,128)(2,1)} %param.22) | copy-start | bytes 6291460
  0.7 0.8 copy-start.3
  1.5 7.8 %copy-start.4 = (s32[1024]{0:T(1024)S(1)}, s32[1024]{0:T(1024)}, u32[]{:S(2)}) copy-start(s32[1024]{0:T(1024)} %param.13) | copy-start | bytes 12292
  6.0 7.9 %copy-start.6 = (f32[1,1024]{1,0:T(1,128)}, f32[1,1024]{1,0:T(1,128)S(1)}, u32[]{:S(2)}) copy-start(f32[1,1024]{1,0:T(1,128)S(1)} %get-tuple-element.18.seen_too_ref) | copy-start | bytes 12292
  6.0 7.9 %collective-permute-start = (bf16[512,1024]{1,0:T(8,128)(2,1)S(1)}, bf16[512,1024]{1,0:T(8,128)(2,1)S(1)}, u32[]{:S(2)}, u32[]{:S(2)}) collective-permute-start(bf16[512,1024]{1,0:T(8,128)(2,1)S(1)} %get-tuple-element.13), channel_id=1, source_target_pairs={{0,8},{8,0},{1,9},{9,1},{2,10},{10,2},{3,11},{11,3},{4,12},{12,4},... | collective-permute-start | bytes 3145736 | tf_op jit(solution)/shard_map/ppermute | solution.py:35
  13.9 0.6 copy-start.7
  14.5 47.8 %copy-start.1 = (bf16[1024,3,128]{2,0,1:T(8,128)(2,1)S(1)}, bf16[1024,3,128]{2,0,1:T(8,128)(2,1)}, u32[]{:S(2)}) copy-start(bf16[1024,3,128]{2,0,1:T(8,128)(2,1)} %param.15) | copy-start | bytes 2359300
  14.5 47.8 %copy-start.5 = (f32[1024]{0:T(1024)S(1)}, f32[1024]{0:T(1024)}, u32[]{:S(2)}) copy-start(f32[1024]{0:T(1024)} %param.19) | copy-start | bytes 12292
  36.2 44.7 %copy-start.2 = (bf16[128,1024]{1,0:T(8,128)(2,1)S(1)}, bf16[128,1024]{1,0:T(8,128)(2,1)}, u32[]{:S(2)}) copy-start(bf16[128,1024]{1,0:T(8,128)(2,1)} %mix_ref.1) | copy-start | bytes 786436
  37.7 3.4 %collective-permute-start.1 = (bf16[32,1024]{1,0:T(8,128)(2,1)S(1)}, bf16[32,1024]{1,0:T(8,128)(2,1)S(1)}, u32[]{:S(2)}, u32[]{:S(2)}) collective-permute-start(bf16[32,1024]{1,0:T(8,128)(2,1)S(1)} %reduce_sum.75), channel_id=1, source_target_pairs={{0,1},{1,0},{2,3},{3,2},{4,5},{5,4},{6,7},{7,6},{8,9},{9,8},{10,11... | collective-permute-start | bytes 196616 | tf_op jit(solution)/shard_map/ppermute | solution.py:39
  62.6 31.3 %copy-start.9 = (bf16[512,1024]{1,0:T(8,128)(2,1)S(1)}, bf16[512,1024]{1,0:T(8,128)(2,1)}, u32[]{:S(2)}) copy-start(bf16[512,1024]{1,0:T(8,128)(2,1)} %param.18) | copy-start | bytes 3145732
  62.6 31.3 %copy-start.10 = (f32[1024]{0:T(1024)S(1)}, f32[1024]{0:T(1024)}, u32[]{:S(2)}) copy-start(f32[1024]{0:T(1024)} %param.20) | copy-start | bytes 12292
  75.9 5.0 %collective-permute-start.2 = (bf16[512,256]{1,0:T(8,128)(2,1)S(1)}, bf16[512,256]{1,0:T(8,128)(2,1)S(1)}, u32[]{:S(2)}, u32[]{:S(2)}) collective-permute-start(bf16[512,256]{1,0:T(8,128)(2,1)S(1)} %bitcast.21), channel_id=1, source_target_pairs={{0,8},{8,0},{1,9},{9,1},{2,10},{10,2},{3,11},{11,3},{4,12},{12,4},... | collective-permute-start | bytes 786440 | tf_op jit(solution)/shard_map/ppermute | solution.py:35
  93.7 11.4 %copy-start.11 = (f32[1024]{0:T(1024)S(1)}, f32[1024]{0:T(1024)}, u32[]{:S(2)}) copy-start(f32[1024]{0:T(1024)} %param.21) | copy-start | bytes 12292
  95.7 40.0 %copy-start.12 = (f32[1024]{0:T(1024)S(1)}, f32[1024]{0:T(1024)}, u32[]{:S(2)}) copy-start(f32[1024]{0:T(1024)} %param.23) | copy-start | bytes 12292
  96.4 8.5 %all-to-all-start.4 = ((bf16[8,4,1024]{2,1,0:T(4,128)(2,1)}), bf16[8,4,1024]{2,1,0:T(4,128)(2,1)S(1)}, u32[]{:S(2)}, u32[]{:S(2)}) async-start(bf16[8,4,1024]{2,1,0:T(4,128)(2,1)} %reshape.60), calls=%async_computation.4 | async-start | bytes 131072 | tf_op jit(solution)/shard_map/all_to_all | solution.py:27
  130.9 8.6 %collective-permute-start.3 = (bf16[512,1024]{1,0:T(8,128)(2,1)S(1)}, bf16[512,1024]{1,0:T(8,128)(2,1)}, u32[]{:S(2)}, u32[]{:S(2)}) collective-permute-start(bf16[512,1024]{1,0:T(8,128)(2,1)S(1)} %bitcast.29), channel_id=1, source_target_pairs={{0,8},{8,0},{1,9},{9,1},{2,10},{10,2},{3,11},{11,3},{4,12},{12,4},... | collective-permute-start | bytes 3145736 | tf_op jit(solution)/shard_map/ppermute | solution.py:35
  135.7 3.9 %copy-start.8 = (s32[1024,1024]{1,0:T(8,128)S(1)}, s32[1024,1024]{1,0:T(8,128)}, u32[]{:S(2)}) copy-start(s32[1024,1024]{1,0:T(8,128)} %spikes_ref.3) | copy-start | bytes 12582916
  144.5 18.1 %all-to-all-start.7 = ((f32[256,1,128]{2,1,0:T(1,128)}), f32[256,1,128]{2,1,0:T(1,128)S(1)}, u32[]{:S(2)}, u32[]{:S(2)}) async-start(f32[256,1,128]{2,1,0:T(1,128)} %get-tuple-element.20), calls=%async_computation.7 | async-start | bytes 262144 | tf_op jit(solution)/shard_map/all_to_all | solution.py:27

commit v6 on v5

--- a/solution.py
+++ b/solution.py
@@ -61,49 +61,43 @@
     return lax.dot_general(left, right, (((1,), (1,)), ((), ())), preferred_element_type=F32)
 
 
-def readin_kernel(at_ref, spikes_ref, held_ref, weight_ref, out_ref, counts_ref, total):
-    step = pl.program_id(0)
+def readin_kernel(at_ref, spikes_ref, held_ref, weight_ref, out_ref, counts_ref):
     block = spikes_ref[...]
     masked = (block * held_ref[...]).astype(F32).astype(BF16)
-    product = matmul(masked, weight_ref[...])
-    counts_ref[...] = jnp.sum(block.astype(F32), 0, keepdims=True)
-
-    @pl.when(step == 0)
-    def _():
-        total[...] = product
-
-    @pl.when(step > 0)
-    def _():
-        total[...] += product
-
-    @pl.when(step == pl.num_programs(0) - 1)
-    def _():
-        out_ref[...] = total[...].astype(out_ref.dtype)
+    out_ref[...] = matmul(masked, weight_ref[...]).astype(out_ref.dtype)
+    counted = jnp.sum(block.astype(F32), 0, keepdims=True)
+
+    @pl.when(pl.program_id(0) == 0)
+    def _():
+        counts_ref[...] = counted
+
+    @pl.when(pl.program_id(0) > 0)
+    def _():
+        counts_ref[...] += counted
 
 
 def readin(spikes, held, weight, which_half, dtype):
     frames, neurons = spikes.shape
     dim = weight.shape[1]
-    rows, width = frames // 2, neurons // 4
+    rows = frames // 4
     return pl.pallas_call(
         readin_kernel,
         out_shape=(
-            jax.ShapeDtypeStruct((rows, dim), dtype),
+            jax.ShapeDtypeStruct((frames // 2, dim), dtype),
             jax.ShapeDtypeStruct((1, neurons), F32),
         ),
         grid_spec=pltpu.PrefetchScalarGridSpec(
             num_scalar_prefetch=1,
-            grid=(4,),
+            grid=(2,),
             in_specs=[
-                pl.BlockSpec((rows, width), lambda k, at: (at[0], k)),
-                pl.BlockSpec((1, width), lambda k, at: (0, k)),
-                pl.BlockSpec((width, dim), lambda k, at: (k, 0)),
+                pl.BlockSpec((rows, neurons), lambda i, at: (2 * at[0] + i, 0)),
+                pl.BlockSpec((1, neurons), lambda i, at: (0, 0)),
+                pl.BlockSpec((neurons, dim), lambda i, at: (0, 0)),
             ],
             out_specs=[
-                pl.BlockSpec((rows, dim), lambda k, at: (0, 0)),
-                pl.BlockSpec((1, width), lambda k, at: (0, k)),
+                pl.BlockSpec((rows, dim), lambda i, at: (i, 0)),
+                pl.BlockSpec((1, neurons), lambda i, at: (0, 0)),
             ],
-            scratch_shapes=[pltpu.VMEM((rows, dim), F32)],
         ),
         compiler_params=params(("arbitrary",)),
         cost_estimate=pl.CostEstimate(
@@ -112,7 +106,63 @@
             transcendentals=0,
         ),
         name="readin",
-    )(which_half.reshape(1), in_hbm(spikes), held, in_hbm(weight))
+    )(which_half.reshape(1), in_hbm(spikes), in_hbm(held), in_hbm(weight))
+
+
+def plane_kernel(parts_ref, out_ref):
+    total = parts_ref[0].astype(F32)
+    for i in range(1, parts_ref.shape[0]):
+        total += parts_ref[i].astype(F32)
+    out_ref[...] = total.astype(BF16)
+
+
+def pair_kernel(mine_ref, other_ref, out_ref):
+    total = (mine_ref[...].astype(F32) + other_ref[...].astype(F32)).astype(BF16)
+    piece = out_ref.shape[1]
+    for i in range(out_ref.shape[0]):
+        start = piece * (i % 4)
+        out_ref[i] = total[start : start + piece]
+
+
+def small(body, name, out_shapes, *operands, scalar=None):
+    specs = [whole(array) for array in operands]
+    if scalar is not None:
+        specs.insert(0, pl.BlockSpec(memory_space=pltpu.SMEM))
+        operands = (scalar.reshape(1),) + operands
+    return pl.pallas_call(
+        body,
+        out_shape=[jax.ShapeDtypeStruct(*shape) for shape in out_shapes],
+        in_specs=specs,
+        out_specs=[
+            pl.BlockSpec(shape, lambda n=len(shape): (0,) * n) for shape, _ in out_shapes
+        ],
+        compiler_params=params(None),
+        name=name,
+    )(*operands)
+
+
+def mlp_kernel(parts_ref, stream_ref, gain_ref, up_ref, down_ref, mixed_ref, out_ref):
+    mixed = stream_ref[...]
+    attn = parts_ref[0].astype(F32)
+    for i in range(1, parts_ref.shape[0]):
+        attn += parts_ref[i].astype(F32)
+    mixed += attn
+    mlp_in = normed(mixed, gain_ref[...]).astype(BF16)
+    hidden_act = jax.nn.gelu(matmul(mlp_in, up_ref[...])).astype(BF16)
+    part = matmul(hidden_act, down_ref[...])
+    rows = out_ref.shape[1]
+    for i in range(out_ref.shape[0]):
+        mixed_ref[i] = mixed[rows * i : rows * (i + 1)]
+        out_ref[i] = part[rows * i : rows * (i + 1)].astype(BF16)
+
+
+def latents_kernel(at_ref, parts_ref, mixed_ref, gain_ref, out_ref):
+    total = parts_ref[0].astype(F32)
+    for i in range(1, parts_ref.shape[0]):
+        total += parts_ref[i].astype(F32)
+    own = normed(mixed_ref[at_ref[0]] + total, gain_ref[...]).astype(BF16)
+    for i in range(out_ref.shape[0]):
+        out_ref[i] = own
 
 
 def project_kernel(parts_ref, gain_ref, weight_ref, stream_ref, queries_ref, kv_ref):
@@ -173,31 +223,79 @@
     )(*operands)
 
 
-def score_kernel(frames, near_ref, far_ref, held_ref, seen_ref, seen_too_ref, bits_ref, sums_ref):
-    heldout = (1 - held_ref[...]).astype(F32)
-    count = seen_ref[...] + seen_too_ref[...]
+def likelihood(lat_ref, spikes_ref, weight_ref, bias_ref):
+    log_rate = matmul_nt(lat_ref[...], weight_ref[...]) + bias_ref[...]
+    observed = spikes_ref[...].astype(F32)
+    return jnp.sum(observed * log_rate - jnp.exp(log_rate), 0, keepdims=True)
+
+
+def readout_kernel(at_ref, lat, spikes, weight, bias, out):
+    out[...] = likelihood(lat, spikes, weight, bias)
+
+
+def score_kernel(
+    frames, at_ref, lat, spikes, weight, bias, before, held, seen, seen_too, bits, sums, total
+):
+    step = pl.program_id(0)
+    model_ll = before[...] + likelihood(lat, spikes, weight, bias)
+    heldout = (1 - held[...]).astype(F32)
+    count = seen[...] + seen_too[...]
     null_ll = count * jnp.log((count + 1.0) / frames) - (count + 1.0)
-    gained = heldout * (near_ref[...] + far_ref[...] - null_ll)
-    bits_ref[...] = gained / (math.log(2.0) * (count + 1.0))
+    gained = heldout * (model_ll - null_ll)
+    bits[...] = gained / (math.log(2.0) * (count + 1.0))
     lane = lax.broadcasted_iota(jnp.int32, (1, 128), 1)
     gain_sum = jnp.sum(gained, 1, keepdims=True)
     spike_sum = jnp.sum(heldout * count, 1, keepdims=True)
     here = jnp.where(lane == 0, gain_sum, jnp.where(lane == 1, spike_sum, 0.0))
-    sums_ref[...] = jnp.broadcast_to(here[None], sums_ref.shape)
-
-
-def score(frames, copies, *rows):
-    shape = (copies, 1, 128)
-    return pl.pallas_call(
-        functools.partial(score_kernel, float(frames)),
-        out_shape=(
-            jax.ShapeDtypeStruct(rows[0].shape, F32),
-            jax.ShapeDtypeStruct(shape, F32),
-        ),
-        in_specs=[whole(row) for row in rows],
-        out_specs=[whole(rows[0]), pl.BlockSpec(shape, lambda: (0, 0, 0))],
-        name="score",
-    )(*rows)
+
+    @pl.when(step == 0)
+    def _():
+        total[...] = here
+
+    @pl.when(step > 0)
+    def _():
+        total[...] += here
+
+    @pl.when(step == pl.num_programs(0) - 1)
+    def _():
+        sums[...] = jnp.broadcast_to(total[...][None], sums.shape)
+
+
+def readout(which_half, lat, spikes, weight, bias, scoring=(), copies=256):
+    frames, neurons = spikes.shape
+    rows, dim = lat.shape
+    width = neurons // 4
+    row = pl.BlockSpec((1, width), lambda j, at: (0, j))
+    out_shape, out_specs = [jax.ShapeDtypeStruct((1, neurons), F32)], [row]
+    body, scratch = readout_kernel, []
+    if scoring:
+        body = functools.partial(score_kernel, float(frames))
+        out_shape.append(jax.ShapeDtypeStruct((copies, 1, 128), F32))
+        out_specs.append(pl.BlockSpec((copies, 1, 128), lambda j, at: (0, 0, 0)))
+        scratch = [pltpu.VMEM((1, 128), F32)]
+    return pl.pallas_call(
+        body,
+        out_shape=out_shape,
+        grid_spec=pltpu.PrefetchScalarGridSpec(
+            num_scalar_prefetch=1,
+            grid=(neurons // width,),
+            in_specs=[
+                pl.BlockSpec((rows, dim), lambda j, at: (0, 0)),
+                pl.BlockSpec((rows, width), lambda j, at: (at[0], j)),
+                pl.BlockSpec((width, dim), lambda j, at: (j, 0)),
+            ]
+            + [row] * (1 + len(scoring)),
+            out_specs=out_specs,
+            scratch_shapes=scratch,
+        ),
+        compiler_params=params(("arbitrary",)),
+        cost_estimate=pl.CostEstimate(
+            flops=2 * rows * dim * neurons,
+            bytes_accessed=4 * rows * neurons + 2 * weight.size,
+            transcendentals=rows * neurons,
+        ),
+        name="score" if scoring else "readout",
+    )(which_half.reshape(1), lat, in_hbm(spikes), weight, bias, *scoring)
 
 
 def on_device(
@@ -225,43 +323,40 @@
     theirs = other_core(given)
     own, counts_near = readin(spikes, held_row, readin_weight, core, F32)
     chip_sum = (own + theirs.astype(F32)).astype(BF16)
-    plane_sum = jnp.sum(exchange(chip_sum.reshape(16, -1, model_dim), PLANE).astype(F32), 0)
-    plane_sum = plane_sum.astype(BF16)
-    pair_sum = (plane_sum.astype(F32) + other_layer(plane_sum).astype(F32)).astype(BF16)
-    blocks = jnp.broadcast_to(pair_sum.reshape(1, 4, -1, model_dim), (4, 4, 8, model_dim))
-    parts = exchange(blocks.reshape(16, 8, model_dim), ("x", "zh"))
+    wide = ((rows_here, model_dim), BF16)
+    (plane_sum,) = small(
+        plane_kernel, "plane", [wide], exchange(chip_sum.reshape(16, -1, model_dim), PLANE)
+    )
+    (blocks,) = small(
+        pair_kernel, "pair", [((16, rows_here // 4, model_dim), BF16)],
+        plane_sum, other_layer(plane_sum),
+    )
+    parts = exchange(blocks, ("x", "zh"))
 
     stream, queries, kv_own = project(
         parts, norm_gain[None, :], jnp.swapaxes(qkv_weight, 0, 1), lax.axis_size(YZ)
     )
     kv_near = exchange(kv_own, YZ).reshape(half, 2 * HEAD_DIM)
     attn_parts = attend(queries, kv_near, other_core(kv_near), out_weight, lax.axis_size(TM))
-    mixed_state = stream + jnp.sum(exchange(attn_parts, TM).astype(F32), 0)
-
-    mlp_in = normed(mixed_state, mlp_gain).astype(BF16)
-    hidden_act = jax.nn.gelu(jnp.dot(mlp_in, up_weight, preferred_element_type=F32)).astype(BF16)
-    mlp_part = jnp.dot(hidden_act, down_weight, preferred_element_type=F32)
-    mlp_sum = jnp.sum(
-        exchange(mlp_part.astype(BF16).reshape(8, -1, model_dim), TM).astype(F32), 0
-    )
-    rows_own = mlp_sum.shape[0]
-    own_mixed = lax.dynamic_slice_in_dim(mixed_state, lax.axis_index(TM) * rows_own, rows_own, 0)
-    own_latents = normed(own_mixed + mlp_sum, final_gain).astype(BF16)
-
-    column = to_all(own_latents, ("zh", "zl")).reshape(rows_here, model_dim)
+
+    thin = (8, rows_here // 8, model_dim)
+    mixed, mlp_parts = small(
+        mlp_kernel, "mlp", [(thin, F32), (thin, BF16)],
+        exchange(attn_parts, TM), stream, mlp_gain[None, :], up_weight, down_weight,
+    )
+    (own_latents,) = small(
+        latents_kernel, "latents", [(thin, BF16)],
+        exchange(mlp_parts, TM), mixed, final_gain[None, :], scalar=lax.axis_index(TM),
+    )
+
+    column = exchange(own_latents, ("zh", "zl")).reshape(rows_here, model_dim)
     lat_near = to_all(column, PLANE).reshape(half, model_dim)
     lat_far = other_core(lat_near)
 
-    def likelihood(lat, start):
-        log_rate = matmul_nt(lat, readout_weight) + readout_bias[None, :]
-        observed = lax.dynamic_slice_in_dim(spikes, start, half, 0).astype(F32)
-        return jnp.sum(observed * log_rate - jnp.exp(log_rate), 0, keepdims=True)
-
-    bits, sums = score(
-        frames_all, lax.axis_size(ALL),
-        likelihood(lat_near, core * half), likelihood(lat_far, (1 - core) * half),
-        held_row, counts_near, counts_far,
-    )
+    bias_row = readout_bias[None, :]
+    (ll_near,) = readout(core, lat_near, spikes, readout_weight, bias_row)
+    scoring = (ll_near, held_row, counts_near, counts_far)
+    bits, sums = readout(1 - core, lat_far, spikes, readout_weight, bias_row, scoring)
     totals = jnp.sum(exchange(sums, ALL), (0, 1))
     bits_total = totals[0] / (math.log(2.0) * (1.0 + totals[1]))
 

time: 167 us -> 160 us (0.958)
  matrix products: 9.02 us -> 0 us
  Pallas kernels: 11.4 us -> 18 us
  other arithmetic: 4.12 us -> 2.16 us
  local copies, waits for them, and re-layouts: 2.48 us -> 0.77 us
    dot_general x3 -> x0, matrix products: 9.02 us -> none  [the longest x2 7.21 us: matmul_nt(): lax.dot_general(left, right, (((1,), (1,)), ((), ())), preferred_element_...]
    pallas_call x3 -> x8, Pallas kernels: 10.5 us -> 17.1 us  [the longest x2 8.65 us: readout(): pl.pallas_call(body, out_shape=out_shape, grid_spec=pltpu.PrefetchScalarG...]
    reduce_sum x5 -> x0, other arithmetic: 1.84 us -> none  [the longest x1 1.46 us: on_device(): jnp.sum(exchange(chip_sum.reshape(16, -1, model_dim), PLANE).astype(F32), 0)]
  transfers between devices with their start and end apart: 6 -> 6, of which waited for: 4 -> 4; matrix products, arithmetic and copies ran while one was open for 3% -> 1% of each run, Pallas kernels for 3% -> 4%
where the time goes in v6:
time: 160 us
  blocking collectives  93.9 us (59%)
  starting transfers between devices  22.2 us (14%)
  waiting for transfers between devices  19.5 us (12%)
  Pallas kernels  18 us (11%)
  between operations  3.25 us (2%)
  other arithmetic  2.16 us (1%)
    all_to_all x6, blocking collectives, exchange(): return lax.all_to_all(blocks, axes, 0, 0, tiled=True)  93.9 us
    all_to_all x2, waiting for transfers between devices, exchange(): return lax.all_to_all(blocks, axes, 0, 0, tiled=True)  16.7 us
    ppermute x3, starting transfers between devices, other_core(): return lax.ppermute(block, 'c', [(0, 1), (1, 0)])  12 us
    pallas_call x2, Pallas kernels, readout(): pl.pallas_call(body, out_shape=out_shape, grid_spec=pltpu.PrefetchScalarG...  8.65 us
    all_to_all x2, starting transfers between devices, exchange(): return lax.all_to_all(blocks, axes, 0, 0, tiled=True)  8.58 us
    pallas_call x2, Pallas kernels, readin(): pl.pallas_call(readin_kernel, out_shape=(jax.ShapeDtypeStruct((frames //...  6.89 us
  transfers between devices with their start and end apart: 6, of which 4 were waited for; matrix products, arithmetic and copies ran while one was open for 1% of the time, Pallas kernels for 4%

profile of v6, /device:TPU:1, one launch (start us, length us, event | category | flops | bytes accessed | tf_op | source)
XLA Modules:
  0.0 159.8 jit_solution(940533318010282059)
XLA Ops:
  0.6 3.5 %readin.3 = (bf16[512,1024]{1,0:T(8,128)(2,1)S(1)}, f32[1,1024]{1,0:T(1,128)S(1)}) custom-call(s32[1]{0:T(128)} %bitcast.3.at_ref, s32[1024,1024]{1,0:T(8,128)} %spikes.3, s32[1,1024]{1,0:T(1,128)} %bitcast.20, bf16[1024,1024]{1,0:T(8,128)(2,1)} %weight_ref.3), custom_call_target="tpu_custom_call" | custom-call | flops 1073741824 | bytes 5242880 | tf_op jit(solution)/shard_map/readin/pallas_call | solution.py:83
  4.1 3.3 %collective-permute-start = (bf16[512,1024]{1,0:T(8,128)(2,1)S(1)}, bf16[512,1024]{1,0:T(8,128)(2,1)S(1)}, u32[]{:S(2)}, u32[]{:S(2)}) collective-permute-start(bf16[512,1024]{1,0:T(8,128)(2,1)S(1)} %get-tuple-element.15), channel_id=1, source_target_pairs={{0,8},{8,0},{1,9},{9,1},{2,10},{10,2},{3,11},{11,3},{4,12},{12,4},... | collective-permute-start | bytes 3145736 | tf_op jit(solution)/shard_map/ppermute | solution.py:35
  7.4 3.4 %readin.2 = (f32[512,1024]{1,0:T(8,128)S(1)}, f32[1,1024]{1,0:T(1,128)S(1)}) custom-call(s32[1]{0:T(128)} %bitcast.1.at_ref, s32[1024,1024]{1,0:T(8,128)} %spikes.3, s32[1,1024]{1,0:T(1,128)} %bitcast.21, bf16[1024,1024]{1,0:T(8,128)(2,1)} %weight_ref.3), custom_call_target="tpu_custom_call" | custom-call | flops 1073741824 | bytes 5242880 | tf_op jit(solution)/shard_map/readin/pallas_call | solution.py:83
  10.9 0.0 collective-permute-done
  10.9 0.4 add_convert_fusion
  11.3 0.0 copy-start.4
  11.3 0.0 copy-start.8
  11.3 21.7 %all_to_all.40.parts_ref = bf16[16,32,1024]{2,1,0:T(8,128)(2,1)S(1)} all-to-all(bf16[16,32,1024]{2,1,0:T(8,128)(2,1)S(1)} %bitcast.28), channel_id=1, replica_groups=mesh['y'=4,'zh'=4,'c'=2,'x'=4,'zl'=2] {'y','x'}, dimensions={0} | all-to-all | bytes 2097152 | tf_op jit(solution)/shard_map/all_to_all | solution.py:27
  33.0 0.0 copy-start.5
  33.0 0.1 plane.1.mine_ref
  33.1 1.7 %collective-permute-start.1 = (bf16[32,1024]{1,0:T(8,128)(2,1)S(1)}, bf16[32,1024]{1,0:T(8,128)(2,1)S(1)}, u32[]{:S(2)}, u32[]{:S(2)}) collective-permute-start(bf16[32,1024]{1,0:T(8,128)(2,1)S(1)} %plane.1.mine_ref), channel_id=1, source_target_pairs={{0,1},{1,0},{2,3},{3,2},{4,5},{5,4},{6,7},{7,6},{8,9},{9,8},{10,11... | collective-permute-start | bytes 196616 | tf_op jit(solution)/shard_map/ppermute | solution.py:39
  34.8 1.7 %collective-permute-done.1.other_ref = bf16[32,1024]{1,0:T(8,128)(2,1)S(1)} collective-permute-done((bf16[32,1024]{1,0:T(8,128)(2,1)S(1)}, bf16[32,1024]{1,0:T(8,128)(2,1)S(1)}, u32[]{:S(2)}, u32[]{:S(2)}) %collective-permute-start.1) | collective-permute-done | bytes 65568 | tf_op jit(solution)/shard_map/ppermute | solution.py:39
  36.5 21.1 %all_to_all.41.parts_ref = bf16[16,8,1024]{2,1,0:T(8,128)(2,1)S(1)} all-to-all(bf16[16,8,1024]{2,1,0:T(8,128)(2,1)S(1)} %pair.1), channel_id=1, replica_groups=mesh['y'=4,'zh'=4,'c'=2,'x'=4,'zl'=2] {'x','zh'}, dimensions={0} | all-to-all | bytes 524288 | tf_op jit(solution)/shard_map/all_to_all | solution.py:27
  57.6 0.0 copy-done.4
  57.6 0.0 copy-done.8
  57.7 0.4 project.1
  58.0 13.3 %all_to_all.42 = bf16[16,32,256]{2,1,0:T(8,128)(2,1)S(1)} all-to-all(bf16[16,32,256]{2,1,0:T(8,128)(2,1)S(1)} %get-tuple-element.17), channel_id=1, replica_groups=mesh['y'=4,'zh'=4,'c'=2,'x'=4,'zl'=2] {'y','zh'}, dimensions={0} | all-to-all | bytes 524288 | tf_op jit(solution)/shard_map/all_to_all | solution.py:27
  71.3 3.8 %collective-permute-start.2 = (bf16[512,256]{1,0:T(8,128)(2,1)S(1)}, bf16[512,256]{1,0:T(8,128)(2,1)S(1)}, u32[]{:S(2)}, u32[]{:S(2)}) collective-permute-start(bf16[512,256]{1,0:T(8,128)(2,1)S(1)} %bitcast.17), channel_id=1, source_target_pairs={{0,8},{8,0},{1,9},{9,1},{2,10},{10,2},{3,11},{11,3},{4,12},{12,4},... | collective-permute-start | bytes 786440 | tf_op jit(solution)/shard_map/ppermute | solution.py:35
  75.2 1.2 collective-permute-done.2.far_ref
  76.3 0.0 copy-done.5
  76.3 0.5 attend.1
  76.8 0.0 copy-start.10
  76.9 12.2 %all_to_all.43.parts_ref = bf16[8,32,1024]{2,1,0:T(8,128)(2,1)S(1)} all-to-all(bf16[8,32,1024]{2,1,0:T(8,128)(2,1)S(1)} %attend.1), channel_id=1, replica_groups=mesh['y'=4,'zh'=4,'c'=2,'x'=4,'zl'=2] {'x','zl'}, dimensions={0} | all-to-all | bytes 1048576 | tf_op jit(solution)/shard_map/all_to_all | solution.py:27
  89.1 0.0 copy-done.2
  89.1 0.0 copy-done.3
  89.1 0.0 copy-done.9
  89.1 1.3 mlp.1
  90.4 3.5 %all-to-all-start.4 = ((bf16[8,4,1024]{2,1,0:T(4,128)(2,1)}), bf16[8,4,1024]{2,1,0:T(4,128)(2,1)S(1)}, u32[]{:S(2)}, u32[]{:S(2)}) async-start(bf16[8,4,1024]{2,1,0:T(4,128)(2,1)} %get-tuple-element.19), calls=%async_computation.4 | async-start | bytes 131072 | tf_op jit(solution)/shard_map/all_to_all | solution.py:27
  93.9 5.1 %all-to-all-done.4.parts_ref = bf16[8,4,1024]{2,1,0:T(4,128)(2,1)S(1)} async-done(((bf16[8,4,1024]{2,1,0:T(4,128)(2,1)}), bf16[8,4,1024]{2,1,0:T(4,128)(2,1)S(1)}, u32[]{:S(2)}, u32[]{:S(2)}) %all-to-all-start.4) | async-done | bytes 65568 | tf_op jit(solution)/shard_map/all_to_all | solution.py:27
  99.0 0.0 copy-done.10
  99.0 0.1 latents.1
  99.1 9.6 %all_to_all.44 = bf16[8,4,1024]{2,1,0:T(4,128)(2,1)S(1)} all-to-all(bf16[8,4,1024]{2,1,0:T(4,128)(2,1)S(1)} %latents.1), channel_id=1, replica_groups=mesh['y'=4,'zh'=4,'c'=2,'x'=4,'zl'=2] {'zh','zl'}, dimensions={0} | all-to-all | bytes 131072 | tf_op jit(solution)/shard_map/all_to_all | solution.py:27
  108.8 0.1 broadcast_in_dim.27
  108.9 16.0 %all_to_all.45 = bf16[16,32,1024]{2,1,0:T(8,128)(2,1)S(1)} all-to-all(bf16[16,32,1024]{2,1,0:T(8,128)(2,1)S(1)} %broadcast_in_dim.27), channel_id=1, replica_groups=mesh['y'=4,'zh'=4,'c'=2,'x'=4,'zl'=2] {'y','x'}, dimensions={0} | all-to-all | bytes 2097152 | tf_op jit(solution)/shard_map/all_to_all | solution.py:27
  124.9 4.8 %collective-permute-start.3 = (bf16[512,1024]{1,0:T(8,128)(2,1)S(1)}, bf16[512,1024]{1,0:T(8,128)(2,1)S(1)}, u32[]{:S(2)}, u32[]{:S(2)}) collective-permute-start(bf16[512,1024]{1,0:T(8,128)(2,1)S(1)} %bitcast.14), channel_id=1, source_target_pairs={{0,8},{8,0},{1,9},{9,1},{2,10},{10,2},{3,11},{11,3},{4,12},{12,4},... | collective-permute-start | bytes 3145736 | tf_op jit(solution)/shard_map/ppermute | solution.py:35
  129.7 0.0 copy-done
  129.7 0.0 copy-done.7
  129.7 3.7 %readout.1.before = f32[1,1024]{1,0:T(1,128)S(1)} custom-call(s32[1]{0:T(128)} %bitcast.1.at_ref, bf16[512,1024]{1,0:T(8,128)(2,1)S(1)} %bitcast.15, s32[1024,1024]{1,0:T(8,128)} %spikes.3, bf16[1024,1024]{1,0:T(8,128)(2,1)S(1)} %copy-done, f32[1,1024]{1,0:T(1,128)S(1)} %bitcast.23), custom_call_target="tpu_custom_call" | custom-call | flops 1073741824 | bytes 4194304 | tf_op jit(solution)/shard_map/readout/pallas_call | solution.py:276
  133.3 0.0 collective-permute-done.3.lat
  133.4 0.0 copy-start.1
  133.4 0.0 copy-done.6
  133.4 5.0 %score.1 = (f32[1,1024]{1,0:T(1,128)}, f32[256,1,128]{2,1,0:T(1,128)}) custom-call(s32[1]{0:T(128)} %bitcast.3.at_ref, bf16[512,1024]{1,0:T(8,128)(2,1)S(1)} %collective-permute-done.3.lat, s32[1024,1024]{1,0:T(8,128)} %spikes.3, bf16[1024,1024]{1,0:T(8,128)(2,1)S(1)} %copy-done, f32[1,1024]{1,0:T(1,128)S(1)} %bitcast.24, f32[1,1024]{1,0:T(1,128)S(1)} %readout.1.before, ...), custom_call_target="tpu_custom_call" | custom-call | flops 1073741824 | bytes 4194304 | tf_op jit(solution)/shard_map/score/pallas_call | solution.py:276
  138.4 0.0 copy-done.1
  138.4 5.1 %all-to-all-start.7 = ((f32[256,1,128]{2,1,0:T(1,128)}), f32[256,1,128]{2,1,0:T(1,128)S(1)}, u32[]{:S(2)}, u32[]{:S(2)}) async-start(f32[256,1,128]{2,1,0:T(1,128)} %get-tuple-element.24), calls=%async_computation.7 | async-start | bytes 262144 | tf_op jit(solution)/shard_map/all_to_all | solution.py:27
  143.5 1.5 dynamic-slice_select_fusion
  145.0 11.6 %all-to-all-done.7 = f32[256,1,128]{2,1,0:T(1,128)S(1)} async-done(((f32[256,1,128]{2,1,0:T(1,128)}), f32[256,1,128]{2,1,0:T(1,128)S(1)}, u32[]{:S(2)}, u32[]{:S(2)}) %all-to-all-start.7) | async-done | bytes 131104 | tf_op jit(solution)/shard_map/all_to_all | solution.py:27
  156.5 0.3 reduce_sum.9
  156.8 0.6 fusion
  (8 shorter events, 0.1 us)
Async XLA Ops:
  4.1 6.8 %collective-permute-start = (bf16[512,1024]{1,0:T(8,128)(2,1)S(1)}, bf16[512,1024]{1,0:T(8,128)(2,1)S(1)}, u32[]{:S(2)}, u32[]{:S(2)}) collective-permute-start(bf16[512,1024]{1,0:T(8,128)(2,1)S(1)} %get-tuple-element.15), channel_id=1, source_target_pairs={{0,8},{8,0},{1,9},{9,1},{2,10},{10,2},{3,11},{11,3},{4,12},{12,4},... | collective-permute-start | bytes 3145736 | tf_op jit(solution)/shard_map/ppermute | solution.py:35
  11.3 46.4 %copy-start.4 = (bf16[1024,3,128]{2,0,1:T(8,128)(2,1)S(1)}, bf16[1024,3,128]{2,0,1:T(8,128)(2,1)}, u32[]{:S(2)}) copy-start(bf16[1024,3,128]{2,0,1:T(8,128)(2,1)} %param.15) | copy-start | bytes 2359300
  11.3 46.4 %copy-start.8 = (f32[1024]{0:T(1024)S(1)}, f32[1024]{0:T(1024)}, u32[]{:S(2)}) copy-start(f32[1024]{0:T(1024)} %param.19) | copy-start | bytes 12292
  33.0 43.4 %copy-start.5 = (bf16[128,1024]{1,0:T(8,128)(2,1)S(1)}, bf16[128,1024]{1,0:T(8,128)(2,1)}, u32[]{:S(2)}) copy-start(bf16[128,1024]{1,0:T(8,128)(2,1)} %mix_ref.1) | copy-start | bytes 786436
  33.1 3.4 %collective-permute-start.1 = (bf16[32,1024]{1,0:T(8,128)(2,1)S(1)}, bf16[32,1024]{1,0:T(8,128)(2,1)S(1)}, u32[]{:S(2)}, u32[]{:S(2)}) collective-permute-start(bf16[32,1024]{1,0:T(8,128)(2,1)S(1)} %plane.1.mine_ref), channel_id=1, source_target_pairs={{0,1},{1,0},{2,3},{3,2},{4,5},{5,4},{6,7},{7,6},{8,9},{9,8},{10,11... | collective-permute-start | bytes 196616 | tf_op jit(solution)/shard_map/ppermute | solution.py:39
  57.6 31.5 %copy-start.2 = (bf16[1024,512]{1,0:T(8,128)(2,1)S(1)}, bf16[1024,512]{1,0:T(8,128)(2,1)}, u32[]{:S(2)}) copy-start(bf16[1024,512]{1,0:T(8,128)(2,1)} %up_ref.1) | copy-start | bytes 3145732
  57.6 31.5 %copy-start.3 = (bf16[512,1024]{1,0:T(8,128)(2,1)S(1)}, bf16[512,1024]{1,0:T(8,128)(2,1)}, u32[]{:S(2)}) copy-start(bf16[512,1024]{1,0:T(8,128)(2,1)} %down_ref.1) | copy-start | bytes 3145732
  57.6 31.5 %copy-start.9 = (f32[1024]{0:T(1024)S(1)}, f32[1024]{0:T(1024)}, u32[]{:S(2)}) copy-start(f32[1024]{0:T(1024)} %param.20) | copy-start | bytes 12292
  71.3 5.0 %collective-permute-start.2 = (bf16[512,256]{1,0:T(8,128)(2,1)S(1)}, bf16[512,256]{1,0:T(8,128)(2,1)S(1)}, u32[]{:S(2)}, u32[]{:S(2)}) collective-permute-start(bf16[512,256]{1,0:T(8,128)(2,1)S(1)} %bitcast.17), channel_id=1, source_target_pairs={{0,8},{8,0},{1,9},{9,1},{2,10},{10,2},{3,11},{11,3},{4,12},{12,4},... | collective-permute-start | bytes 786440 | tf_op jit(solution)/shard_map/ppermute | solution.py:35
  76.8 22.2 %copy-start.10 = (f32[1024]{0:T(1024)S(1)}, f32[1024]{0:T(1024)}, u32[]{:S(2)}) copy-start(f32[1024]{0:T(1024)} %param.21) | copy-start | bytes 12292
  90.4 39.3 %copy-start = (bf16[1024,1024]{1,0:T(8,128)(2,1)S(1)}, bf16[1024,1024]{1,0:T(8,128)(2,1)}, u32[]{:S(2)}) copy-start(bf16[1024,1024]{1,0:T(8,128)(2,1)} %weight.3) | copy-start | bytes 6291460
  90.4 39.3 %copy-start.7 = (f32[1024]{0:T(1024)S(1)}, f32[1024]{0:T(1024)}, u32[]{:S(2)}) copy-start(f32[1024]{0:T(1024)} %param.23) | copy-start | bytes 12292
  90.4 8.6 %all-to-all-start.4 = ((bf16[8,4,1024]{2,1,0:T(4,128)(2,1)}), bf16[8,4,1024]{2,1,0:T(4,128)(2,1)S(1)}, u32[]{:S(2)}, u32[]{:S(2)}) async-start(bf16[8,4,1024]{2,1,0:T(4,128)(2,1)} %get-tuple-element.19), calls=%async_computation.4 | async-start | bytes 131072 | tf_op jit(solution)/shard_map/all_to_all | solution.py:27
  124.9 8.5 %collective-permute-start.3 = (bf16[512,1024]{1,0:T(8,128)(2,1)S(1)}, bf16[512,1024]{1,0:T(8,128)(2,1)S(1)}, u32[]{:S(2)}, u32[]{:S(2)}) collective-permute-start(bf16[512,1024]{1,0:T(8,128)(2,1)S(1)} %bitcast.14), channel_id=1, source_target_pairs={{0,8},{8,0},{1,9},{9,1},{2,10},{10,2},{3,11},{11,3},{4,12},{12,4},... | collective-permute-start | bytes 3145736 | tf_op jit(solution)/shard_map/ppermute | solution.py:35
  129.7 3.7 %copy-start.6 = (s32[1024]{0:T(1024)S(1)}, s32[1024]{0:T(1024)}, u32[]{:S(2)}) copy-start(s32[1024]{0:T(1024)} %param.13) | copy-start | bytes 12292
  133.4 5.0 %copy-start.1 = (bf16[512,1024]{1,0:T(8,128)(2,1)}, bf16[512,1024]{1,0:T(8,128)(2,1)S(1)}, u32[]{:S(2)}) copy-start(bf16[512,1024]{1,0:T(8,128)(2,1)S(1)} %collective-permute-done.3.lat) | copy-start | bytes 3145732
  138.4 18.2 %all-to-all-start.7 = ((f32[256,1,128]{2,1,0:T(1,128)}), f32[256,1,128]{2,1,0:T(1,128)S(1)}, u32[]{:S(2)}, u32[]{:S(2)}) async-start(f32[256,1,128]{2,1,0:T(1,128)} %get-tuple-element.24), calls=%async_computation.7 | async-start | bytes 262144 | tf_op jit(solution)/shard_map/all_to_all | solution.py:27

commit v7 on v6

--- a/solution.py
+++ b/solution.py
@@ -106,7 +106,7 @@
             transcendentals=0,
         ),
         name="readin",
-    )(which_half.reshape(1), in_hbm(spikes), in_hbm(held), in_hbm(weight))
+    )(which_half.reshape(1), in_hbm(spikes), in_hbm(held), weight)
 
 
 def plane_kernel(parts_ref, out_ref):
@@ -237,42 +237,48 @@
     frames, at_ref, lat, spikes, weight, bias, before, held, seen, seen_too, bits, sums, total
 ):
     step = pl.program_id(0)
-    model_ll = before[...] + likelihood(lat, spikes, weight, bias)
-    heldout = (1 - held[...]).astype(F32)
-    count = seen[...] + seen_too[...]
-    null_ll = count * jnp.log((count + 1.0) / frames) - (count + 1.0)
-    gained = heldout * (model_ll - null_ll)
-    bits[...] = gained / (math.log(2.0) * (count + 1.0))
-    lane = lax.broadcasted_iota(jnp.int32, (1, 128), 1)
-    gain_sum = jnp.sum(gained, 1, keepdims=True)
-    spike_sum = jnp.sum(heldout * count, 1, keepdims=True)
-    here = jnp.where(lane == 0, gain_sum, jnp.where(lane == 1, spike_sum, 0.0))
-
-    @pl.when(step == 0)
-    def _():
-        total[...] = here
-
-    @pl.when(step > 0)
-    def _():
-        total[...] += here
+    width = spikes.shape[1]
+    found = likelihood(lat, spikes, weight, bias)
+    for j in range(total.shape[1] // width):
+
+        @pl.when(step == j)
+        def _():
+            total[:, width * j : width * (j + 1)] = found
 
     @pl.when(step == pl.num_programs(0) - 1)
     def _():
-        sums[...] = jnp.broadcast_to(total[...][None], sums.shape)
+        heldout = (1 - held[...]).astype(F32)
+        count = seen[...] + seen_too[...]
+        null_ll = count * jnp.log((count + 1.0) / frames) - (count + 1.0)
+        gained = heldout * (before[...] + total[...] - null_ll)
+        bits[...] = gained / (math.log(2.0) * (count + 1.0))
+        lane = lax.broadcasted_iota(jnp.int32, (1, 128), 1)
+        gain_sum = jnp.sum(gained, 1, keepdims=True)
+        spike_sum = jnp.sum(heldout * count, 1, keepdims=True)
+        here = jnp.where(lane == 0, gain_sum, jnp.where(lane == 1, spike_sum, 0.0))
+        sums[...] = jnp.broadcast_to(here[None], sums.shape)
+
+
+def total_kernel(sums_ref, out_ref):
+    totals = jnp.sum(sums_ref[...], 0)
+    out_ref[...] = totals[:, 0:1] / (math.log(2.0) * (1.0 + totals[:, 1:2]))
 
 
 def readout(which_half, lat, spikes, weight, bias, scoring=(), copies=256):
     frames, neurons = spikes.shape
     rows, dim = lat.shape
-    width = neurons // 4
+    width = neurons // 2
     row = pl.BlockSpec((1, width), lambda j, at: (0, j))
     out_shape, out_specs = [jax.ShapeDtypeStruct((1, neurons), F32)], [row]
     body, scratch = readout_kernel, []
     if scoring:
         body = functools.partial(score_kernel, float(frames))
         out_shape.append(jax.ShapeDtypeStruct((copies, 1, 128), F32))
-        out_specs.append(pl.BlockSpec((copies, 1, 128), lambda j, at: (0, 0, 0)))
-        scratch = [pltpu.VMEM((1, 128), F32)]
+        out_specs = [
+            pl.BlockSpec((1, neurons), lambda j, at: (0, 0)),
+            pl.BlockSpec((copies, 1, 128), lambda j, at: (0, 0, 0)),
+        ]
+        scratch = [pltpu.VMEM((1, neurons), F32)]
     return pl.pallas_call(
         body,
         out_shape=out_shape,
@@ -284,7 +290,8 @@
                 pl.BlockSpec((rows, width), lambda j, at: (at[0], j)),
                 pl.BlockSpec((width, dim), lambda j, at: (j, 0)),
             ]
-            + [row] * (1 + len(scoring)),
+            + [row]
+            + [pl.BlockSpec((1, neurons), lambda j, at: (0, 0))] * len(scoring),
             out_specs=out_specs,
             scratch_shapes=scratch,
         ),
@@ -319,7 +326,7 @@
     core = lax.axis_index("c")
     held_row = held_in[None, :]
 
-    given, counts_far = readin(spikes, held_row, readin_weight, 1 - core, BF16)
+    given, counts_far = readin(spikes, held_row, in_hbm(readin_weight), 1 - core, BF16)
     theirs = other_core(given)
     own, counts_near = readin(spikes, held_row, readin_weight, core, F32)
     chip_sum = (own + theirs.astype(F32)).astype(BF16)
@@ -357,8 +364,7 @@
     (ll_near,) = readout(core, lat_near, spikes, readout_weight, bias_row)
     scoring = (ll_near, held_row, counts_near, counts_far)
     bits, sums = readout(1 - core, lat_far, spikes, readout_weight, bias_row, scoring)
-    totals = jnp.sum(exchange(sums, ALL), (0, 1))
-    bits_total = totals[0] / (math.log(2.0) * (1.0 + totals[1]))
+    (bits_total,) = small(total_kernel, "total", [((1, 1), F32)], exchange(sums, ALL))
 
     out_start = lax.axis_index(ROWS) * rows_here
     out_row = lax.rem(out_start, half)
@@ -367,7 +373,7 @@
         lax.dynamic_slice_in_dim(lat_near, out_row, rows_here, 0),
         lax.dynamic_slice_in_dim(lat_far, out_row, rows_here, 0),
     )
-    return (latents, bits[0], bits_total)
+    return (latents, bits[0], bits_total[0, 0])
 
 
 def solution(mesh):

time: 160 us -> 156 us (0.975)
  between operations: 3.25 us -> 0.84 us
where the time goes in v7:
time: 156 us; the launch traced here: 155 us
  blocking collectives  93.9 us (60%)
  starting transfers between devices  22.3 us (14%)
  waiting for transfers between devices  19.5 us (12%)
  Pallas kernels  16.8 us (11%)
  other arithmetic  1.88 us (1%)
    all_to_all x6, blocking collectives, exchange(): return lax.all_to_all(blocks, axes, 0, 0, tiled=True)  93.9 us
    all_to_all x2, waiting for transfers between devices, exchange(): return lax.all_to_all(blocks, axes, 0, 0, tiled=True)  16.7 us
    ppermute x3, starting transfers between devices, other_core(): return lax.ppermute(block, 'c', [(0, 1), (1, 0)])  12 us
    all_to_all x2, starting transfers between devices, exchange(): return lax.all_to_all(blocks, axes, 0, 0, tiled=True)  8.58 us
    pallas_call x2, Pallas kernels, readout(): pl.pallas_call(body, out_shape=out_shape, grid_spec=pltpu.PrefetchScalarG...  7.19 us
    pallas_call x2, Pallas kernels, readin(): pl.pallas_call(readin_kernel, out_shape=(jax.ShapeDtypeStruct((frames //...  6.31 us
  transfers between devices with their start and end apart: 6, of which 4 were waited for; matrix products, arithmetic and copies ran while one was open for 1% of the time, Pallas kernels for 4%

profile of v7, /device:TPU:1, one launch (start us, length us, event | category | flops | bytes accessed | tf_op | source)
XLA Modules:
  0.0 155.4 jit_solution(2134967917288454144)
XLA Ops:
  0.6 0.0 copy-start.1
  0.6 3.6 %readin.3 = (bf16[512,1024]{1,0:T(8,128)(2,1)S(1)}, f32[1,1024]{1,0:T(1,128)S(1)}) custom-call(s32[1]{0:T(128)} %bitcast.3.at_ref, s32[1024,1024]{1,0:T(8,128)} %spikes.3, s32[1,1024]{1,0:T(1,128)} %bitcast.20, bf16[1024,1024]{1,0:T(8,128)(2,1)} %weight_ref.3), custom_call_target="tpu_custom_call" | custom-call | flops 1073741824 | bytes 5242880 | tf_op jit(solution)/shard_map/readin/pallas_call | solution.py:83
  4.2 3.3 %collective-permute-start = (bf16[512,1024]{1,0:T(8,128)(2,1)S(1)}, bf16[512,1024]{1,0:T(8,128)(2,1)S(1)}, u32[]{:S(2)}, u32[]{:S(2)}) collective-permute-start(bf16[512,1024]{1,0:T(8,128)(2,1)S(1)} %get-tuple-element.15), channel_id=1, source_target_pairs={{0,8},{8,0},{1,9},{9,1},{2,10},{10,2},{3,11},{11,3},{4,12},{12,4},... | collective-permute-start | bytes 3145736 | tf_op jit(solution)/shard_map/ppermute | solution.py:35
  7.6 0.0 copy-done.1
  7.6 2.7 %readin.2 = (f32[512,1024]{1,0:T(8,128)S(1)}, f32[1,1024]{1,0:T(1,128)S(1)}) custom-call(s32[1]{0:T(128)} %bitcast.1.at_ref, s32[1024,1024]{1,0:T(8,128)} %spikes.3, s32[1,1024]{1,0:T(1,128)} %bitcast.21, bf16[1024,1024]{1,0:T(8,128)(2,1)S(1)} %copy-done.1), custom_call_target="tpu_custom_call" | custom-call | flops 1073741824 | bytes 5242880 | tf_op jit(solution)/shard_map/readin/pallas_call | solution.py:83
  10.3 0.0 collective-permute-done
  10.3 0.4 add_convert_fusion
  10.7 0.0 copy-start.5
  10.7 0.0 copy-start.9
  10.7 21.7 %all_to_all.40.parts_ref = bf16[16,32,1024]{2,1,0:T(8,128)(2,1)S(1)} all-to-all(bf16[16,32,1024]{2,1,0:T(8,128)(2,1)S(1)} %bitcast.28), channel_id=1, replica_groups=mesh['y'=4,'zh'=4,'c'=2,'x'=4,'zl'=2] {'y','x'}, dimensions={0} | all-to-all | bytes 2097152 | tf_op jit(solution)/shard_map/all_to_all | solution.py:27
  32.4 0.1 plane.1.mine_ref
  32.5 1.7 %collective-permute-start.1 = (bf16[32,1024]{1,0:T(8,128)(2,1)S(1)}, bf16[32,1024]{1,0:T(8,128)(2,1)S(1)}, u32[]{:S(2)}, u32[]{:S(2)}) collective-permute-start(bf16[32,1024]{1,0:T(8,128)(2,1)S(1)} %plane.1.mine_ref), channel_id=1, source_target_pairs={{0,1},{1,0},{2,3},{3,2},{4,5},{5,4},{6,7},{7,6},{8,9},{9,8},{10,11... | collective-permute-start | bytes 196616 | tf_op jit(solution)/shard_map/ppermute | solution.py:39
  34.3 1.7 %collective-permute-done.1.other_ref = bf16[32,1024]{1,0:T(8,128)(2,1)S(1)} collective-permute-done((bf16[32,1024]{1,0:T(8,128)(2,1)S(1)}, bf16[32,1024]{1,0:T(8,128)(2,1)S(1)}, u32[]{:S(2)}, u32[]{:S(2)}) %collective-permute-start.1) | collective-permute-done | bytes 65568 | tf_op jit(solution)/shard_map/ppermute | solution.py:39
  35.9 21.1 %all_to_all.41.parts_ref = bf16[16,8,1024]{2,1,0:T(8,128)(2,1)S(1)} all-to-all(bf16[16,8,1024]{2,1,0:T(8,128)(2,1)S(1)} %pair.1), channel_id=1, replica_groups=mesh['y'=4,'zh'=4,'c'=2,'x'=4,'zl'=2] {'x','zh'}, dimensions={0} | all-to-all | bytes 524288 | tf_op jit(solution)/shard_map/all_to_all | solution.py:27
  57.1 0.0 copy-done.5
  57.1 0.0 copy-done.9
  57.1 0.4 project.1
  57.4 13.3 %all_to_all.42 = bf16[16,32,256]{2,1,0:T(8,128)(2,1)S(1)} all-to-all(bf16[16,32,256]{2,1,0:T(8,128)(2,1)S(1)} %get-tuple-element.17), channel_id=1, replica_groups=mesh['y'=4,'zh'=4,'c'=2,'x'=4,'zl'=2] {'y','zh'}, dimensions={0} | all-to-all | bytes 524288 | tf_op jit(solution)/shard_map/all_to_all | solution.py:27
  70.7 3.9 %collective-permute-start.2 = (bf16[512,256]{1,0:T(8,128)(2,1)S(1)}, bf16[512,256]{1,0:T(8,128)(2,1)S(1)}, u32[]{:S(2)}, u32[]{:S(2)}) collective-permute-start(bf16[512,256]{1,0:T(8,128)(2,1)S(1)} %bitcast.17), channel_id=1, source_target_pairs={{0,8},{8,0},{1,9},{9,1},{2,10},{10,2},{3,11},{11,3},{4,12},{12,4},... | collective-permute-start | bytes 786440 | tf_op jit(solution)/shard_map/ppermute | solution.py:35
  74.6 1.2 collective-permute-done.2.far_ref
  75.8 0.0 copy-done.6
  75.8 0.5 attend.1
  76.3 0.0 copy-start.11
  76.3 12.2 %all_to_all.43.parts_ref = bf16[8,32,1024]{2,1,0:T(8,128)(2,1)S(1)} all-to-all(bf16[8,32,1024]{2,1,0:T(8,128)(2,1)S(1)} %attend.1), channel_id=1, replica_groups=mesh['y'=4,'zh'=4,'c'=2,'x'=4,'zl'=2] {'x','zl'}, dimensions={0} | all-to-all | bytes 1048576 | tf_op jit(solution)/shard_map/all_to_all | solution.py:27
  88.5 0.0 copy-done.3
  88.5 0.0 copy-done.4
  88.5 0.0 copy-done.10
  88.5 1.3 mlp.1
  89.8 3.5 %all-to-all-start.4 = ((bf16[8,4,1024]{2,1,0:T(4,128)(2,1)}), bf16[8,4,1024]{2,1,0:T(4,128)(2,1)S(1)}, u32[]{:S(2)}, u32[]{:S(2)}) async-start(bf16[8,4,1024]{2,1,0:T(4,128)(2,1)} %get-tuple-element.19), calls=%async_computation.4 | async-start | bytes 131072 | tf_op jit(solution)/shard_map/all_to_all | solution.py:27
  93.3 5.1 %all-to-all-done.4.parts_ref = bf16[8,4,1024]{2,1,0:T(4,128)(2,1)S(1)} async-done(((bf16[8,4,1024]{2,1,0:T(4,128)(2,1)}), bf16[8,4,1024]{2,1,0:T(4,128)(2,1)S(1)}, u32[]{:S(2)}, u32[]{:S(2)}) %all-to-all-start.4) | async-done | bytes 65568 | tf_op jit(solution)/shard_map/all_to_all | solution.py:27
  98.5 0.0 copy-done.11
  98.5 0.1 latents.1
  98.6 9.6 %all_to_all.44 = bf16[8,4,1024]{2,1,0:T(4,128)(2,1)S(1)} all-to-all(bf16[8,4,1024]{2,1,0:T(4,128)(2,1)S(1)} %latents.1), channel_id=1, replica_groups=mesh['y'=4,'zh'=4,'c'=2,'x'=4,'zl'=2] {'zh','zl'}, dimensions={0} | all-to-all | bytes 131072 | tf_op jit(solution)/shard_map/all_to_all | solution.py:27
  108.2 0.1 broadcast_in_dim.27
  108.3 16.0 %all_to_all.45 = bf16[16,32,1024]{2,1,0:T(8,128)(2,1)S(1)} all-to-all(bf16[16,32,1024]{2,1,0:T(8,128)(2,1)S(1)} %broadcast_in_dim.27), channel_id=1, replica_groups=mesh['y'=4,'zh'=4,'c'=2,'x'=4,'zl'=2] {'y','x'}, dimensions={0} | all-to-all | bytes 2097152 | tf_op jit(solution)/shard_map/all_to_all | solution.py:27
  124.3 4.8 %collective-permute-start.3 = (bf16[512,1024]{1,0:T(8,128)(2,1)S(1)}, bf16[512,1024]{1,0:T(8,128)(2,1)S(1)}, u32[]{:S(2)}, u32[]{:S(2)}) collective-permute-start(bf16[512,1024]{1,0:T(8,128)(2,1)S(1)} %bitcast.14), channel_id=1, source_target_pairs={{0,8},{8,0},{1,9},{9,1},{2,10},{10,2},{3,11},{11,3},{4,12},{12,4},... | collective-permute-start | bytes 3145736 | tf_op jit(solution)/shard_map/ppermute | solution.py:35
  129.1 0.0 copy-done
  129.1 0.0 copy-done.8
  129.1 3.0 %readout.1.before = f32[1,1024]{1,0:T(1,128)S(1)} custom-call(s32[1]{0:T(128)} %bitcast.1.at_ref, bf16[512,1024]{1,0:T(8,128)(2,1)S(1)} %bitcast.15, s32[1024,1024]{1,0:T(8,128)} %spikes.3, bf16[1024,1024]{1,0:T(8,128)(2,1)S(1)} %copy-done, f32[1,1024]{1,0:T(1,128)S(1)} %bitcast.23), custom_call_target="tpu_custom_call" | custom-call | flops 1073741824 | bytes 4194304 | tf_op jit(solution)/shard_map/readout/pallas_call | solution.py:282
  132.1 0.0 collective-permute-done.3.lat
  132.1 0.0 copy-start.2
  132.1 0.0 copy-done.7
  132.1 4.2 %score.1 = (f32[1,1024]{1,0:T(1,128)}, f32[256,1,128]{2,1,0:T(1,128)}) custom-call(s32[1]{0:T(128)} %bitcast.3.at_ref, bf16[512,1024]{1,0:T(8,128)(2,1)S(1)} %collective-permute-done.3.lat, s32[1024,1024]{1,0:T(8,128)} %spikes.3, bf16[1024,1024]{1,0:T(8,128)(2,1)S(1)} %copy-done, f32[1,1024]{1,0:T(1,128)S(1)} %bitcast.24, f32[1,1024]{1,0:T(1,128)S(1)} %readout.1.before, ...), custom_call_target="tpu_custom_call" | custom-call | flops 1073741824 | bytes 4194304 | tf_op jit(solution)/shard_map/score/pallas_call | solution.py:282
  136.3 0.0 copy-done.2
  136.3 5.1 %all-to-all-start.7 = ((f32[256,1,128]{2,1,0:T(1,128)}), f32[256,1,128]{2,1,0:T(1,128)S(1)}, u32[]{:S(2)}, u32[]{:S(2)}) async-start(f32[256,1,128]{2,1,0:T(1,128)} %get-tuple-element.24), calls=%async_computation.7 | async-start | bytes 262144 | tf_op jit(solution)/shard_map/all_to_all | solution.py:27
  141.5 1.5 dynamic-slice_select_fusion
  143.0 11.6 %all-to-all-done.7.sums_ref = f32[256,1,128]{2,1,0:T(1,128)S(1)} async-done(((f32[256,1,128]{2,1,0:T(1,128)}), f32[256,1,128]{2,1,0:T(1,128)S(1)}, u32[]{:S(2)}, u32[]{:S(2)}) %all-to-all-start.7) | async-done | bytes 131104 | tf_op jit(solution)/shard_map/all_to_all | solution.py:27
  154.5 0.9 total.1
  (9 shorter events, 0.1 us)
Async XLA Ops:
  0.6 6.9 %copy-start.1 = (bf16[1024,1024]{1,0:T(8,128)(2,1)S(1)}, bf16[1024,1024]{1,0:T(8,128)(2,1)}, u32[]{:S(2)}) copy-start(bf16[1024,1024]{1,0:T(8,128)(2,1)} %weight_ref.3) | copy-start | bytes 6291460
  4.2 6.1 %collective-permute-start = (bf16[512,1024]{1,0:T(8,128)(2,1)S(1)}, bf16[512,1024]{1,0:T(8,128)(2,1)S(1)}, u32[]{:S(2)}, u32[]{:S(2)}) collective-permute-start(bf16[512,1024]{1,0:T(8,128)(2,1)S(1)} %get-tuple-element.15), channel_id=1, source_target_pairs={{0,8},{8,0},{1,9},{9,1},{2,10},{10,2},{3,11},{11,3},{4,12},{12,4},... | collective-permute-start | bytes 3145736 | tf_op jit(solution)/shard_map/ppermute | solution.py:35
  10.7 46.4 %copy-start.5 = (bf16[1024,3,128]{2,0,1:T(8,128)(2,1)S(1)}, bf16[1024,3,128]{2,0,1:T(8,128)(2,1)}, u32[]{:S(2)}) copy-start(bf16[1024,3,128]{2,0,1:T(8,128)(2,1)} %param.15) | copy-start | bytes 2359300
  10.7 46.3 %copy-start.9 = (f32[1024]{0:T(1024)S(1)}, f32[1024]{0:T(1024)}, u32[]{:S(2)}) copy-start(f32[1024]{0:T(1024)} %param.19) | copy-start | bytes 12292
  32.4 43.4 %copy-start.6 = (bf16[128,1024]{1,0:T(8,128)(2,1)S(1)}, bf16[128,1024]{1,0:T(8,128)(2,1)}, u32[]{:S(2)}) copy-start(bf16[128,1024]{1,0:T(8,128)(2,1)} %mix_ref.1) | copy-start | bytes 786436
  32.5 3.4 %collective-permute-start.1 = (bf16[32,1024]{1,0:T(8,128)(2,1)S(1)}, bf16[32,1024]{1,0:T(8,128)(2,1)S(1)}, u32[]{:S(2)}, u32[]{:S(2)}) collective-permute-start(bf16[32,1024]{1,0:T(8,128)(2,1)S(1)} %plane.1.mine_ref), channel_id=1, source_target_pairs={{0,1},{1,0},{2,3},{3,2},{4,5},{5,4},{6,7},{7,6},{8,9},{9,8},{10,11... | collective-permute-start | bytes 196616 | tf_op jit(solution)/shard_map/ppermute | solution.py:39
  57.0 31.5 %copy-start.3 = (bf16[1024,512]{1,0:T(8,128)(2,1)S(1)}, bf16[1024,512]{1,0:T(8,128)(2,1)}, u32[]{:S(2)}) copy-start(bf16[1024,512]{1,0:T(8,128)(2,1)} %up_ref.1) | copy-start | bytes 3145732
  57.1 31.5 %copy-start.4 = (bf16[512,1024]{1,0:T(8,128)(2,1)S(1)}, bf16[512,1024]{1,0:T(8,128)(2,1)}, u32[]{:S(2)}) copy-start(bf16[512,1024]{1,0:T(8,128)(2,1)} %down_ref.1) | copy-start | bytes 3145732
  57.1 31.5 %copy-start.10 = (f32[1024]{0:T(1024)S(1)}, f32[1024]{0:T(1024)}, u32[]{:S(2)}) copy-start(f32[1024]{0:T(1024)} %param.20) | copy-start | bytes 12292
  70.7 5.0 %collective-permute-start.2 = (bf16[512,256]{1,0:T(8,128)(2,1)S(1)}, bf16[512,256]{1,0:T(8,128)(2,1)S(1)}, u32[]{:S(2)}, u32[]{:S(2)}) collective-permute-start(bf16[512,256]{1,0:T(8,128)(2,1)S(1)} %bitcast.17), channel_id=1, source_target_pairs={{0,8},{8,0},{1,9},{9,1},{2,10},{10,2},{3,11},{11,3},{4,12},{12,4},... | collective-permute-start | bytes 786440 | tf_op jit(solution)/shard_map/ppermute | solution.py:35
  76.3 22.2 %copy-start.11 = (f32[1024]{0:T(1024)S(1)}, f32[1024]{0:T(1024)}, u32[]{:S(2)}) copy-start(f32[1024]{0:T(1024)} %param.21) | copy-start | bytes 12292
  89.8 39.3 %copy-start = (bf16[1024,1024]{1,0:T(8,128)(2,1)S(1)}, bf16[1024,1024]{1,0:T(8,128)(2,1)}, u32[]{:S(2)}) copy-start(bf16[1024,1024]{1,0:T(8,128)(2,1)} %weight.3) | copy-start | bytes 6291460
  89.8 39.3 %copy-start.8 = (f32[1024]{0:T(1024)S(1)}, f32[1024]{0:T(1024)}, u32[]{:S(2)}) copy-start(f32[1024]{0:T(1024)} %param.23) | copy-start | bytes 12292
  89.8 8.6 %all-to-all-start.4 = ((bf16[8,4,1024]{2,1,0:T(4,128)(2,1)}), bf16[8,4,1024]{2,1,0:T(4,128)(2,1)S(1)}, u32[]{:S(2)}, u32[]{:S(2)}) async-start(bf16[8,4,1024]{2,1,0:T(4,128)(2,1)} %get-tuple-element.19), calls=%async_computation.4 | async-start | bytes 131072 | tf_op jit(solution)/shard_map/all_to_all | solution.py:27
  124.3 7.8 %collective-permute-start.3 = (bf16[512,1024]{1,0:T(8,128)(2,1)S(1)}, bf16[512,1024]{1,0:T(8,128)(2,1)S(1)}, u32[]{:S(2)}, u32[]{:S(2)}) collective-permute-start(bf16[512,1024]{1,0:T(8,128)(2,1)S(1)} %bitcast.14), channel_id=1, source_target_pairs={{0,8},{8,0},{1,9},{9,1},{2,10},{10,2},{3,11},{11,3},{4,12},{12,4},... | collective-permute-start | bytes 3145736 | tf_op jit(solution)/shard_map/ppermute | solution.py:35
  129.1 3.0 %copy-start.7 = (s32[1024]{0:T(1024)S(1)}, s32[1024]{0:T(1024)}, u32[]{:S(2)}) copy-start(s32[1024]{0:T(1024)} %param.13) | copy-start | bytes 12292
  132.1 4.2 %copy-start.2 = (bf16[512,1024]{1,0:T(8,128)(2,1)}, bf16[512,1024]{1,0:T(8,128)(2,1)S(1)}, u32[]{:S(2)}) copy-start(bf16[512,1024]{1,0:T(8,128)(2,1)S(1)} %collective-permute-done.3.lat) | copy-start | bytes 3145732
  136.3 18.2 %all-to-all-start.7 = ((f32[256,1,128]{2,1,0:T(1,128)}), f32[256,1,128]{2,1,0:T(1,128)S(1)}, u32[]{:S(2)}, u32[]{:S(2)}) async-start(f32[256,1,128]{2,1,0:T(1,128)} %get-tuple-element.24), calls=%async_computation.7 | async-start | bytes 262144 | tf_op jit(solution)/shard_map/all_to_all | solution.py:27

commit v8 on v7

--- a/solution.py
+++ b/solution.py
@@ -62,10 +62,10 @@
 
 
 def readin_kernel(at_ref, spikes_ref, held_ref, weight_ref, out_ref, counts_ref):
-    block = spikes_ref[...]
-    masked = (block * held_ref[...]).astype(F32).astype(BF16)
+    block = spikes_ref[...].astype(F32)
+    masked = (block * held_ref[...].astype(F32)).astype(BF16)
     out_ref[...] = matmul(masked, weight_ref[...]).astype(out_ref.dtype)
-    counted = jnp.sum(block.astype(F32), 0, keepdims=True)
+    counted = jnp.sum(block, 0, keepdims=True)
 
     @pl.when(pl.program_id(0) == 0)
     def _():
@@ -302,7 +302,7 @@
             transcendentals=rows * neurons,
         ),
         name="score" if scoring else "readout",
-    )(which_half.reshape(1), lat, in_hbm(spikes), weight, bias, *scoring)
+    )(which_half.reshape(1), lat, spikes if scoring else in_hbm(spikes), weight, bias, *scoring)
 
 
 def on_device(

time: 156 us -> 154 us (0.987)
  no operation moved by 1% of the time
where the time goes in v8:
time: 154 us
  blocking collectives  93.5 us (61%)
  starting transfers between devices  22.4 us (15%)
  waiting for transfers between devices  19.4 us (13%)
  Pallas kernels  15.5 us (10%)
  other arithmetic  1.88 us (1%)
    all_to_all x6, blocking collectives, exchange(): return lax.all_to_all(blocks, axes, 0, 0, tiled=True)  93.5 us
    all_to_all x2, waiting for transfers between devices, exchange(): return lax.all_to_all(blocks, axes, 0, 0, tiled=True)  16.6 us
    ppermute x3, starting transfers between devices, other_core(): return lax.ppermute(block, 'c', [(0, 1), (1, 0)])  12 us
    all_to_all x2, starting transfers between devices, exchange(): return lax.all_to_all(blocks, axes, 0, 0, tiled=True)  8.6 us
    pallas_call x2, Pallas kernels, readin(): pl.pallas_call(readin_kernel, out_shape=(jax.ShapeDtypeStruct((frames //...  6.3 us
    pallas_call x2, Pallas kernels, readout(): pl.pallas_call(body, out_shape=out_shape, grid_spec=pltpu.PrefetchScalarG...  5.88 us
  transfers between devices with their start and end apart: 6, of which 4 were waited for; matrix products, arithmetic and copies ran while one was open for 1% of the time, Pallas kernels for 4%

profile of v8, /device:TPU:1, one launch (start us, length us, event | category | flops | bytes accessed | tf_op | source)
XLA Modules:
  0.0 153.7 jit_solution(15255927876103879007)
XLA Ops:
  0.6 0.0 copy-start.2
  0.6 3.6 %readin.3 = (bf16[512,1024]{1,0:T(8,128)(2,1)S(1)}, f32[1,1024]{1,0:T(1,128)S(1)}) custom-call(s32[1]{0:T(128)} %bitcast.3.at_ref, s32[1024,1024]{1,0:T(8,128)} %spikes.3, s32[1,1024]{1,0:T(1,128)} %bitcast.20, bf16[1024,1024]{1,0:T(8,128)(2,1)} %weight_ref.3), custom_call_target="tpu_custom_call" | custom-call | flops 1073741824 | bytes 5242880 | tf_op jit(solution)/shard_map/readin/pallas_call | solution.py:83
  4.2 3.3 %collective-permute-start = (bf16[512,1024]{1,0:T(8,128)(2,1)S(1)}, bf16[512,1024]{1,0:T(8,128)(2,1)S(1)}, u32[]{:S(2)}, u32[]{:S(2)}) collective-permute-start(bf16[512,1024]{1,0:T(8,128)(2,1)S(1)} %get-tuple-element.15), channel_id=1, source_target_pairs={{0,8},{8,0},{1,9},{9,1},{2,10},{10,2},{3,11},{11,3},{4,12},{12,4},... | collective-permute-start | bytes 3145736 | tf_op jit(solution)/shard_map/ppermute | solution.py:35
  7.6 0.0 copy-done.2
  7.6 2.7 %readin.2 = (f32[512,1024]{1,0:T(8,128)S(1)}, f32[1,1024]{1,0:T(1,128)S(1)}) custom-call(s32[1]{0:T(128)} %bitcast.1.at_ref, s32[1024,1024]{1,0:T(8,128)} %spikes.3, s32[1,1024]{1,0:T(1,128)} %bitcast.21, bf16[1024,1024]{1,0:T(8,128)(2,1)S(1)} %copy-done.2), custom_call_target="tpu_custom_call" | custom-call | flops 1073741824 | bytes 5242880 | tf_op jit(solution)/shard_map/readin/pallas_call | solution.py:83
  10.3 0.0 collective-permute-done
  10.3 0.4 add_convert_fusion
  10.7 0.0 copy-start.6
  10.7 0.0 copy-start.10
  10.7 21.7 %all_to_all.40.parts_ref = bf16[16,32,1024]{2,1,0:T(8,128)(2,1)S(1)} all-to-all(bf16[16,32,1024]{2,1,0:T(8,128)(2,1)S(1)} %bitcast.28), channel_id=1, replica_groups=mesh['y'=4,'zh'=4,'c'=2,'x'=4,'zl'=2] {'y','x'}, dimensions={0} | all-to-all | bytes 2097152 | tf_op jit(solution)/shard_map/all_to_all | solution.py:27
  32.4 0.1 plane.1.mine_ref
  32.5 1.7 %collective-permute-start.1 = (bf16[32,1024]{1,0:T(8,128)(2,1)S(1)}, bf16[32,1024]{1,0:T(8,128)(2,1)S(1)}, u32[]{:S(2)}, u32[]{:S(2)}) collective-permute-start(bf16[32,1024]{1,0:T(8,128)(2,1)S(1)} %plane.1.mine_ref), channel_id=1, source_target_pairs={{0,1},{1,0},{2,3},{3,2},{4,5},{5,4},{6,7},{7,6},{8,9},{9,8},{10,11... | collective-permute-start | bytes 196616 | tf_op jit(solution)/shard_map/ppermute | solution.py:39
  34.3 1.7 %collective-permute-done.1.other_ref = bf16[32,1024]{1,0:T(8,128)(2,1)S(1)} collective-permute-done((bf16[32,1024]{1,0:T(8,128)(2,1)S(1)}, bf16[32,1024]{1,0:T(8,128)(2,1)S(1)}, u32[]{:S(2)}, u32[]{:S(2)}) %collective-permute-start.1) | collective-permute-done | bytes 65568 | tf_op jit(solution)/shard_map/ppermute | solution.py:39
  36.0 21.1 %all_to_all.41.parts_ref = bf16[16,8,1024]{2,1,0:T(8,128)(2,1)S(1)} all-to-all(bf16[16,8,1024]{2,1,0:T(8,128)(2,1)S(1)} %pair.1), channel_id=1, replica_groups=mesh['y'=4,'zh'=4,'c'=2,'x'=4,'zl'=2] {'x','zh'}, dimensions={0} | all-to-all | bytes 524288 | tf_op jit(solution)/shard_map/all_to_all | solution.py:27
  57.1 0.0 copy-done.6
  57.1 0.0 copy-done.10
  57.1 0.4 project.1
  57.4 13.3 %all_to_all.42 = bf16[16,32,256]{2,1,0:T(8,128)(2,1)S(1)} all-to-all(bf16[16,32,256]{2,1,0:T(8,128)(2,1)S(1)} %get-tuple-element.17), channel_id=1, replica_groups=mesh['y'=4,'zh'=4,'c'=2,'x'=4,'zl'=2] {'y','zh'}, dimensions={0} | all-to-all | bytes 524288 | tf_op jit(solution)/shard_map/all_to_all | solution.py:27
  70.8 3.8 %collective-permute-start.2 = (bf16[512,256]{1,0:T(8,128)(2,1)S(1)}, bf16[512,256]{1,0:T(8,128)(2,1)S(1)}, u32[]{:S(2)}, u32[]{:S(2)}) collective-permute-start(bf16[512,256]{1,0:T(8,128)(2,1)S(1)} %bitcast.17), channel_id=1, source_target_pairs={{0,8},{8,0},{1,9},{9,1},{2,10},{10,2},{3,11},{11,3},{4,12},{12,4},... | collective-permute-start | bytes 786440 | tf_op jit(solution)/shard_map/ppermute | solution.py:35
  74.6 1.2 collective-permute-done.2.far_ref
  75.8 0.0 copy-done.7
  75.8 0.5 attend.1
  76.3 0.0 copy-start.12
  76.3 11.8 %all_to_all.43.parts_ref = bf16[8,32,1024]{2,1,0:T(8,128)(2,1)S(1)} all-to-all(bf16[8,32,1024]{2,1,0:T(8,128)(2,1)S(1)} %attend.1), channel_id=1, replica_groups=mesh['y'=4,'zh'=4,'c'=2,'x'=4,'zl'=2] {'x','zl'}, dimensions={0} | all-to-all | bytes 1048576 | tf_op jit(solution)/shard_map/all_to_all | solution.py:27
  88.1 0.0 copy-done.4
  88.1 0.0 copy-done.5
  88.1 0.0 copy-done.11
  88.1 1.3 mlp.1
  89.4 3.5 %all-to-all-start.4 = ((bf16[8,4,1024]{2,1,0:T(4,128)(2,1)}), bf16[8,4,1024]{2,1,0:T(4,128)(2,1)S(1)}, u32[]{:S(2)}, u32[]{:S(2)}) async-start(bf16[8,4,1024]{2,1,0:T(4,128)(2,1)} %get-tuple-element.19), calls=%async_computation.4 | async-start | bytes 131072 | tf_op jit(solution)/shard_map/all_to_all | solution.py:27
  92.9 5.1 %all-to-all-done.4.parts_ref = bf16[8,4,1024]{2,1,0:T(4,128)(2,1)S(1)} async-done(((bf16[8,4,1024]{2,1,0:T(4,128)(2,1)}), bf16[8,4,1024]{2,1,0:T(4,128)(2,1)S(1)}, u32[]{:S(2)}, u32[]{:S(2)}) %all-to-all-start.4) | async-done | bytes 65568 | tf_op jit(solution)/shard_map/all_to_all | solution.py:27
  98.0 0.0 copy-done.12
  98.0 0.1 latents.1
  98.1 9.7 %all_to_all.44 = bf16[8,4,1024]{2,1,0:T(4,128)(2,1)S(1)} all-to-all(bf16[8,4,1024]{2,1,0:T(4,128)(2,1)S(1)} %latents.1), channel_id=1, replica_groups=mesh['y'=4,'zh'=4,'c'=2,'x'=4,'zl'=2] {'zh','zl'}, dimensions={0} | all-to-all | bytes 131072 | tf_op jit(solution)/shard_map/all_to_all | solution.py:27
  107.8 0.1 broadcast_in_dim.27
  107.9 15.9 %all_to_all.45 = bf16[16,32,1024]{2,1,0:T(8,128)(2,1)S(1)} all-to-all(bf16[16,32,1024]{2,1,0:T(8,128)(2,1)S(1)} %broadcast_in_dim.27), channel_id=1, replica_groups=mesh['y'=4,'zh'=4,'c'=2,'x'=4,'zl'=2] {'y','x'}, dimensions={0} | all-to-all | bytes 2097152 | tf_op jit(solution)/shard_map/all_to_all | solution.py:27
  123.9 4.9 %collective-permute-start.3 = (bf16[512,1024]{1,0:T(8,128)(2,1)S(1)}, bf16[512,1024]{1,0:T(8,128)(2,1)S(1)}, u32[]{:S(2)}, u32[]{:S(2)}) collective-permute-start(bf16[512,1024]{1,0:T(8,128)(2,1)S(1)} %bitcast.14), channel_id=1, source_target_pairs={{0,8},{8,0},{1,9},{9,1},{2,10},{10,2},{3,11},{11,3},{4,12},{12,4},... | collective-permute-start | bytes 3145736 | tf_op jit(solution)/shard_map/ppermute | solution.py:35
  128.8 0.0 copy-done.1
  128.8 0.0 copy-done.9
  128.8 3.1 %readout.1.before = f32[1,1024]{1,0:T(1,128)S(1)} custom-call(s32[1]{0:T(128)} %bitcast.1.at_ref, bf16[512,1024]{1,0:T(8,128)(2,1)S(1)} %bitcast.15, s32[1024,1024]{1,0:T(8,128)} %spikes.3, bf16[1024,1024]{1,0:T(8,128)(2,1)S(1)} %copy-done.1, f32[1,1024]{1,0:T(1,128)S(1)} %bitcast.23), custom_call_target="tpu_custom_call" | custom-call | flops 1073741824 | bytes 4194304 | tf_op jit(solution)/shard_map/readout/pallas_call | solution.py:282
  131.9 0.0 collective-permute-done.3.lat
  131.9 0.0 copy-start.3
  132.0 0.0 copy-done
  132.0 0.0 copy-done.8
  132.0 2.7 %score.1 = (f32[1,1024]{1,0:T(1,128)}, f32[256,1,128]{2,1,0:T(1,128)}) custom-call(s32[1]{0:T(128)} %bitcast.3.at_ref, bf16[512,1024]{1,0:T(8,128)(2,1)S(1)} %collective-permute-done.3.lat, s32[1024,1024]{1,0:T(8,128)S(1)} %copy-done, bf16[1024,1024]{1,0:T(8,128)(2,1)S(1)} %copy-done.1, f32[1,1024]{1,0:T(1,128)S(1)} %bitcast.24, ...), custom_call_target="tpu_custom_call" | custom-call | flops 1073741824 | bytes 4194304 | tf_op jit(solution)/shard_map/score/pallas_call | solution.py:282
  134.7 5.1 %all-to-all-start.7 = ((f32[256,1,128]{2,1,0:T(1,128)}), f32[256,1,128]{2,1,0:T(1,128)S(1)}, u32[]{:S(2)}, u32[]{:S(2)}) async-start(f32[256,1,128]{2,1,0:T(1,128)} %get-tuple-element.24), calls=%async_computation.7 | async-start | bytes 262144 | tf_op jit(solution)/shard_map/all_to_all | solution.py:27
  139.9 1.5 dynamic-slice_select_fusion
  141.4 11.5 %all-to-all-done.7.sums_ref = f32[256,1,128]{2,1,0:T(1,128)S(1)} async-done(((f32[256,1,128]{2,1,0:T(1,128)}), f32[256,1,128]{2,1,0:T(1,128)S(1)}, u32[]{:S(2)}, u32[]{:S(2)}) %all-to-all-start.7) | async-done | bytes 131104 | tf_op jit(solution)/shard_map/all_to_all | solution.py:27
  152.8 0.9 total.1
  (11 shorter events, 0.1 us)
Async XLA Ops:
  0.6 6.9 %copy-start.2 = (bf16[1024,1024]{1,0:T(8,128)(2,1)S(1)}, bf16[1024,1024]{1,0:T(8,128)(2,1)}, u32[]{:S(2)}) copy-start(bf16[1024,1024]{1,0:T(8,128)(2,1)} %weight_ref.3) | copy-start | bytes 6291460
  4.2 6.1 %collective-permute-start = (bf16[512,1024]{1,0:T(8,128)(2,1)S(1)}, bf16[512,1024]{1,0:T(8,128)(2,1)S(1)}, u32[]{:S(2)}, u32[]{:S(2)}) collective-permute-start(bf16[512,1024]{1,0:T(8,128)(2,1)S(1)} %get-tuple-element.15), channel_id=1, source_target_pairs={{0,8},{8,0},{1,9},{9,1},{2,10},{10,2},{3,11},{11,3},{4,12},{12,4},... | collective-permute-start | bytes 3145736 | tf_op jit(solution)/shard_map/ppermute | solution.py:35
  10.7 46.4 %copy-start.6 = (bf16[1024,3,128]{2,0,1:T(8,128)(2,1)S(1)}, bf16[1024,3,128]{2,0,1:T(8,128)(2,1)}, u32[]{:S(2)}) copy-start(bf16[1024,3,128]{2,0,1:T(8,128)(2,1)} %param.15) | copy-start | bytes 2359300
  10.7 46.4 %copy-start.10 = (f32[1024]{0:T(1024)S(1)}, f32[1024]{0:T(1024)}, u32[]{:S(2)}) copy-start(f32[1024]{0:T(1024)} %param.19) | copy-start | bytes 12292
  32.4 43.4 %copy-start.7 = (bf16[128,1024]{1,0:T(8,128)(2,1)S(1)}, bf16[128,1024]{1,0:T(8,128)(2,1)}, u32[]{:S(2)}) copy-start(bf16[128,1024]{1,0:T(8,128)(2,1)} %mix_ref.1) | copy-start | bytes 786436
  32.5 3.4 %collective-permute-start.1 = (bf16[32,1024]{1,0:T(8,128)(2,1)S(1)}, bf16[32,1024]{1,0:T(8,128)(2,1)S(1)}, u32[]{:S(2)}, u32[]{:S(2)}) collective-permute-start(bf16[32,1024]{1,0:T(8,128)(2,1)S(1)} %plane.1.mine_ref), channel_id=1, source_target_pairs={{0,1},{1,0},{2,3},{3,2},{4,5},{5,4},{6,7},{7,6},{8,9},{9,8},{10,11... | collective-permute-start | bytes 196616 | tf_op jit(solution)/shard_map/ppermute | solution.py:39
  57.1 31.0 %copy-start.4 = (bf16[1024,512]{1,0:T(8,128)(2,1)S(1)}, bf16[1024,512]{1,0:T(8,128)(2,1)}, u32[]{:S(2)}) copy-start(bf16[1024,512]{1,0:T(8,128)(2,1)} %up_ref.1) | copy-start | bytes 3145732
  57.1 31.0 %copy-start.5 = (bf16[512,1024]{1,0:T(8,128)(2,1)S(1)}, bf16[512,1024]{1,0:T(8,128)(2,1)}, u32[]{:S(2)}) copy-start(bf16[512,1024]{1,0:T(8,128)(2,1)} %down_ref.1) | copy-start | bytes 3145732
  57.1 31.0 %copy-start.11 = (f32[1024]{0:T(1024)S(1)}, f32[1024]{0:T(1024)}, u32[]{:S(2)}) copy-start(f32[1024]{0:T(1024)} %param.20) | copy-start | bytes 12292
  70.8 5.0 %collective-permute-start.2 = (bf16[512,256]{1,0:T(8,128)(2,1)S(1)}, bf16[512,256]{1,0:T(8,128)(2,1)S(1)}, u32[]{:S(2)}, u32[]{:S(2)}) collective-permute-start(bf16[512,256]{1,0:T(8,128)(2,1)S(1)} %bitcast.17), channel_id=1, source_target_pairs={{0,8},{8,0},{1,9},{9,1},{2,10},{10,2},{3,11},{11,3},{4,12},{12,4},... | collective-permute-start | bytes 786440 | tf_op jit(solution)/shard_map/ppermute | solution.py:35
  76.3 21.7 %copy-start.12 = (f32[1024]{0:T(1024)S(1)}, f32[1024]{0:T(1024)}, u32[]{:S(2)}) copy-start(f32[1024]{0:T(1024)} %param.21) | copy-start | bytes 12292
  89.4 39.4 %copy-start.1 = (bf16[1024,1024]{1,0:T(8,128)(2,1)S(1)}, bf16[1024,1024]{1,0:T(8,128)(2,1)}, u32[]{:S(2)}) copy-start(bf16[1024,1024]{1,0:T(8,128)(2,1)} %weight.3) | copy-start | bytes 6291460
  89.4 39.4 %copy-start.9 = (f32[1024]{0:T(1024)S(1)}, f32[1024]{0:T(1024)}, u32[]{:S(2)}) copy-start(f32[1024]{0:T(1024)} %param.23) | copy-start | bytes 12292
  89.4 8.6 %all-to-all-start.4 = ((bf16[8,4,1024]{2,1,0:T(4,128)(2,1)}), bf16[8,4,1024]{2,1,0:T(4,128)(2,1)S(1)}, u32[]{:S(2)}, u32[]{:S(2)}) async-start(bf16[8,4,1024]{2,1,0:T(4,128)(2,1)} %get-tuple-element.19), calls=%async_computation.4 | async-start | bytes 131072 | tf_op jit(solution)/shard_map/all_to_all | solution.py:27
  123.9 8.1 %collective-permute-start.3 = (bf16[512,1024]{1,0:T(8,128)(2,1)S(1)}, bf16[512,1024]{1,0:T(8,128)(2,1)S(1)}, u32[]{:S(2)}, u32[]{:S(2)}) collective-permute-start(bf16[512,1024]{1,0:T(8,128)(2,1)S(1)} %bitcast.14), channel_id=1, source_target_pairs={{0,8},{8,0},{1,9},{9,1},{2,10},{10,2},{3,11},{11,3},{4,12},{12,4},... | collective-permute-start | bytes 3145736 | tf_op jit(solution)/shard_map/ppermute | solution.py:35
  128.8 3.2 %copy-start = (s32[1024,1024]{1,0:T(8,128)S(1)}, s32[1024,1024]{1,0:T(8,128)}, u32[]{:S(2)}) copy-start(s32[1024,1024]{1,0:T(8,128)} %spikes.3) | copy-start | bytes 12582916
  128.8 3.2 %copy-start.8 = (s32[1024]{0:T(1024)S(1)}, s32[1024]{0:T(1024)}, u32[]{:S(2)}) copy-start(s32[1024]{0:T(1024)} %param.13) | copy-start | bytes 12292
  131.9 2.8 %copy-start.3 = (bf16[512,1024]{1,0:T(8,128)(2,1)}, bf16[512,1024]{1,0:T(8,128)(2,1)S(1)}, u32[]{:S(2)}) copy-start(bf16[512,1024]{1,0:T(8,128)(2,1)S(1)} %collective-permute-done.3.lat) | copy-start | bytes 3145732
  134.7 18.1 %all-to-all-start.7 = ((f32[256,1,128]{2,1,0:T(1,128)}), f32[256,1,128]{2,1,0:T(1,128)S(1)}, u32[]{:S(2)}, u32[]{:S(2)}) async-start(f32[256,1,128]{2,1,0:T(1,128)} %get-tuple-element.24), calls=%async_computation.7 | async-start | bytes 262144 | tf_op jit(solution)/shard_map/all_to_all | solution.py:27

commit v9 on v8

--- a/solution.py
+++ b/solution.py
@@ -49,7 +49,7 @@
 
 def params(semantics):
     return pltpu.CompilerParams(
-        dimension_semantics=semantics, vmem_limit_bytes=40 * 1024 * 1024
+        dimension_semantics=semantics, vmem_limit_bytes=16 * 1024 * 1024
     )
 
 
@@ -61,11 +61,13 @@
     return lax.dot_general(left, right, (((1,), (1,)), ((), ())), preferred_element_type=F32)
 
 
-def readin_kernel(at_ref, spikes_ref, held_ref, weight_ref, out_ref, counts_ref):
+def readin_kernel(at_ref, spikes_ref, held_ref, weight_ref, out_ref, counts_ref, seen_ref=None):
     block = spikes_ref[...].astype(F32)
     masked = (block * held_ref[...].astype(F32)).astype(BF16)
     out_ref[...] = matmul(masked, weight_ref[...]).astype(out_ref.dtype)
     counted = jnp.sum(block, 0, keepdims=True)
+    if seen_ref is not None:
+        seen_ref[...] = block.astype(BF16)
 
     @pl.when(pl.program_id(0) == 0)
     def _():
@@ -76,16 +78,17 @@
         counts_ref[...] += counted
 
 
-def readin(spikes, held, weight, which_half, dtype):
+def readin(spikes, held, weight, which_half, dtype, keep=False):
     frames, neurons = spikes.shape
     dim = weight.shape[1]
     rows = frames // 4
     return pl.pallas_call(
         readin_kernel,
-        out_shape=(
+        out_shape=[
             jax.ShapeDtypeStruct((frames // 2, dim), dtype),
             jax.ShapeDtypeStruct((1, neurons), F32),
-        ),
+        ]
+        + [jax.ShapeDtypeStruct((frames // 2, neurons), BF16)] * keep,
         grid_spec=pltpu.PrefetchScalarGridSpec(
             num_scalar_prefetch=1,
             grid=(2,),
@@ -97,7 +100,8 @@
             out_specs=[
                 pl.BlockSpec((rows, dim), lambda i, at: (i, 0)),
                 pl.BlockSpec((1, neurons), lambda i, at: (0, 0)),
-            ],
+            ]
+            + [pl.BlockSpec((rows, neurons), lambda i, at: (i, 0))] * keep,
         ),
         compiler_params=params(("arbitrary",)),
         cost_estimate=pl.CostEstimate(
@@ -302,7 +306,7 @@
             transcendentals=rows * neurons,
         ),
         name="score" if scoring else "readout",
-    )(which_half.reshape(1), lat, spikes if scoring else in_hbm(spikes), weight, bias, *scoring)
+    )(which_half.reshape(1), lat, spikes, weight, bias, *scoring)
 
 
 def on_device(
@@ -328,7 +332,7 @@
 
     given, counts_far = readin(spikes, held_row, in_hbm(readin_weight), 1 - core, BF16)
     theirs = other_core(given)
-    own, counts_near = readin(spikes, held_row, readin_weight, core, F32)
+    own, counts_near, seen_near = readin(spikes, held_row, readin_weight, core, F32, keep=True)
     chip_sum = (own + theirs.astype(F32)).astype(BF16)
     wide = ((rows_here, model_dim), BF16)
     (plane_sum,) = small(
@@ -361,7 +365,7 @@
     lat_far = other_core(lat_near)
 
     bias_row = readout_bias[None, :]
-    (ll_near,) = readout(core, lat_near, spikes, readout_weight, bias_row)
+    (ll_near,) = readout(jnp.int32(0), lat_near, in_hbm(seen_near), readout_weight, bias_row)
     scoring = (ll_near, held_row, counts_near, counts_far)
     bits, sums = readout(1 - core, lat_far, spikes, readout_weight, bias_row, scoring)
     (bits_total,) = small(total_kernel, "total", [((1, 1), F32)], exchange(sums, ALL))

time: 154 us -> 155 us (level)
  no operation moved by 1% of the time
where the time goes in v9:
time: 155 us
  blocking collectives  93.9 us (61%)
  starting transfers between devices  22.3 us (14%)
  waiting for transfers between devices  19.5 us (13%)
  Pallas kernels  15.3 us (10%)
  other arithmetic  1.86 us (1%)
    all_to_all x6, blocking collectives, exchange(): return lax.all_to_all(blocks, axes, 0, 0, tiled=True)  93.9 us
    all_to_all x2, waiting for transfers between devices, exchange(): return lax.all_to_all(blocks, axes, 0, 0, tiled=True)  16.7 us
    ppermute x3, starting transfers between devices, other_core(): return lax.ppermute(block, 'c', [(0, 1), (1, 0)])  11.9 us
    all_to_all x2, starting transfers between devices, exchange(): return lax.all_to_all(blocks, axes, 0, 0, tiled=True)  8.59 us
    pallas_call x2, Pallas kernels, readin(): pl.pallas_call(readin_kernel, out_shape=[jax.ShapeDtypeStruct((frames //...  6.32 us
    pallas_call x2, Pallas kernels, readout(): pl.pallas_call(body, out_shape=out_shape, grid_spec=pltpu.PrefetchScalarG...  5.68 us
  transfers between devices with their start and end apart: 6, of which 4 were waited for; matrix products, arithmetic and copies ran while one was open for 1% of the time, Pallas kernels for 4%

profile of v9, /device:TPU:1, one launch (start us, length us, event | category | flops | bytes accessed | tf_op | source)
XLA Modules:
  0.0 154.9 jit_solution(281069323793870632)
XLA Ops:
  0.6 0.0 copy-start.2
  0.6 3.6 %readin.3 = (bf16[512,1024]{1,0:T(8,128)(2,1)S(1)}, f32[1,1024]{1,0:T(1,128)S(1)}) custom-call(s32[1]{0:T(128)} %bitcast.3.at_ref, s32[1024,1024]{1,0:T(8,128)} %spikes.1, s32[1,1024]{1,0:T(1,128)} %bitcast.20, bf16[1024,1024]{1,0:T(8,128)(2,1)} %weight_ref.3), custom_call_target="tpu_custom_call" | custom-call | flops 1073741824 | bytes 5242880 | tf_op jit(solution)/shard_map/readin/pallas_call | solution.py:85
  4.2 3.3 %collective-permute-start = (bf16[512,1024]{1,0:T(8,128)(2,1)S(1)}, bf16[512,1024]{1,0:T(8,128)(2,1)S(1)}, u32[]{:S(2)}, u32[]{:S(2)}) collective-permute-start(bf16[512,1024]{1,0:T(8,128)(2,1)S(1)} %get-tuple-element.16), channel_id=1, source_target_pairs={{0,8},{8,0},{1,9},{9,1},{2,10},{10,2},{3,11},{11,3},{4,12},{12,4},... | collective-permute-start | bytes 3145736 | tf_op jit(solution)/shard_map/ppermute | solution.py:35
  7.6 0.0 copy-done.2
  7.6 2.7 %readin.2 = (f32[512,1024]{1,0:T(8,128)S(1)}, f32[1,1024]{1,0:T(1,128)S(1)}, bf16[512,1024]{1,0:T(8,128)(2,1)S(1)}) custom-call(s32[1]{0:T(128)} %bitcast.1.at_ref, s32[1024,1024]{1,0:T(8,128)} %spikes.1, s32[1,1024]{1,0:T(1,128)} %bitcast.21, bf16[1024,1024]{1,0:T(8,128)(2,1)S(1)} %copy-done.2), custom_call_target="tpu_custom_call" | custom-call | flops 1073741824 | bytes 5242880 | tf_op jit(solution)/shard_map/readin/pallas_call | solution.py:85
  10.3 0.0 copy-start.4
  10.3 1.0 copy-done.4
  11.3 0.0 collective-permute-done
  11.3 0.4 add_convert_fusion
  11.7 0.0 copy-start.7
  11.7 0.0 copy-start.11
  11.7 21.7 %all_to_all.40.parts_ref = bf16[16,32,1024]{2,1,0:T(8,128)(2,1)S(1)} all-to-all(bf16[16,32,1024]{2,1,0:T(8,128)(2,1)S(1)} %bitcast.28), channel_id=1, replica_groups=mesh['y'=4,'zh'=4,'c'=2,'x'=4,'zl'=2] {'y','x'}, dimensions={0} | all-to-all | bytes 2097152 | tf_op jit(solution)/shard_map/all_to_all | solution.py:27
  33.4 0.1 plane.1.mine_ref
  33.6 1.7 %collective-permute-start.1 = (bf16[32,1024]{1,0:T(8,128)(2,1)S(1)}, bf16[32,1024]{1,0:T(8,128)(2,1)S(1)}, u32[]{:S(2)}, u32[]{:S(2)}) collective-permute-start(bf16[32,1024]{1,0:T(8,128)(2,1)S(1)} %plane.1.mine_ref), channel_id=1, source_target_pairs={{0,1},{1,0},{2,3},{3,2},{4,5},{5,4},{6,7},{7,6},{8,9},{9,8},{10,11... | collective-permute-start | bytes 196616 | tf_op jit(solution)/shard_map/ppermute | solution.py:39
  35.3 1.7 %collective-permute-done.1.other_ref = bf16[32,1024]{1,0:T(8,128)(2,1)S(1)} collective-permute-done((bf16[32,1024]{1,0:T(8,128)(2,1)S(1)}, bf16[32,1024]{1,0:T(8,128)(2,1)S(1)}, u32[]{:S(2)}, u32[]{:S(2)}) %collective-permute-start.1) | collective-permute-done | bytes 65568 | tf_op jit(solution)/shard_map/ppermute | solution.py:39
  37.0 21.1 %all_to_all.41.parts_ref = bf16[16,8,1024]{2,1,0:T(8,128)(2,1)S(1)} all-to-all(bf16[16,8,1024]{2,1,0:T(8,128)(2,1)S(1)} %pair.1), channel_id=1, replica_groups=mesh['y'=4,'zh'=4,'c'=2,'x'=4,'zl'=2] {'x','zh'}, dimensions={0} | all-to-all | bytes 524288 | tf_op jit(solution)/shard_map/all_to_all | solution.py:27
  58.1 0.0 copy-done.7
  58.1 0.0 copy-done.11
  58.1 0.4 project.1
  58.5 13.3 %all_to_all.42 = bf16[16,32,256]{2,1,0:T(8,128)(2,1)S(1)} all-to-all(bf16[16,32,256]{2,1,0:T(8,128)(2,1)S(1)} %get-tuple-element.18), channel_id=1, replica_groups=mesh['y'=4,'zh'=4,'c'=2,'x'=4,'zl'=2] {'y','zh'}, dimensions={0} | all-to-all | bytes 524288 | tf_op jit(solution)/shard_map/all_to_all | solution.py:27
  71.8 3.8 %collective-permute-start.2 = (bf16[512,256]{1,0:T(8,128)(2,1)S(1)}, bf16[512,256]{1,0:T(8,128)(2,1)S(1)}, u32[]{:S(2)}, u32[]{:S(2)}) collective-permute-start(bf16[512,256]{1,0:T(8,128)(2,1)S(1)} %bitcast.17), channel_id=1, source_target_pairs={{0,8},{8,0},{1,9},{9,1},{2,10},{10,2},{3,11},{11,3},{4,12},{12,4},... | collective-permute-start | bytes 786440 | tf_op jit(solution)/shard_map/ppermute | solution.py:35
  75.6 1.2 collective-permute-done.2.far_ref
  76.8 0.0 copy-done.8
  76.8 0.5 attend.1
  77.3 0.0 copy-start.13
  77.3 12.2 %all_to_all.43.parts_ref = bf16[8,32,1024]{2,1,0:T(8,128)(2,1)S(1)} all-to-all(bf16[8,32,1024]{2,1,0:T(8,128)(2,1)S(1)} %attend.1), channel_id=1, replica_groups=mesh['y'=4,'zh'=4,'c'=2,'x'=4,'zl'=2] {'x','zl'}, dimensions={0} | all-to-all | bytes 1048576 | tf_op jit(solution)/shard_map/all_to_all | solution.py:27
  89.5 0.0 copy-done.5
  89.6 0.0 copy-done.6
  89.6 0.0 copy-done.12
  89.6 1.3 mlp.1
  90.9 3.5 %all-to-all-start.4 = ((bf16[8,4,1024]{2,1,0:T(4,128)(2,1)}), bf16[8,4,1024]{2,1,0:T(4,128)(2,1)S(1)}, u32[]{:S(2)}, u32[]{:S(2)}) async-start(bf16[8,4,1024]{2,1,0:T(4,128)(2,1)} %get-tuple-element.20), calls=%async_computation.4 | async-start | bytes 131072 | tf_op jit(solution)/shard_map/all_to_all | solution.py:27
  94.4 5.1 %all-to-all-done.4.parts_ref = bf16[8,4,1024]{2,1,0:T(4,128)(2,1)S(1)} async-done(((bf16[8,4,1024]{2,1,0:T(4,128)(2,1)}), bf16[8,4,1024]{2,1,0:T(4,128)(2,1)S(1)}, u32[]{:S(2)}, u32[]{:S(2)}) %all-to-all-start.4) | async-done | bytes 65568 | tf_op jit(solution)/shard_map/all_to_all | solution.py:27
  99.5 0.0 copy-done.13
  99.5 0.1 latents.1
  99.6 9.6 %all_to_all.44 = bf16[8,4,1024]{2,1,0:T(4,128)(2,1)S(1)} all-to-all(bf16[8,4,1024]{2,1,0:T(4,128)(2,1)S(1)} %latents.1), channel_id=1, replica_groups=mesh['y'=4,'zh'=4,'c'=2,'x'=4,'zl'=2] {'zh','zl'}, dimensions={0} | all-to-all | bytes 131072 | tf_op jit(solution)/shard_map/all_to_all | solution.py:27
  109.2 0.1 broadcast_in_dim.27
  109.3 16.0 %all_to_all.45 = bf16[16,32,1024]{2,1,0:T(8,128)(2,1)S(1)} all-to-all(bf16[16,32,1024]{2,1,0:T(8,128)(2,1)S(1)} %broadcast_in_dim.27), channel_id=1, replica_groups=mesh['y'=4,'zh'=4,'c'=2,'x'=4,'zl'=2] {'y','x'}, dimensions={0} | all-to-all | bytes 2097152 | tf_op jit(solution)/shard_map/all_to_all | solution.py:27
  125.3 4.8 %collective-permute-start.3 = (bf16[512,1024]{1,0:T(8,128)(2,1)S(1)}, bf16[512,1024]{1,0:T(8,128)(2,1)S(1)}, u32[]{:S(2)}, u32[]{:S(2)}) collective-permute-start(bf16[512,1024]{1,0:T(8,128)(2,1)S(1)} %bitcast.14), channel_id=1, source_target_pairs={{0,8},{8,0},{1,9},{9,1},{2,10},{10,2},{3,11},{11,3},{4,12},{12,4},... | collective-permute-start | bytes 3145736 | tf_op jit(solution)/shard_map/ppermute | solution.py:35
  130.1 0.0 copy-done.1
  130.1 0.0 copy-done.10
  130.1 3.0 %readout.1.before = f32[1,1024]{1,0:T(1,128)S(1)} custom-call(s32[1]{0:T(128)} %constant.45.clone.1.at_ref, bf16[512,1024]{1,0:T(8,128)(2,1)S(1)} %bitcast.15, bf16[512,1024]{1,0:T(8,128)(2,1)} %copy-done.4, bf16[1024,1024]{1,0:T(8,128)(2,1)S(1)} %copy-done.1, f32[1,1024]{1,0:T(1,128)S(1)} %bitcast.23), custom_call_target="tpu_custom_call" | custom-call | flops 1073741824 | bytes 4194304 | tf_op jit(solution)/shard_map/readout/pallas_call | solution.py:286
  133.1 0.0 collective-permute-done.3.lat
  133.1 0.0 copy-start.3
  133.1 2.7 %score.1 = (f32[1,1024]{1,0:T(1,128)}, f32[256,1,128]{2,1,0:T(1,128)}) custom-call(s32[1]{0:T(128)} %bitcast.3.at_ref, bf16[512,1024]{1,0:T(8,128)(2,1)S(1)} %collective-permute-done.3.lat, s32[1024,1024]{1,0:T(8,128)S(1)} %copy-done, bf16[1024,1024]{1,0:T(8,128)(2,1)S(1)} %copy-done.1, f32[1,1024]{1,0:T(1,128)S(1)} %bitcast.24, ...), custom_call_target="tpu_custom_call" | custom-call | flops 1073741824 | bytes 4194304 | tf_op jit(solution)/shard_map/score/pallas_call | solution.py:286
  135.9 5.1 %all-to-all-start.7 = ((f32[256,1,128]{2,1,0:T(1,128)}), f32[256,1,128]{2,1,0:T(1,128)S(1)}, u32[]{:S(2)}, u32[]{:S(2)}) async-start(f32[256,1,128]{2,1,0:T(1,128)} %get-tuple-element.26), calls=%async_computation.7 | async-start | bytes 262144 | tf_op jit(solution)/shard_map/all_to_all | solution.py:27
  141.0 1.5 dynamic-slice_select_fusion
  142.5 11.6 %all-to-all-done.7.sums_ref = f32[256,1,128]{2,1,0:T(1,128)S(1)} async-done(((f32[256,1,128]{2,1,0:T(1,128)}), f32[256,1,128]{2,1,0:T(1,128)S(1)}, u32[]{:S(2)}, u32[]{:S(2)}) %all-to-all-start.7) | async-done | bytes 131104 | tf_op jit(solution)/shard_map/all_to_all | solution.py:27
  154.1 0.9 total.1
  (13 shorter events, 0.1 us)
Async XLA Ops:
  0.6 6.9 %copy-start.2 = (bf16[1024,1024]{1,0:T(8,128)(2,1)S(1)}, bf16[1024,1024]{1,0:T(8,128)(2,1)}, u32[]{:S(2)}) copy-start(bf16[1024,1024]{1,0:T(8,128)(2,1)} %weight_ref.3) | copy-start | bytes 6291460
  4.2 7.1 %collective-permute-start = (bf16[512,1024]{1,0:T(8,128)(2,1)S(1)}, bf16[512,1024]{1,0:T(8,128)(2,1)S(1)}, u32[]{:S(2)}, u32[]{:S(2)}) collective-permute-start(bf16[512,1024]{1,0:T(8,128)(2,1)S(1)} %get-tuple-element.16), channel_id=1, source_target_pairs={{0,8},{8,0},{1,9},{9,1},{2,10},{10,2},{3,11},{11,3},{4,12},{12,4},... | collective-permute-start | bytes 3145736 | tf_op jit(solution)/shard_map/ppermute | solution.py:35
  10.3 1.0 copy-start.4
  11.7 46.4 %copy-start.7 = (bf16[1024,3,128]{2,0,1:T(8,128)(2,1)S(1)}, bf16[1024,3,128]{2,0,1:T(8,128)(2,1)}, u32[]{:S(2)}) copy-start(bf16[1024,3,128]{2,0,1:T(8,128)(2,1)} %param.15) | copy-start | bytes 2359300
  11.7 46.4 %copy-start.11 = (f32[1024]{0:T(1024)S(1)}, f32[1024]{0:T(1024)}, u32[]{:S(2)}) copy-start(f32[1024]{0:T(1024)} %param.19) | copy-start | bytes 12292
  33.4 43.4 %copy-start.8 = (bf16[128,1024]{1,0:T(8,128)(2,1)S(1)}, bf16[128,1024]{1,0:T(8,128)(2,1)}, u32[]{:S(2)}) copy-start(bf16[128,1024]{1,0:T(8,128)(2,1)} %mix_ref.1) | copy-start | bytes 786436
  33.6 3.4 %collective-permute-start.1 = (bf16[32,1024]{1,0:T(8,128)(2,1)S(1)}, bf16[32,1024]{1,0:T(8,128)(2,1)S(1)}, u32[]{:S(2)}, u32[]{:S(2)}) collective-permute-start(bf16[32,1024]{1,0:T(8,128)(2,1)S(1)} %plane.1.mine_ref), channel_id=1, source_target_pairs={{0,1},{1,0},{2,3},{3,2},{4,5},{5,4},{6,7},{7,6},{8,9},{9,8},{10,11... | collective-permute-start | bytes 196616 | tf_op jit(solution)/shard_map/ppermute | solution.py:39
  58.1 31.5 %copy-start.5 = (bf16[1024,512]{1,0:T(8,128)(2,1)S(1)}, bf16[1024,512]{1,0:T(8,128)(2,1)}, u32[]{:S(2)}) copy-start(bf16[1024,512]{1,0:T(8,128)(2,1)} %up_ref.1) | copy-start | bytes 3145732
  58.1 31.5 %copy-start.6 = (bf16[512,1024]{1,0:T(8,128)(2,1)S(1)}, bf16[512,1024]{1,0:T(8,128)(2,1)}, u32[]{:S(2)}) copy-start(bf16[512,1024]{1,0:T(8,128)(2,1)} %down_ref.1) | copy-start | bytes 3145732
  58.1 31.5 %copy-start.12 = (f32[1024]{0:T(1024)S(1)}, f32[1024]{0:T(1024)}, u32[]{:S(2)}) copy-start(f32[1024]{0:T(1024)} %param.20) | copy-start | bytes 12292
  71.8 5.0 %collective-permute-start.2 = (bf16[512,256]{1,0:T(8,128)(2,1)S(1)}, bf16[512,256]{1,0:T(8,128)(2,1)S(1)}, u32[]{:S(2)}, u32[]{:S(2)}) collective-permute-start(bf16[512,256]{1,0:T(8,128)(2,1)S(1)} %bitcast.17), channel_id=1, source_target_pairs={{0,8},{8,0},{1,9},{9,1},{2,10},{10,2},{3,11},{11,3},{4,12},{12,4},... | collective-permute-start | bytes 786440 | tf_op jit(solution)/shard_map/ppermute | solution.py:35
  77.3 22.2 %copy-start.13 = (f32[1024]{0:T(1024)S(1)}, f32[1024]{0:T(1024)}, u32[]{:S(2)}) copy-start(f32[1024]{0:T(1024)} %param.21) | copy-start | bytes 12292
  90.9 39.3 %copy-start.1 = (bf16[1024,1024]{1,0:T(8,128)(2,1)S(1)}, bf16[1024,1024]{1,0:T(8,128)(2,1)}, u32[]{:S(2)}) copy-start(bf16[1024,1024]{1,0:T(8,128)(2,1)} %weight.3) | copy-start | bytes 6291460
  90.9 39.3 %copy-start.10 = (f32[1024]{0:T(1024)S(1)}, f32[1024]{0:T(1024)}, u32[]{:S(2)}) copy-start(f32[1024]{0:T(1024)} %param.23) | copy-start | bytes 12292
  90.9 8.6 %all-to-all-start.4 = ((bf16[8,4,1024]{2,1,0:T(4,128)(2,1)}), bf16[8,4,1024]{2,1,0:T(4,128)(2,1)S(1)}, u32[]{:S(2)}, u32[]{:S(2)}) async-start(bf16[8,4,1024]{2,1,0:T(4,128)(2,1)} %get-tuple-element.20), calls=%async_computation.4 | async-start | bytes 131072 | tf_op jit(solution)/shard_map/all_to_all | solution.py:27
  125.3 7.8 %collective-permute-start.3 = (bf16[512,1024]{1,0:T(8,128)(2,1)S(1)}, bf16[512,1024]{1,0:T(8,128)(2,1)S(1)}, u32[]{:S(2)}, u32[]{:S(2)}) collective-permute-start(bf16[512,1024]{1,0:T(8,128)(2,1)S(1)} %bitcast.14), channel_id=1, source_target_pairs={{0,8},{8,0},{1,9},{9,1},{2,10},{10,2},{3,11},{11,3},{4,12},{12,4},... | collective-permute-start | bytes 3145736 | tf_op jit(solution)/shard_map/ppermute | solution.py:35
  130.1 3.0 %copy-start = (s32[1024,1024]{1,0:T(8,128)S(1)}, s32[1024,1024]{1,0:T(8,128)}, u32[]{:S(2)}) copy-start(s32[1024,1024]{1,0:T(8,128)} %spikes.1) | copy-start | bytes 12582916
  130.1 3.0 %copy-start.9 = (s32[1024]{0:T(1024)S(1)}, s32[1024]{0:T(1024)}, u32[]{:S(2)}) copy-start(s32[1024]{0:T(1024)} %param.13) | copy-start | bytes 12292
  133.1 2.8 %copy-start.3 = (bf16[512,1024]{1,0:T(8,128)(2,1)}, bf16[512,1024]{1,0:T(8,128)(2,1)S(1)}, u32[]{:S(2)}) copy-start(bf16[512,1024]{1,0:T(8,128)(2,1)S(1)} %collective-permute-done.3.lat) | copy-start | bytes 3145732
  135.9 18.2 %all-to-all-start.7 = ((f32[256,1,128]{2,1,0:T(1,128)}), f32[256,1,128]{2,1,0:T(1,128)S(1)}, u32[]{:S(2)}, u32[]{:S(2)}) async-start(f32[256,1,128]{2,1,0:T(1,128)} %get-tuple-element.26), calls=%async_computation.7 | async-start | bytes 262144 | tf_op jit(solution)/shard_map/all_to_all | solution.py:27
